TPU v7x, 32 devices: a whole 2x2x4 slice. The times are simulated.
32 devices in a mesh: ctx: 8 (over y, x, core), head: 4 (over z).
Axes of the slice: x: 2, y: 2, z: 4, core: 2. Of those that a mesh axis runs over, the one named last changes fastest.
Arguments:
- hidden: bfloat16 [16384, 1024], P(('ctx', 'head')), may hold values from -6 to 6
- cotangent: bfloat16 [16384, 1024], P(('ctx', 'head')), may hold values from -6 to 6
- segment_ids: int32 [16384], replicated, may hold values from 0 to 15, as said below
- adapter_ids: int32 [4], replicated, may hold values from 0 to 7
- attn_gain: float32 [1024], replicated, may hold values from 0.1 to 1.9
- query_gain: float32 [64], replicated, may hold values from 0.1 to 1.9
- key_gain: float32 [64], replicated, may hold values from 0.1 to 1.9
- ffn_gain: float32 [1024], replicated, may hold values from 0.1 to 1.9
- qkv_weight: bfloat16 [1024, 2048], P(('ctx', 'head')), may hold values from -0.1875 to 0.1875
- out_weight: bfloat16 [1024, 1024], P(('ctx', 'head')), may hold values from -1.5 to 1.5
- gate_up_weight: bfloat16 [1024, 9216], P(('ctx', 'head')), may hold values from -0.1875 to 0.1875
- down_weight: bfloat16 [4608, 1024], P(('ctx', 'head')), may hold values from -0.1875 to 0.1875
- qkv_down: bfloat16 [8, 48, 1024], P(None, None, ('ctx', 'head')), may hold values from -0.1875 to 0.1875
- qkv_up: bfloat16 [8, 16, 2048], P(None, None, ('ctx', 'head')), may hold values from -0.4375 to 0.4375
- out_down: bfloat16 [8, 16, 1024], P(None, None, ('ctx', 'head')), may hold values from -1.5 to 1.5
- out_up: bfloat16 [8, 16, 1024], P(None, None, ('ctx', 'head')), may hold values from -0.75 to 0.75
- mlp_down: bfloat16 [8, 32, 1024], P(None, None, ('ctx', 'head')), may hold values from -0.1875 to 0.1875
- mlp_up: bfloat16 [8, 16, 9216], P(None, None, ('ctx', 'head')), may hold values from -0.4375 to 0.4375
- ffd_down: bfloat16 [8, 16, 4608], P(None, None, ('ctx', 'head')), may hold values from -0.09375 to 0.09375
- ffd_up: bfloat16 [8, 16, 1024], P(None, None, ('ctx', 'head')), may hold values from -0.75 to 0.75
Outputs:
- output: bfloat16 [16384, 1024], P(('ctx', 'head'))
- input_grad: float32 [16384, 1024], P(('ctx', 'head'))
- qkv_down_grad: float32 [8, 48, 1024], P(None, None, ('ctx', 'head'))
- qkv_up_grad: float32 [8, 16, 2048], P(None, None, ('ctx', 'head'))
- out_down_grad: float32 [8, 16, 1024], P(None, None, ('ctx', 'head'))
- out_up_grad: float32 [8, 16, 1024], P(None, None, ('ctx', 'head'))
- mlp_down_grad: float32 [8, 32, 1024], P(None, None, ('ctx', 'head'))
- mlp_up_grad: float32 [8, 16, 9216], P(None, None, ('ctx', 'head'))
- ffd_down_grad: float32 [8, 16, 4608], P(None, None, ('ctx', 'head'))
- ffd_up_grad: float32 [8, 16, 1024], P(None, None, ('ctx', 'head'))
Inputs may be any that keep to these rules, and one draw needn't show every extreme that they name: `segment_ids`: never falling along the tokens and taking every value from 0 to the most; every document holds at most 2048 tokens and one holds exactly 2048.
All inputs are finite; a program needn't handle non-finite values.
Results may differ from a plain program's by a relative error of at most 0.018.
Values may be sent and summed in bfloat16 or wider, within the bound.
No kernel may reach another device: no remote copies, remote signals or barrier semaphores. Data moves between devices by JAX's collectives and lax.ppermute only.
A program may use at most 256 MiB of HBM per device.

v0:
```python
import jax
import jax.numpy as jnp
from jax import lax
from jax.sharding import PartitionSpec as P

D = 1024
HEADS = 16
KV_HEADS = 8
HEAD_DIM = 64
FF = 4608
RANK = 16
ADAPTERS = 8
NSEQ = 4
SEGMAX = 2048
QBLOCK = 512
QW = 1024
KW = 512


epsilon = 1e-05
rope_base = 1000000.0


def passed_along(value, axis, by):
    count = lax.axis_size(axis)
    pairs = [(i, i + by) for i in range(count) if 0 <= i + by < count]
    return lax.ppermute(value, axis, pairs)


def matmul(left_side, right_side):
    return jnp.dot(left_side, right_side, preferred_element_type=jnp.float32)


def contract_rows(left_side, right_side):
    return lax.dot_general(
        left_side, right_side, (((0,), (0,)), ((), ())), preferred_element_type=jnp.float32
    )


def contract_cols(left_side, right_side):
    return lax.dot_general(
        left_side, right_side, (((1,), (1,)), ((), ())), preferred_element_type=jnp.float32
    )


def rms_norm(values, gain_row):
    return (
        values * lax.rsqrt(jnp.mean(values * values, axis=-1, keepdims=True) + epsilon) * gain_row
    )


def rope_tables(positions):
    middle = HEAD_DIM // 2
    frequency = jnp.power(rope_base, -(2.0 / HEAD_DIM) * jnp.arange(middle, dtype=jnp.float32))
    angles = positions.astype(jnp.float32)[:, None] * frequency[None, :]
    return (jnp.cos(angles)[:, None, :], jnp.sin(angles)[:, None, :])


def rotate(values, cosine, sine_part):
    middle = values.shape[-1] // 2
    leading = values[..., :middle]
    trailing = values[..., middle:]
    return jnp.concatenate(
        [leading * cosine - trailing * sine_part, trailing * cosine + leading * sine_part], axis=-1
    )


def prepare_heads(projected, positions, query_gain, key_gain):
    length = projected.shape[0]
    cosine, sine_part = rope_tables(positions)
    query_rows = projected[:, :QW].reshape(length, HEADS, HEAD_DIM)
    key_rows = projected[:, QW : QW + KW].reshape(length, KV_HEADS, HEAD_DIM)
    value_rows = projected[:, QW + KW :].reshape(length, KV_HEADS, HEAD_DIM)
    query_rows = rotate(rms_norm(query_rows, query_gain), cosine, sine_part)
    key_rows = rotate(rms_norm(key_rows, key_gain), cosine, sine_part)
    grouped = query_rows.reshape(length, KV_HEADS, HEADS // KV_HEADS * HEAD_DIM)
    return (grouped, jnp.concatenate([key_rows, value_rows], axis=-1))


def rank_apply(reduced, up_rows, bounds):
    return jnp.concatenate(
        [
            matmul(
                reduced[:, RANK * member : RANK * (member + 1)],
                up_rows[:, bounds[member] : bounds[member + 1]],
            )
            for member in range(len(bounds) - 1)
        ],
        axis=1,
    )


def rank_back(grad_low, reduced, up_rows, bounds):
    up_grad = jnp.concatenate(
        [
            contract_rows(
                reduced[:, RANK * member : RANK * (member + 1)],
                grad_low[:, bounds[member] : bounds[member + 1]],
            )
            for member in range(len(bounds) - 1)
        ],
        axis=1,
    )
    reduced_grad = jnp.concatenate(
        [
            contract_cols(
                grad_low[:, bounds[member] : bounds[member + 1]],
                up_rows[:, bounds[member] : bounds[member + 1]],
            )
            for member in range(len(bounds) - 1)
        ],
        axis=1,
    )
    return (up_grad, reduced_grad)


def local(
    hidden,
    cotangent,
    segment_ids,
    adapter_ids,
    attn_gain,
    query_gain,
    key_gain,
    ffn_gain,
    qkv_weight,
    out_weight,
    gate_up_weight,
    down_weight,
    qkv_down,
    qkv_up,
    out_down,
    out_up,
    mlp_down,
    mlp_up,
    ffd_down,
    ffd_up,
):
    local_rows = hidden.shape[0]
    head_count = lax.axis_size("head")
    span_rows = local_rows * head_count
    seq_length = span_rows * lax.axis_size("ctx") // NSEQ
    ctx_index = lax.axis_index("ctx")
    head_index = lax.axis_index("head")
    span_start = ctx_index * span_rows
    first_row = span_start + head_index * local_rows
    seq_index = first_row // seq_length
    adapter_pick = lax.dynamic_index_in_dim(adapter_ids, seq_index, 0, keepdims=False)
    positions = first_row - seq_index * seq_length + jnp.arange(local_rows, dtype=jnp.int32)
    gathered = (
        lax.all_gather(qkv_weight, ("ctx", "head"), axis=0, tiled=True),
        lax.all_gather(out_weight, ("ctx", "head"), axis=0, tiled=True),
        lax.all_gather(gate_up_weight, ("ctx", "head"), axis=0, tiled=True),
        lax.all_gather(down_weight, ("ctx", "head"), axis=0, tiled=True),
        lax.all_gather(qkv_down, ("ctx", "head"), axis=2, tiled=True),
        lax.all_gather(qkv_up, ("ctx", "head"), axis=2, tiled=True),
        lax.all_gather(out_down, ("ctx", "head"), axis=2, tiled=True),
        lax.all_gather(out_up, ("ctx", "head"), axis=2, tiled=True),
        lax.all_gather(mlp_down, ("ctx", "head"), axis=2, tiled=True),
        lax.all_gather(mlp_up, ("ctx", "head"), axis=2, tiled=True),
        lax.all_gather(ffd_down, ("ctx", "head"), axis=2, tiled=True),
        lax.all_gather(ffd_up, ("ctx", "head"), axis=2, tiled=True),
    )
    qkv_full, out_full, gate_up_full, down_full = (
        gathered[0],
        gathered[1],
        gathered[2],
        gathered[3],
    )
    chosen = [
        lax.dynamic_index_in_dim(member, adapter_pick, 0, keepdims=False) for member in gathered[4:]
    ]
    qkv_bounds = (0, QW, QW + KW, QW + 2 * KW)
    inputs = hidden.astype(jnp.float32)
    normed, norm_pull = jax.vjp(lambda operand: rms_norm(operand, attn_gain), inputs)
    normed_low = normed.astype(jnp.bfloat16)
    reduced_qkv = contract_cols(normed_low, chosen[0]).astype(jnp.bfloat16)
    projected = matmul(normed_low, qkv_full) + rank_apply(reduced_qkv, chosen[1], qkv_bounds)
    (grouped, keyvals), head_pull = jax.vjp(
        lambda operand: prepare_heads(operand, positions, query_gain, key_gain), projected
    )
    query_all, keyval_all = (
        lax.all_to_all(
            grouped.astype(jnp.bfloat16), "head", split_axis=1, concat_axis=0, tiled=True
        ),
        lax.all_to_all(
            keyvals.astype(jnp.bfloat16), "head", split_axis=1, concat_axis=0, tiled=True
        ),
    )
    prior_rows = passed_along(keyval_all, "ctx", 1)
    lead_rows = prior_rows.shape[0]
    extended = jnp.concatenate([prior_rows, keyval_all], axis=0)
    seg_padded = jnp.concatenate([jnp.full((SEGMAX,), -1, jnp.int32), segment_ids])
    seg_window = lax.dynamic_slice_in_dim(seg_padded, span_start, SEGMAX + span_rows, 0)
    window_rows = SEGMAX + QBLOCK
    group_size = HEADS // KV_HEADS
    local_groups = query_all.shape[1]
    score_scale = HEAD_DIM ** (-0.5)
    block_starts = jnp.arange(span_rows // QBLOCK, dtype=jnp.int32) * QBLOCK

    def allowed_mask(offset):
        seg_keys = lax.dynamic_slice_in_dim(seg_window, offset, window_rows, 0)
        seg_query = lax.dynamic_slice_in_dim(seg_window, offset + SEGMAX, QBLOCK, 0)
        query_pos = span_start + offset + jnp.arange(QBLOCK, dtype=jnp.int32)
        key_pos = span_start + offset - SEGMAX + jnp.arange(window_rows, dtype=jnp.int32)
        same_seq = key_pos[None, :] // seq_length == query_pos[:, None] // seq_length
        return (
            same_seq
            & (key_pos[None, :] <= query_pos[:, None])
            & (seg_keys[None, :] == seg_query[:, None])
        )

    def block_operands(offset):
        query_block = lax.dynamic_slice_in_dim(query_all, offset, QBLOCK, 0).reshape(
            QBLOCK, local_groups, group_size, HEAD_DIM
        )
        window = lax.dynamic_slice_in_dim(extended, lead_rows - SEGMAX + offset, window_rows, 0)
        return (query_block, window[..., :HEAD_DIM], window[..., HEAD_DIM:])

    def block_scores(query_block, key_rows, offset):
        scores = (
            jnp.einsum("qcgd,scd->cgqs", query_block, key_rows, preferred_element_type=jnp.float32)
            * score_scale
        )
        return jnp.where(allowed_mask(offset)[None, None], scores, -1e30)

    def forward_block(offset):
        query_block, key_rows, value_rows = block_operands(offset)
        scores = block_scores(query_block, key_rows, offset)
        largest = jnp.max(scores, axis=-1, keepdims=True)
        exponent = jnp.exp(scores - largest)
        totals = jnp.sum(exponent, axis=-1, keepdims=True)
        attention = (exponent / totals).astype(jnp.bfloat16)
        mixture = jnp.einsum(
            "cgqs,scd->qcgd", attention, value_rows, preferred_element_type=jnp.float32
        )
        return (
            mixture.reshape(QBLOCK, local_groups, group_size * HEAD_DIM).astype(jnp.bfloat16),
            (largest + jnp.log(totals))[..., 0],
        )

    mixed_blocks, log_totals = lax.map(forward_block, block_starts)
    mixture_all = mixed_blocks.reshape(span_rows, local_groups, group_size * HEAD_DIM)
    mixture_tok = lax.all_to_all(
        mixture_all, "head", split_axis=0, concat_axis=1, tiled=True
    ).reshape(local_rows, QW)
    reduced_out = contract_cols(mixture_tok, chosen[2]).astype(jnp.bfloat16)
    branch = matmul(mixture_tok, out_full) + rank_apply(reduced_out, chosen[3], (0, D))
    middle = inputs + branch
    normed_two, norm_two_pull = jax.vjp(lambda operand: rms_norm(operand, ffn_gain), middle)
    normed_two_low = normed_two.astype(jnp.bfloat16)
    reduced_mlp = contract_cols(normed_two_low, chosen[4]).astype(jnp.bfloat16)
    gate_up = matmul(normed_two_low, gate_up_full) + rank_apply(
        reduced_mlp, chosen[5], (0, FF, 2 * FF)
    )
    hidden_units, unit_pull = jax.vjp(
        lambda operand: jax.nn.silu(operand[:, :FF]) * operand[:, FF:], gate_up
    )
    units_low = hidden_units.astype(jnp.bfloat16)
    reduced_down = contract_cols(units_low, chosen[6]).astype(jnp.bfloat16)
    branch_two = matmul(units_low, down_full) + rank_apply(reduced_down, chosen[7], (0, D))
    output = (middle + branch_two).astype(jnp.bfloat16)
    qkv_back, out_back, gate_up_back, down_back = (qkv_full, out_full, gate_up_full, down_full)
    ffd_up_grad, reduced_down_grad = rank_back(cotangent, reduced_down, chosen[7], (0, D))
    reduced_down_low = reduced_down_grad.astype(jnp.bfloat16)
    ffd_down_grad = contract_rows(reduced_down_low, units_low)
    units_grad = contract_cols(cotangent, down_back) + matmul(reduced_down_low, chosen[6])
    gate_up_grad = unit_pull(units_grad)[0].astype(jnp.bfloat16)
    mlp_up_grad, reduced_mlp_grad = rank_back(gate_up_grad, reduced_mlp, chosen[5], (0, FF, 2 * FF))
    reduced_mlp_low = reduced_mlp_grad.astype(jnp.bfloat16)
    mlp_down_grad = contract_rows(reduced_mlp_low, normed_two_low)
    normed_two_grad = contract_cols(gate_up_grad, gate_up_back) + matmul(reduced_mlp_low, chosen[4])
    middle_grad = cotangent.astype(jnp.float32) + norm_two_pull(normed_two_grad)[0]
    branch_grad = middle_grad.astype(jnp.bfloat16)
    out_up_grad, reduced_out_grad = rank_back(branch_grad, reduced_out, chosen[3], (0, D))
    reduced_out_low = reduced_out_grad.astype(jnp.bfloat16)
    out_down_grad = contract_rows(reduced_out_low, mixture_tok)
    mixture_grad = (
        contract_cols(branch_grad, out_back) + matmul(reduced_out_low, chosen[2])
    ).astype(jnp.bfloat16)
    grad_heads = lax.all_to_all(
        mixture_grad.reshape(local_rows, KV_HEADS, group_size * HEAD_DIM),
        "head",
        split_axis=1,
        concat_axis=0,
        tiled=True,
    )

    def backward_block(ext_grad, scanned):
        offset, log_total = scanned
        query_block, key_rows, value_rows = block_operands(offset)
        grad_block = lax.dynamic_slice_in_dim(grad_heads, offset, QBLOCK, 0).reshape(
            QBLOCK, local_groups, group_size, HEAD_DIM
        )
        scores = block_scores(query_block, key_rows, offset)
        attention = jnp.exp(scores - log_total[..., None])
        prob_grad = jnp.einsum(
            "qcgd,scd->cgqs", grad_block, value_rows, preferred_element_type=jnp.float32
        )
        inner_sum = jnp.sum(attention * prob_grad, axis=-1, keepdims=True)
        score_grad = (attention * (prob_grad - inner_sum)).astype(jnp.bfloat16)
        query_grad = (
            jnp.einsum("cgqs,scd->qcgd", score_grad, key_rows, preferred_element_type=jnp.float32)
            * score_scale
        )
        key_grad = (
            jnp.einsum(
                "cgqs,qcgd->scd", score_grad, query_block, preferred_element_type=jnp.float32
            )
            * score_scale
        )
        value_grad = jnp.einsum(
            "cgqs,qcgd->scd",
            attention.astype(jnp.bfloat16),
            grad_block,
            preferred_element_type=jnp.float32,
        )
        start_row = lead_rows - SEGMAX + offset
        current = lax.dynamic_slice_in_dim(ext_grad, start_row, window_rows, 0)
        ext_grad = lax.dynamic_update_slice_in_dim(
            ext_grad, current + jnp.concatenate([key_grad, value_grad], axis=-1), start_row, 0
        )
        return (ext_grad, query_grad.reshape(QBLOCK, local_groups, group_size * HEAD_DIM))

    ext_grad, query_grads = lax.scan(
        backward_block, jnp.zeros(extended.shape, jnp.float32), (block_starts, log_totals)
    )
    own_grad = ext_grad[lead_rows:]
    returned = passed_along(ext_grad[:lead_rows].astype(jnp.bfloat16), "ctx", -1).astype(
        jnp.float32
    )
    own_grad = own_grad + returned
    query_grad_all = query_grads.reshape(span_rows, local_groups, group_size * HEAD_DIM).astype(
        jnp.bfloat16
    )
    keyval_grad_all = own_grad.astype(jnp.bfloat16)
    query_grad_tok, keyval_grad_tok = (
        lax.all_to_all(query_grad_all, "head", split_axis=0, concat_axis=1, tiled=True),
        lax.all_to_all(keyval_grad_all, "head", split_axis=0, concat_axis=1, tiled=True),
    )
    projected_grad = head_pull(
        (query_grad_tok.astype(jnp.float32), keyval_grad_tok.astype(jnp.float32))
    )[0].astype(jnp.bfloat16)
    qkv_up_grad, reduced_qkv_grad = rank_back(projected_grad, reduced_qkv, chosen[1], qkv_bounds)
    reduced_qkv_low = reduced_qkv_grad.astype(jnp.bfloat16)
    qkv_down_grad = contract_rows(reduced_qkv_low, normed_low)
    normed_grad = contract_cols(projected_grad, qkv_back) + matmul(reduced_qkv_low, chosen[0])
    input_grad = middle_grad + norm_pull(normed_grad)[0]
    local_grads = (
        qkv_down_grad,
        qkv_up_grad,
        out_down_grad,
        out_up_grad,
        mlp_down_grad,
        mlp_up_grad,
        ffd_down_grad,
        ffd_up_grad,
    )
    selector = (jnp.arange(ADAPTERS, dtype=jnp.int32) == adapter_pick).astype(jnp.float32)
    spread = [selector[:, None, None] * member[None] for member in local_grads]
    owned_grads = (
        lax.psum_scatter(spread[0], ("ctx", "head"), scatter_dimension=2, tiled=True),
        lax.psum_scatter(spread[1], ("ctx", "head"), scatter_dimension=2, tiled=True),
        lax.psum_scatter(spread[2], ("ctx", "head"), scatter_dimension=2, tiled=True),
        lax.psum_scatter(spread[3], ("ctx", "head"), scatter_dimension=2, tiled=True),
        lax.psum_scatter(spread[4], ("ctx", "head"), scatter_dimension=2, tiled=True),
        lax.psum_scatter(spread[5], ("ctx", "head"), scatter_dimension=2, tiled=True),
        lax.psum_scatter(spread[6], ("ctx", "head"), scatter_dimension=2, tiled=True),
        lax.psum_scatter(spread[7], ("ctx", "head"), scatter_dimension=2, tiled=True),
    )
    return (
        output,
        input_grad,
        owned_grads[0],
        owned_grads[1],
        owned_grads[2],
        owned_grads[3],
        owned_grads[4],
        owned_grads[5],
        owned_grads[6],
        owned_grads[7],
    )


def solution(mesh):
    placed = (
        P(("ctx", "head"), None),
        P(("ctx", "head"), None),
        P(),
        P(),
        P(),
        P(),
        P(),
        P(),
        P(("ctx", "head"), None),
        P(("ctx", "head"), None),
        P(("ctx", "head"), None),
        P(("ctx", "head"), None),
        P(None, None, ("ctx", "head")),
        P(None, None, ("ctx", "head")),
        P(None, None, ("ctx", "head")),
        P(None, None, ("ctx", "head")),
        P(None, None, ("ctx", "head")),
        P(None, None, ("ctx", "head")),
        P(None, None, ("ctx", "head")),
        P(None, None, ("ctx", "head")),
    )
    return jax.shard_map(
        local,
        mesh=mesh,
        in_specs=placed,
        out_specs=(
            P(("ctx", "head"), None),
            P(("ctx", "head"), None),
            P(None, None, ("ctx", "head")),
            P(None, None, ("ctx", "head")),
            P(None, None, ("ctx", "head")),
            P(None, None, ("ctx", "head")),
            P(None, None, ("ctx", "head")),
            P(None, None, ("ctx", "head")),
            P(None, None, ("ctx", "head")),
            P(None, None, ("ctx", "head")),
        ),
        check_vma=False,
    )
```

profile of v0, /device:TPU:0, one launch (start us, length us, event | category | flops | bytes accessed | tf_op | source)
XLA Modules:
  0.0 2121.8 jit_solution(15881634754115711756)
XLA Ops:
  17.3 168.6 %all_gather.38 = bf16[8,16,2048]{1,0,2:T(8,128)(2,1)S(1)} all-gather(bf16[8,16,64]{1,0,2:T(8,128)(2,1)S(1)} %copy.116), channel_id=1, replica_groups=mesh['ctx'=8,'head'=4] {'ctx','head'}, dimensions={2}, use_global_device_ids=true | all-gather | bytes 540672 | tf_op jit(solution)/shard_map/all_gather | solution.py:156
  188.3 118.2 %all_gather.37 = bf16[8,48,1024]{1,2,0:T(8,128)(2,1)S(1)} all-gather(bf16[8,48,32]{1,2,0:T(8,128)(2,1)S(1)} %copy-done.64), channel_id=1, replica_groups=mesh['ctx'=8,'head'=4] {'ctx','head'}, dimensions={2}, use_global_device_ids=true | all-gather | bytes 811008 | tf_op jit(solution)/shard_map/all_gather | solution.py:155
  311.5 5.4 maximum_add_fusion.2
  334.1 30.8 %all-to-all-done = bf16[512,8,128]{0,2,1:T(8,128)(2,1)S(1)} async-done(((bf16[512,8,128]{0,2,1:T(8,128)(2,1)}), bf16[512,8,128]{0,2,1:T(8,128)(2,1)S(1)}, u32[]{:S(2)}, u32[]{:S(2)}) %all-to-all-start) | async-done | bytes 1048608 | tf_op jit(solution)/shard_map/all_to_all | solution.py:186
  373.3 116.0 %all_gather.47 = bf16[8,16,1024]{1,0,2:T(8,128)(2,1)S(1)} all-gather(bf16[8,16,32]{1,0,2:T(8,128)(2,1)S(1)} %copy.141), channel_id=1, replica_groups=mesh['ctx'=8,'head'=4] {'ctx','head'}, dimensions={2}, use_global_device_ids=true | all-gather | bytes 270336 | tf_op jit(solution)/shard_map/all_gather | solution.py:162
  490.7 118.5 %all_gather.43 = bf16[8,32,1024]{1,0,2:T(8,128)(2,1)S(1)} all-gather(bf16[8,32,32]{1,0,2:T(8,128)(2,1)S(1)} %copy.135), channel_id=1, replica_groups=mesh['ctx'=8,'head'=4] {'ctx','head'}, dimensions={2}, use_global_device_ids=true | all-gather | bytes 540672 | tf_op jit(solution)/shard_map/all_gather | solution.py:159
  615.5 107.2 %while.30 = (s32[]{:T(128)}, bf16[4,512,2,128]{3,1,0,2:T(8,128)(2,1)S(1)}, f32[4,2,2,512]{3,2,1,0:T(2,128)}, s32[4]{0:T(128)S(1)}, bf16[4096,2,128]{0,2,1:T(8,12...) while((s32[]{:T(128)}, ...), condition=%wide.region_6.7_spmd, body=%wide.region_3.6_spmd.sunk | while | flops 1411823616 | bytes 71717184 | solution.py:242
  624.2 5.2 fusion.197
  634.0 7.5 fusion.199
  651.0 5.2 fusion.197
  660.8 7.5 fusion.199
  677.8 5.2 fusion.197
  687.6 7.5 fusion.199
  704.6 5.2 fusion.197
  714.4 7.5 fusion.199
  722.8 9.5 copy.128
  735.9 103.2 %all_gather.41 = bf16[8,16,1024]{1,0,2:T(8,128)(2,1)S(1)} all-gather(bf16[8,16,32]{1,0,2:T(8,128)(2,1)S(1)} %copy-done.50), channel_id=1, replica_groups=mesh['ctx'=8,'head'=4] {'ctx','head'}, dimensions={2}, use_global_device_ids=true | all-gather | bytes 270336 | tf_op jit(solution)/shard_map/all_gather | solution.py:158
  840.0 85.8 %all_gather.40 = bf16[8,16,1024]{1,0,2:T(8,128)(2,1)S(1)} all-gather(bf16[8,16,32]{1,0,2:T(8,128)(2,1)S(1)} %copy-done.49), channel_id=1, replica_groups=mesh['ctx'=8,'head'=4] {'ctx','head'}, dimensions={2}, use_global_device_ids=true | all-gather | bytes 270336 | tf_op jit(solution)/shard_map/all_gather | solution.py:157
  928.9 6.1 constant_dynamic-slice_fusion.5
  938.7 9.7 constant_dynamic-slice_fusion.6
  948.4 9.7 copy.193
  965.6 5.0 fusion.77
  970.6 5.0 fusion.80
  975.5 11.2 fusion.134
  986.8 24.8 %maximum_add_fusion.1 = f32[512,9216]{1,0:T(8,128)} fusion(f32[512,4608]{1,0:T(8,128)} %fusion.77, f32[512,4608]{1,0:T(8,128)} %fusion.80, bf16[512,1024]{1,0:T(8,128)(2,1)} %copy-done.19, bf16[1024,9216]{1,0:T(8,128)(2,1)} %all-gather.11.cloned.1.call-done), kind=kOutput, calls=%fused_computation.87 | convolution fusion | flops 9673113600 | bytes 57671680 | tf_op jit(solution)/shard_map/dot_general | solution.py:31
  1011.6 17.0 fusion.66
  1028.6 7.4 add_convert_fusion
  1042.1 18.3 multiply_reduce_fusion.1
  1110.6 9.4 copy.178
  1120.0 12.6 reshape.633
  1141.6 18.9 copy.176
  1160.4 24.0 %reshape.631 = f32[9216,128]{1,0:T(8,128)} reshape(f32[9216,8,16]{2,1,0:T(8,128)} %bitcast.297) | data formatting | bytes 9437184
  1189.8 333.9 %while.31 = (s32[]{:T(128)}, f32[4096,2,128]{2,1,0:T(2,128)}, bf16[4,512,2,128]{3,1,0,2:T(8,128)(2,1)}, s32[4]{0:T(128)S(1)}, bf16[2048,2,128]{0,2,1:T(8,128)(2,...) while((s32[]{:T(128)}, f32[4096,2,128]{2,1,0:T(2,128)}, ...), condition=%wide.region_11.12_spmd, body=%wide.region_9.11_spmd.sunk | while | flops 3442587648 | bytes 218378640 | solution.py:325
  1203.6 5.1 copy.222
  1208.8 11.2 fusion.207
  1220.0 10.0 fusion.208
  1230.0 14.8 fusion.209
  1244.8 14.7 fusion.210
  1287.1 5.1 copy.222
  1292.2 11.3 fusion.207
  1303.5 9.9 fusion.208
  1313.5 14.8 fusion.209
  1328.2 14.6 fusion.210
  1370.5 5.2 copy.222
  1375.7 11.2 fusion.207
  1386.9 9.9 fusion.208
  1396.9 14.8 fusion.209
  1411.6 14.6 fusion.210
  1453.8 5.1 copy.222
  1459.0 11.3 fusion.207
  1470.2 9.9 fusion.208
  1480.2 14.8 fusion.209
  1494.9 14.7 fusion.210
  1527.4 5.1 all-to-all-start.5
  1542.2 14.5 all-to-all-done.5
  1566.8 19.3 all-to-all-done.4
  1595.3 4.7 copy.168
  1600.0 6.6 reshape.623
  1612.6 9.4 fusion.133
  1629.7 89.2 %reduce-scatter.35.cloned.1.call-done = f32[144,128]{1,0:T(8,128)} async-done(((f32[4608,128]{1,0:T(8,128)}), f32[144,128]{1,0:T(8,128)}) %reduce-scatter.35.cloned.1.call-update) | async-done | bytes 73744
  1722.8 4.6 fusion.135
  1731.0 100.1 %reduce-scatter.33.cloned.1.call-done = f32[288,128]{1,0:T(8,128)} async-done(((f32[9216,128]{1,0:T(8,128)}), f32[288,128]{1,0:T(8,128)}) %reduce-scatter.33.cloned.1.call-update) | async-done | bytes 147472
  1833.5 134.2 %reduce-scatter.25.cloned.1.call-done = f32[64,128]{1,0:T(8,128)} async-done(((f32[2048,128]{1,0:T(8,128)}), f32[64,128]{1,0:T(8,128)}) %reduce-scatter.25.cloned.1.call-update) | async-done | bytes 32784
  1969.3 145.5 %reduce-scatter.23.cloned.1.call-done = f32[8,48,32]{1,2,0:T(8,128)} async-done(((f32[8,48,1024]{1,2,0:T(8,128)}), f32[8,48,32]{1,2,0:T(8,128)}) %reduce-scatter.23.cloned.1.call-update) | async-done | bytes 49168 | tf_op jit(solution)/shard_map/reduce_scatter | solution.py:362
  (491 shorter events, 324.7 us)
Async XLA Ops:
  7.2 304.3 %all-gather.7.cloned.1.call-start = ((), (), s32[]{:S(2)}) async-start(), calls=%async_computation.14 | async-start | bytes 4325376 | tf_op jit(solution)/shard_map/all_gather | solution.py:151
  7.9 920.9 %all-gather.17.cloned.1.call-start = ((), (), s32[]{:S(2)}) async-start(), calls=%async_computation.19 | async-start | bytes 9732096 | tf_op jit(solution)/shard_map/all_gather | solution.py:161
  9.7 928.9 %all-gather.13.cloned.1.call-start = ((), (), s32[]{:S(2)}) async-start(), calls=%async_computation.17 | async-start | bytes 19464192 | tf_op jit(solution)/shard_map/all_gather | solution.py:160
  11.9 947.2 %all-gather.9.cloned.1.call-start = ((), (), s32[]{:S(2)}) async-start(), calls=%async_computation.15 | async-start | bytes 2162688 | tf_op jit(solution)/shard_map/all_gather | solution.py:152
  12.5 963.1 %all-gather.15.cloned.1.call-start = ((), (), s32[]{:S(2)}) async-start(), calls=%async_computation.18 | async-start | bytes 9732096 | tf_op jit(solution)/shard_map/all_gather | solution.py:154
  187.1 120.8 %copy-start.85 = (f32[1024]{0:T(1024)S(1)}, f32[1024]{0:T(1024)}, u32[]{:S(2)}) copy-start(f32[1024]{0:T(1024)} %param.28) | copy-start | bytes 12292
  187.6 123.4 %copy-start.35 = (bf16[1,16,2048]{2,1,0:T(8,128)(2,1)}, bf16[1,16,2048]{2,1,0:T(8,128)(2,1)S(1)}, u32[]{:S(2)}) copy-start(bf16[1,16,2048]{2,1,0:T(8,128)(2,1)S(1)} %copy.189) | copy-start | bytes 196612
  187.9 121.7 %copy-start.70 = (f32[512]{0:T(512)}, f32[512]{0:T(512)S(1)}, u32[]{:S(2)}) copy-start(f32[512]{0:T(512)S(1)} %fusion.55) | copy-start | bytes 6148
  187.9 123.5 %copy-start.78 = (f32[512]{0:T(512)}, f32[512]{0:T(512)S(1)}, u32[]{:S(2)}) copy-start(f32[512]{0:T(512)S(1)} %fusion.118) | copy-start | bytes 6148
  188.3 144.4 %copy-start.27 = (f32[512,32]{0,1:T(8,128)}, f32[512,32]{0,1:T(8,128)S(1)}, u32[]{:S(2)}) copy-start(f32[512,32]{0,1:T(8,128)S(1)} %get-tuple-element.425) | copy-start | bytes 196612
  188.3 144.4 %copy-start.29 = (f32[512,32]{0,1:T(8,128)}, f32[512,32]{0,1:T(8,128)S(1)}, u32[]{:S(2)}) copy-start(f32[512,32]{0,1:T(8,128)S(1)} %get-tuple-element.426) | copy-start | bytes 196612
  321.7 43.2 %all-to-all-start = ((bf16[512,8,128]{0,2,1:T(8,128)(2,1)}), bf16[512,8,128]{0,2,1:T(8,128)(2,1)S(1)}, u32[]{:S(2)}, u32[]{:S(2)}) async-start(bf16[512,8,128]{0,2,1:T(8,128)(2,1)} %pad_maximum_fusion), calls=%async_computation | async-start | bytes 2097152 | tf_op jit(solution)/shard_map/all_to_all | solution.py:186
  325.2 661.6 %all-gather.11.cloned.1.call-start = ((), (), s32[]{:S(2)}) async-start(), calls=%async_computation.16 | async-start | bytes 19464192 | tf_op jit(solution)/shard_map/all_gather | solution.py:153
  334.1 37.5 %copy-start.67 = (bf16[8,16,32]{2,1,0:T(8,128)(2,1)S(1)}, bf16[8,16,32]{2,1,0:T(8,128)(2,1)}, u32[]{:S(2)}) copy-start(bf16[8,16,32]{2,1,0:T(8,128)(2,1)} %param.38) | copy-start | bytes 24580
  334.1 38.2 %copy-start.68 = (bf16[8,16,32]{2,1,0:T(8,128)(2,1)S(1)}, bf16[8,16,32]{2,1,0:T(8,128)(2,1)}, u32[]{:S(2)}) copy-start(bf16[8,16,32]{2,1,0:T(8,128)(2,1)} %param.39) | copy-start | bytes 24580
  334.1 38.9 %copy-start.66 = (bf16[8,32,32]{2,1,0:T(8,128)(2,1)S(1)}, bf16[8,32,32]{2,1,0:T(8,128)(2,1)}, u32[]{:S(2)}) copy-start(bf16[8,32,32]{2,1,0:T(8,128)(2,1)} %param.40) | copy-start | bytes 49156
  334.1 39.0 %copy-start.69 = (bf16[8,16,32]{2,1,0:T(8,128)(2,1)S(1)}, bf16[8,16,32]{2,1,0:T(8,128)(2,1)}, u32[]{:S(2)}) copy-start(bf16[8,16,32]{2,1,0:T(8,128)(2,1)} %param.43) | copy-start | bytes 24580
  364.9 245.7 %all-to-all-start.1 = ((bf16[512,8,128]{0,2,1:T(8,128)(2,1)}), bf16[512,8,128]{0,2,1:T(8,128)(2,1)S(1)}, u32[]{:S(2)}, u32[]{:S(2)}) async-start(bf16[512,8,128]{0,2,1:T(8,128)(2,1)} %bitcast.37), calls=%async_computation.1 | async-start | bytes 2097152 | tf_op jit(solution)/shard_map/all_to_all | solution.py:183
  368.5 244.1 %collective-permute-start = (bf16[2048,2,128]{0,2,1:T(8,128)(2,1)S(1)}, bf16[2048,2,128]{0,2,1:T(8,128)(2,1)}, u32[]{:S(2)}, u32[]{:S(2)}) collective-permute-start(bf16[2048,2,128]{0,2,1:T(8,128)(2,1)S(1)} %bitcast.327), channel_id=1, source_target_pairs={{0,4},{4,8},{8,12},{12,16},{16,20},{20,24},{24,28},{1,5},{5,9},{9,... | collective-permute-start | bytes 3145736 | tf_op jit(solution)/shard_map/ppermute | solution.py:27
  489.2 121.3 %copy-start.65 = (s32[16384]{0:T(1024)S(1)}, s32[16384]{0:T(1024)}, u32[]{:S(2)}) copy-start(s32[16384]{0:T(1024)} %param.26) | copy-start | bytes 196612
  722.7 9.5 copy-start.31
  722.7 9.5 copy-start.87
  722.7 13.2 copy-start.50
  732.2 107.8 %copy-start.49 = (bf16[8,16,32]{1,0,2:T(8,128)(2,1)S(1)}, bf16[8,16,32]{1,0,2:T(8,128)(2,1)}, u32[]{:S(2)}) copy-start(bf16[8,16,32]{1,0,2:T(8,128)(2,1)} %copy.131) | copy-start | bytes 24580
  732.2 225.9 %all-to-all-start.2 = ((bf16[2048,2,128]{2,1,0:T(2,128)(2,1)}), bf16[2048,2,128]{2,1,0:T(2,128)(2,1)S(1)}, u32[]{:S(2)}, u32[]{:S(2)}) async-start(bf16[2048,2,128]{2,1,0:T(2,128)(2,1)} %copy.128), calls=%async_computation.2 | async-start | bytes 2097152 | tf_op jit(solution)/shard_map/all_to_all | solution.py:244
  735.9 887.6 %reduce-scatter.37.cloned.1.call-start = ((), (), s32[]{:S(2)}) async-start(), calls=%async_computation.27 | async-start | bytes 540672
  839.2 88.7 %copy-start.17 = (bf16[512,1024]{1,0:T(8,128)(2,1)S(1)}, bf16[512,1024]{1,0:T(8,128)(2,1)}, u32[]{:S(2)}) copy-start(bf16[512,1024]{1,0:T(8,128)(2,1)} %param.25) | copy-start | bytes 3145732
  839.2 88.7 %copy-start.43 = (bf16[1,16,1024]{2,1,0:T(8,128)(2,1)S(1)}, bf16[1,16,1024]{2,1,0:T(8,128)(2,1)}, u32[]{:S(2)}) copy-start(bf16[1,16,1024]{2,1,0:T(8,128)(2,1)} %copy.195) | copy-start | bytes 98308
  840.0 122.6 %copy-start.39 = (bf16[1,16,1024]{2,1,0:T(8,128)(2,1)}, bf16[1,16,1024]{2,1,0:T(8,128)(2,1)S(1)}, u32[]{:S(2)}) copy-start(bf16[1,16,1024]{2,1,0:T(8,128)(2,1)S(1)} %copy.191) | copy-start | bytes 98308
  926.6 32.2 %copy-start.45 = (bf16[1,16,1024]{2,1,0:T(8,128)(2,1)}, bf16[1,16,1024]{2,1,0:T(8,128)(2,1)S(1)}, u32[]{:S(2)}) copy-start(bf16[1,16,1024]{2,1,0:T(8,128)(2,1)S(1)} %copy.190) | copy-start | bytes 98308
  959.0 3.6 copy-start.13
  963.3 78.8 %copy-start.8 = (f32[512,1024]{1,0:T(8,128)}, f32[512,1024]{1,0:T(8,128)S(1)}, u32[]{:S(2)}) copy-start(f32[512,1024]{1,0:T(8,128)S(1)} %get-tuple-element.431) | copy-start | bytes 6291460
  970.6 5.0 copy-start.18
  1036.0 3.6 copy-start.5
  1042.1 18.3 copy-start.73
  1042.1 18.4 copy-start.75
  1063.2 28.0 %copy-start.6 = (f32[512,1024]{1,0:T(8,128)}, f32[512,1024]{1,0:T(8,128)S(1)}, u32[]{:S(2)}) copy-start(f32[512,1024]{1,0:T(8,128)S(1)} %fusion.53) | copy-start | bytes 6291460
  1064.3 4.6 copy-start.16
  1064.3 5.0 copy-start.76
  1077.8 547.2 %reduce-scatter.29.cloned.1.call-start = ((), (), s32[]{:S(2)}) async-start(), calls=%async_computation.23 | async-start | bytes 540672
  1084.5 542.0 %reduce-scatter.27.cloned.1.call-start = ((), (), s32[]{:S(2)}) async-start(), calls=%async_computation.22 | async-start | bytes 540672
  1094.6 5.2 copy-start.20
  1094.6 5.2 copy-start.61
  1094.6 5.2 copy-start.63
  1095.8 88.6 %all-to-all-start.3 = ((bf16[512,8,128]{2,0,1:T(8,128)(2,1)}), bf16[512,8,128]{2,0,1:T(8,128)(2,1)S(1)}, u32[]{:S(2)}, u32[]{:S(2)}) async-start(bf16[512,8,128]{2,0,1:T(8,128)(2,1)} %bitcast.232), calls=%async_computation.3 | async-start | bytes 2097152 | tf_op jit(solution)/shard_map/all_to_all | solution.py:281
  1099.3 528.8 %reduce-scatter.31.cloned.1.call-start = ((), (), s32[]{:S(2)}) async-start(), calls=%async_computation.24 | async-start | bytes 1081344
  1103.0 4.3 copy-start.59
  1107.2 611.7 %reduce-scatter.35.cloned.1.call-start = ((), (), s32[]{:S(2)}) async-start(), calls=%async_computation.26 | async-start | bytes 2433024
  1138.8 692.3 %reduce-scatter.33.cloned.1.call-start = ((), (), s32[]{:S(2)}) async-start(), calls=%async_computation.25 | async-start | bytes 4866048
  1220.0 10.0 copy-start.2
  1303.5 9.9 copy-start.2
  1344.9 3.3 copy-start
  1386.9 9.9 copy-start.2
  1470.2 9.9 copy-start.2
  1527.4 29.4 %all-to-all-start.5 = ((bf16[2048,2,128]{2,1,0:T(2,128)(2,1)}), bf16[2048,2,128]{2,1,0:T(2,128)(2,1)S(1)}, u32[]{:S(2)}, u32[]{:S(2)}) async-start(bf16[2048,2,128]{2,1,0:T(2,128)(2,1)} %copy.150), calls=%async_computation.5 | async-start | bytes 2097152 | tf_op jit(solution)/shard_map/all_to_all | solution.py:338
  1534.5 4.6 collective-permute-start.1
  1556.8 29.3 %all-to-all-start.4 = ((bf16[2048,2,128]{2,1,0:T(2,128)(2,1)}), bf16[2048,2,128]{2,1,0:T(2,128)(2,1)S(1)}, u32[]{:S(2)}, u32[]{:S(2)}) async-start(bf16[2048,2,128]{2,1,0:T(2,128)(2,1)} %add_convert_fusion.2), calls=%async_computation.4 | async-start | bytes 2097152 | tf_op jit(solution)/shard_map/all_to_all | solution.py:339
  1560.3 407.4 %reduce-scatter.25.cloned.1.call-start = ((), (), s32[]{:S(2)}) async-start(), calls=%async_computation.21 | async-start | bytes 1081344
  1600.0 6.7 copy-start.36
  1600.0 9.2 copy-start.22
  1606.7 508.2 %reduce-scatter.23.cloned.1.call-start = ((), (), s32[]{:S(2)}) async-start(), calls=%async_computation.20 | async-start | bytes 4325376 | tf_op jit(solution)/shard_map/reduce_scatter | solution.py:362
  1612.5 9.4 copy-start.9
  1612.6 9.4 copy-start.44
  1612.6 9.4 copy-start.54
  (53 other events, 98.2 us)
Sparse Core Ops, SparseCore 0:
  11.0 74.8 all-gather.6
  88.7 105.8 all-gather.16
  197.4 161.0 all-gather.12
  361.2 68.7 all-gather.8
  432.6 100.4 all-gather.14
  535.8 138.1 all-gather.10
  1078.0 130.9 reduce-scatter.36
  1211.3 131.3 reduce-scatter.28
  1345.0 130.4 reduce-scatter.26
  1477.6 137.8 reduce-scatter.30
  1620.8 98.0 reduce-scatter.34
  1725.1 105.9 reduce-scatter.32
  1833.3 134.3 reduce-scatter.24
  1970.5 144.2 reduce-scatter.22
where the time goes:
time: 2130 us; the launch traced here: 2120 us
  blocking collectives  710 us (33%)
  waiting for transfers between devices  539 us (25%)
  matrix products  355 us (17%)
  local copies, waits for them, and re-layouts  296 us (14%)
  other arithmetic  138 us (6%)
  loops' own time  37.2 us (2%)
  starting transfers between devices  28.1 us (1%)
    unnamed x21, waiting for transfers between devices  326 us
    all_gather x1, blocking collectives, local(): lax.all_gather(qkv_up, ('ctx', 'head'), axis=2, tiled=True)  169 us
    unnamed x217, local copies, waits for them, and re-layouts  157 us
    reduce_scatter x1, waiting for transfers between devices, local(): lax.psum_scatter(spread[0], ('ctx', 'head'), scatter_dimension=2, tiled=T...  145 us
    all_gather x1, blocking collectives, local(): lax.all_gather(mlp_down, ('ctx', 'head'), axis=2, tiled=True)  118 us
    all_gather x1, blocking collectives, local(): lax.all_gather(qkv_down, ('ctx', 'head'), axis=2, tiled=True)  118 us
    all_gather x1, blocking collectives, local(): lax.all_gather(ffd_up, ('ctx', 'head'), axis=2, tiled=True)  116 us
    all_gather x1, blocking collectives, local(): lax.all_gather(out_up, ('ctx', 'head'), axis=2, tiled=True)  103 us
  transfers between devices with their start and end apart: 22, of which 8 were waited for; matrix products, arithmetic and copies ran while one was open for 32% of the time, Pallas kernels for 0%

commit v1 on v0

v1 whole, which is shorter than its diff:
```python
import functools
import math

import jax
import jax.numpy as jnp
from jax import lax
from jax.experimental import pallas as pl
from jax.experimental.pallas import tpu as pltpu
from jax.sharding import PartitionSpec as P

D = 1024
HEADS = 16
KV_HEADS = 8
HEAD_DIM = 64
FF = 4608
RANK = 16
ADAPTERS = 8
NSEQ = 4
SEGMAX = 2048
QW = 1024
KW = 512
PAIR = 2 * HEAD_DIM
BLOCK = 256
AXES = ("ctx", "head")

epsilon = 1e-05
rope_base = 1000000.0
LOG2E = math.log2(math.e)
QSCALE = HEAD_DIM**-0.5 * LOG2E
F32 = jnp.float32
BF16 = jnp.bfloat16


def matmul(left_side, right_side):
    return jnp.dot(left_side, right_side, preferred_element_type=F32)


def contract_rows(left_side, right_side):
    return lax.dot_general(left_side, right_side, (((0,), (0,)), ((), ())), preferred_element_type=F32)


def contract_cols(left_side, right_side):
    return lax.dot_general(left_side, right_side, (((1,), (1,)), ((), ())), preferred_element_type=F32)


def rms_norm(values, gain_row):
    return values * lax.rsqrt(jnp.mean(values * values, axis=-1, keepdims=True) + epsilon) * gain_row


def rope_tables(positions):
    middle = HEAD_DIM // 2
    frequency = jnp.power(rope_base, -(2.0 / HEAD_DIM) * jnp.arange(middle, dtype=F32))
    angles = positions.astype(F32)[:, None] * frequency[None, :]
    return (jnp.cos(angles)[:, None, :], jnp.sin(angles)[:, None, :])


def rotate(values, cosine, sine_part):
    middle = values.shape[-1] // 2
    leading = values[..., :middle]
    trailing = values[..., middle:]
    return jnp.concatenate(
        [leading * cosine - trailing * sine_part, trailing * cosine + leading * sine_part], axis=-1
    )


def prepare_heads(projected, positions, query_gain, key_gain):
    length = projected.shape[0]
    cosine, sine_part = rope_tables(positions)
    query_rows = projected[:, :QW].reshape(length, HEADS, HEAD_DIM)
    key_rows = projected[:, QW : QW + KW].reshape(length, KV_HEADS, HEAD_DIM)
    value_rows = projected[:, QW + KW :].reshape(length, KV_HEADS, HEAD_DIM)
    query_rows = rotate(rms_norm(query_rows, query_gain), cosine, sine_part)
    key_rows = rotate(rms_norm(key_rows, key_gain), cosine, sine_part)
    grouped = query_rows.reshape(length, KV_HEADS, PAIR)
    return (grouped, jnp.concatenate([key_rows, value_rows], axis=-1))


def rank_apply(reduced, up_rows, bounds):
    return jnp.concatenate(
        [
            matmul(
                reduced[:, RANK * member : RANK * (member + 1)],
                up_rows[:, bounds[member] : bounds[member + 1]],
            )
            for member in range(len(bounds) - 1)
        ],
        axis=1,
    )


def rank_back(grad_low, reduced, up_rows, bounds):
    up_grad = jnp.concatenate(
        [
            contract_rows(
                reduced[:, RANK * member : RANK * (member + 1)],
                grad_low[:, bounds[member] : bounds[member + 1]],
            )
            for member in range(len(bounds) - 1)
        ],
        axis=1,
    )
    reduced_grad = jnp.concatenate(
        [
            contract_cols(
                grad_low[:, bounds[member] : bounds[member + 1]],
                up_rows[:, bounds[member] : bounds[member + 1]],
            )
            for member in range(len(bounds) - 1)
        ],
        axis=1,
    )
    return (up_grad, reduced_grad)


VMEM_SPEC = pl.BlockSpec(memory_space=pltpu.VMEM)
SMEM_SPEC = pl.BlockSpec(memory_space=pltpu.SMEM)


def lane_pad(width):
    return -(-width // 128) * 128


def layout_of(shapes):
    places = []
    offset = 0
    for index, (rows, width) in enumerate(shapes):
        for part in range(rows // RANK):
            places.append((index, part, offset, width))
            offset += width
    return places, lane_pad(offset)


def pack_adapters(adapter_ids, members, devices):
    places, width = layout_of([member.shape[1:] for member in members])
    per_seq = devices // NSEQ

    def kernel(ids, *refs):
        sources, out, slab = refs[: len(members)], refs[len(members)], refs[len(members) + 1]
        slab[...] = jnp.zeros_like(slab)
        for index, part, offset, size in places:
            slab[:, offset : offset + size] = sources[index][
                ids[pl.program_id(0)], RANK * part : RANK * (part + 1), :
            ]
        for step in range(per_seq):
            out[step] = slab[...]

    return pl.pallas_call(
        kernel,
        grid=(NSEQ,),
        in_specs=[SMEM_SPEC] + [pl.BlockSpec(member.shape, lambda s: (0, 0, 0)) for member in members],
        out_specs=pl.BlockSpec((per_seq, RANK, width), lambda s: (s, 0, 0)),
        out_shape=jax.ShapeDtypeStruct((devices, RANK, width), BF16),
        scratch_shapes=[pltpu.VMEM((RANK, width), BF16)],
        name="pack_adapters",
    )(adapter_ids, *members)


def unpack_adapters(slabs, shapes):
    devices = slabs.shape[0]
    places, _ = layout_of(shapes)

    def kernel(source, *outs):
        for index, part, offset, size in places:
            for device in range(devices):
                outs[index][RANK * part : RANK * (part + 1), device * size : (device + 1) * size] = source[
                    device, :, offset : offset + size
                ]

    return pl.pallas_call(
        kernel,
        in_specs=[VMEM_SPEC],
        out_specs=[VMEM_SPEC] * len(shapes),
        out_shape=[jax.ShapeDtypeStruct((rows, width * devices), BF16) for rows, width in shapes],
        name="unpack_adapters",
    )(slabs)


def pack_grads(grads, devices):
    places, width = layout_of([(grad.shape[0], grad.shape[1] // devices) for grad in grads])

    def kernel(*refs):
        sources, out = refs[: len(grads)], refs[len(grads)]
        for device in range(devices):
            for index, part, offset, size in places:
                out[device, :, offset : offset + size] = sources[index][
                    RANK * part : RANK * (part + 1), device * size : (device + 1) * size
                ].astype(BF16)

    return pl.pallas_call(
        kernel,
        in_specs=[VMEM_SPEC] * len(grads),
        out_specs=VMEM_SPEC,
        out_shape=jax.ShapeDtypeStruct((devices, RANK, width), BF16),
        name="pack_grads",
    )(*grads)


def reduce_grads(adapter_ids, slabs, shapes):
    devices, _, width = slabs.shape
    places, _ = layout_of(shapes)
    per_seq = devices // NSEQ

    def kernel(ids, source, *refs):
        outs, total = refs[: len(shapes)], refs[len(shapes)]
        total[...] = jnp.zeros_like(total)
        for seq in range(NSEQ):
            part_sum = jnp.sum(source[seq * per_seq : (seq + 1) * per_seq].astype(F32), axis=0)
            total[ids[seq]] += part_sum
        for index, part, offset, size in places:
            outs[index][:, RANK * part : RANK * (part + 1), :] = total[:, :, offset : offset + size]

    return pl.pallas_call(
        kernel,
        in_specs=[SMEM_SPEC, VMEM_SPEC],
        out_specs=[VMEM_SPEC] * len(shapes),
        out_shape=[jax.ShapeDtypeStruct((ADAPTERS, rows, size), F32) for rows, size in shapes],
        scratch_shapes=[pltpu.VMEM((ADAPTERS, RANK, width), F32)],
        name="reduce_grads",
    )(adapter_ids, slabs)


def split_three(value):
    first = value.astype(BF16)
    rest = value - first.astype(F32)
    second = rest.astype(BF16)
    third = (rest - second.astype(F32)).astype(BF16)
    return first, second, third


def with_columns(block, columns, lanes):
    out = jnp.where(lanes < HEAD_DIM, block, jnp.zeros_like(block))
    for step, column in enumerate(columns):
        out = jnp.where(lanes == HEAD_DIM + step, column, out)
    return out


def stacked_heads(pair, lanes):
    return jnp.concatenate([pair, pltpu.roll(pair, HEAD_DIM, 1)], axis=0)


def allowed(start_row, key_base, query_base, diagonal):
    keys = key_base + lax.broadcasted_iota(jnp.int32, (BLOCK, BLOCK), 0)
    inside = keys >= start_row
    if diagonal:
        queries = query_base + lax.broadcasted_iota(jnp.int32, (BLOCK, BLOCK), 1)
        inside = inside & (keys <= queries)
    return jnp.concatenate([inside, inside], axis=1)


def forward_attention(bounds, starts, queries, keyvals):
    rows = queries.shape[0]
    length = keyvals.shape[0]
    halo = length - rows
    steps = rows // BLOCK

    def kernel(bound_ref, start_ref, query_ref, keyval_ref, out_ref, log_ref, key_scr, value_scr):
        step = pl.program_id(0)

        @pl.when(step == 0)
        def _():
            lanes = lax.broadcasted_iota(jnp.int32, (length, 128), 1)
            both = keyval_ref[...].astype(F32)
            key_scr[...] = jnp.where(lanes < HEAD_DIM, both, 0.0).astype(BF16)
            values = jnp.where(lanes < HEAD_DIM, pltpu.roll(both, HEAD_DIM, 1), 1.0)
            value_scr[...] = values.T.astype(BF16)

        lanes = lax.broadcasted_iota(jnp.int32, (BLOCK, 128), 1)
        pair = query_ref[...].astype(F32)
        query = stacked_heads(pair, lanes).astype(BF16)
        start_row = start_ref[...]
        diagonal = halo // BLOCK + step
        first = bound_ref[0, step]
        clear = jnp.minimum(bound_ref[1, step], diagonal)

        def block(index, total, masked, is_diagonal):
            base = pl.multiple_of(index * BLOCK, BLOCK)
            scores = contract_cols(key_scr[pl.ds(base, BLOCK), :], query)
            weights = jnp.exp2(scores)
            if masked:
                keep = allowed(start_row, base, diagonal * BLOCK, is_diagonal)
                weights = jnp.where(keep, weights, 0.0)
            return total + matmul(value_scr[:, pl.ds(base, BLOCK)], weights.astype(BF16))

        total = jnp.zeros((128, 2 * BLOCK), F32)
        total = lax.fori_loop(first, clear, lambda i, t: block(i, t, True, False), total)
        total = lax.fori_loop(clear, diagonal, lambda i, t: block(i, t, False, False), total)
        total = block(diagonal, total, True, True)
        norm = total[HEAD_DIM : HEAD_DIM + 1, :]
        mixed = total[:HEAD_DIM, :] / norm
        out_ref[...] = jnp.concatenate([mixed[:, :BLOCK], mixed[:, BLOCK:]], axis=0).T.astype(BF16)
        log_ref[0] = jnp.broadcast_to(jnp.log2(norm), (8, 2 * BLOCK))

    return pl.pallas_call(
        kernel,
        grid_spec=pltpu.PrefetchScalarGridSpec(
            num_scalar_prefetch=1,
            grid=(steps,),
            in_specs=[
                pl.BlockSpec((1, BLOCK), lambda i, b: (0, i)),
                pl.BlockSpec((BLOCK, 128), lambda i, b: (i, 0)),
                pl.BlockSpec((length, 128), lambda i, b: (0, 0)),
            ],
            out_specs=[
                pl.BlockSpec((BLOCK, 128), lambda i, b: (i, 0)),
                pl.BlockSpec((1, 8, 2 * BLOCK), lambda i, b: (i, 0, 0)),
            ],
            scratch_shapes=[pltpu.VMEM((length, 128), BF16), pltpu.VMEM((128, length), BF16)],
        ),
        out_shape=[
            jax.ShapeDtypeStruct((rows, 128), BF16),
            jax.ShapeDtypeStruct((steps, 8, 2 * BLOCK), F32),
        ],
        compiler_params=pltpu.CompilerParams(vmem_limit_bytes=40 << 20),
        cost_estimate=pl.CostEstimate(
            flops=4 * rows * 1024 * 256 * 2, bytes_accessed=4 * rows * 256, transcendentals=rows * 2048
        ),
        name="forward_attention",
    )(bounds, starts, queries, keyvals)


def backward_attention(bounds, starts, queries, keyvals, mixed, logs, grads):
    rows = queries.shape[0]
    length = keyvals.shape[0]
    halo = length - rows
    steps = rows // BLOCK

    def kernel(
        bound_ref, start_ref, query_ref, keyval_ref, mixed_ref, log_ref, grad_ref,
        query_out, keyval_out, key_scr, value_scr, turned_scr, key_sum, value_sum,
    ):
        step = pl.program_id(0)

        @pl.when(step == 0)
        def _():
            lanes = lax.broadcasted_iota(jnp.int32, (length, 128), 1)
            both = keyval_ref[...].astype(F32)
            ones = jnp.where(lanes < HEAD_DIM + 3, 1.0, 0.0)
            keys = jnp.where(lanes < HEAD_DIM, both, ones)
            key_scr[...] = keys.astype(BF16)
            value_scr[...] = jnp.where(lanes < HEAD_DIM, pltpu.roll(both, HEAD_DIM, 1), ones).astype(BF16)
            turned_scr[...] = keys.T.astype(BF16)
            key_sum[...] = jnp.zeros_like(key_sum)
            value_sum[...] = jnp.zeros_like(value_sum)

        lanes = lax.broadcasted_iota(jnp.int32, (2 * BLOCK, 128), 1)
        query = stacked_heads(query_ref[...].astype(F32), lanes)
        grad = stacked_heads(grad_ref[...].astype(F32), lanes)
        weighed = stacked_heads(mixed_ref[...].astype(F32), lanes)
        inner = jnp.sum(jnp.where(lanes < HEAD_DIM, grad * weighed, 0.0), axis=1, keepdims=True)
        log_column = log_ref[0].T[:, :1]
        query_low = with_columns(query, [part.astype(F32) for part in split_three(-log_column)], lanes).astype(BF16)
        grad_low = with_columns(grad, [part.astype(F32) for part in split_three(-inner)], lanes).astype(BF16)
        start_row = start_ref[...]
        diagonal = halo // BLOCK + step
        first = bound_ref[0, step]
        clear = jnp.minimum(bound_ref[1, step], diagonal)

        def block(index, total, masked, is_diagonal):
            base = pl.multiple_of(index * BLOCK, BLOCK)
            where = pl.ds(base, BLOCK)
            weights = jnp.exp2(contract_cols(key_scr[where, :], query_low))
            if masked:
                keep = allowed(start_row, base, diagonal * BLOCK, is_diagonal)
                weights = jnp.where(keep, weights, 0.0)
            slopes = (weights * contract_cols(value_scr[where, :], grad_low)).astype(BF16)
            value_sum[where, :] += matmul(weights.astype(BF16), grad_low)
            key_sum[where, :] += matmul(slopes, query_low)
            return total + matmul(turned_scr[:, where], slopes)

        total = jnp.zeros((128, 2 * BLOCK), F32)
        total = lax.fori_loop(first, clear, lambda i, t: block(i, t, True, False), total)
        total = lax.fori_loop(clear, diagonal, lambda i, t: block(i, t, False, False), total)
        total = block(diagonal, total, True, True)
        total = total[:HEAD_DIM] * HEAD_DIM**-0.5
        query_out[...] = jnp.concatenate([total[:, :BLOCK], total[:, BLOCK:]], axis=0).T.astype(BF16)

        @pl.when(step == steps - 1)
        def _():
            whole = lax.broadcasted_iota(jnp.int32, (length, 128), 1)
            keyval_out[...] = jnp.where(
                whole < HEAD_DIM, key_sum[...] * (1.0 / LOG2E), pltpu.roll(value_sum[...], HEAD_DIM, 1)
            ).astype(keyval_out.dtype)

    return pl.pallas_call(
        kernel,
        grid_spec=pltpu.PrefetchScalarGridSpec(
            num_scalar_prefetch=1,
            grid=(steps,),
            in_specs=[
                pl.BlockSpec((1, BLOCK), lambda i, b: (0, i)),
                pl.BlockSpec((BLOCK, 128), lambda i, b: (i, 0)),
                pl.BlockSpec((length, 128), lambda i, b: (0, 0)),
                pl.BlockSpec((BLOCK, 128), lambda i, b: (i, 0)),
                pl.BlockSpec((1, 8, 2 * BLOCK), lambda i, b: (i, 0, 0)),
                pl.BlockSpec((BLOCK, 128), lambda i, b: (i, 0)),
            ],
            out_specs=[
                pl.BlockSpec((BLOCK, 128), lambda i, b: (i, 0)),
                pl.BlockSpec((length, 128), lambda i, b: (0, 0)),
            ],
            scratch_shapes=[
                pltpu.VMEM((length, 128), BF16),
                pltpu.VMEM((length, 128), BF16),
                pltpu.VMEM((128, length), BF16),
                pltpu.VMEM((length, 128), F32),
                pltpu.VMEM((length, 128), F32),
            ],
        ),
        out_shape=[
            jax.ShapeDtypeStruct((rows, 128), BF16),
            jax.ShapeDtypeStruct((length, 128), F32 if halo else BF16),
        ],
        compiler_params=pltpu.CompilerParams(vmem_limit_bytes=48 << 20),
        cost_estimate=pl.CostEstimate(
            flops=10 * rows * 1024 * 256 * 2, bytes_accessed=8 * rows * 256, transcendentals=rows * 2048
        ),
        name="backward_attention",
    )(bounds, starts, queries, keyvals, mixed, logs, grads)


def document_bounds(segment_ids, origin, halo, span, seq_start):
    tokens = segment_ids.shape[0]
    names = jnp.arange(tokens // (SEGMAX // 2), dtype=jnp.int32)
    begin = jnp.sum((segment_ids[None, :] < names[:, None]).astype(jnp.int32), axis=1)
    own = lax.dynamic_slice_in_dim(segment_ids, origin, span, 0)
    start = jnp.sum(jnp.where(own[None, :] == names[:, None], begin[:, None], 0), axis=0)
    start = jnp.maximum(start, seq_start) - (origin - halo)
    first = start[::BLOCK] // BLOCK
    clear = -(-start[BLOCK - 1 :: BLOCK] // BLOCK)
    bounds = jnp.stack([first, jnp.maximum(clear, first)])
    return bounds, start[None, :]


def local(
    hidden, cotangent, segment_ids, adapter_ids, attn_gain, query_gain, key_gain, ffn_gain,
    qkv_weight, out_weight, gate_up_weight, down_weight, *adapters,
):
    rows = hidden.shape[0]
    devices = lax.axis_size("ctx") * lax.axis_size("head")
    members = KV_HEADS
    groups = [[members * g + i for i in range(members)] for g in range(devices // members)]
    span = rows * members
    seq_length = rows * devices // NSEQ
    halo = 0 if span == seq_length else SEGMAX
    here = lax.axis_index("ctx") * lax.axis_size("head") + lax.axis_index("head")
    origin = here // members * span
    seq_start = origin // seq_length * seq_length
    positions = here * rows - seq_start + jnp.arange(rows, dtype=jnp.int32)
    bounds, starts = document_bounds(segment_ids, origin, halo, span, seq_start)

    def swap(value):
        return lax.all_to_all(value, AXES, 0, 0, axis_index_groups=groups, tiled=True)

    def shifted(value, by):
        pairs = [(i, i + by) for i in range(devices) if 0 <= i + by < devices]
        return lax.ppermute(value, AXES, pairs)

    def gather(value):
        return lax.all_gather(value, AXES, axis=0, tiled=True)

    shapes = [member.shape[1:] for member in adapters]
    slabs = lax.all_to_all(pack_adapters(adapter_ids, adapters, devices), AXES, 0, 0, tiled=True)
    chosen = unpack_adapters(slabs, shapes)

    qkv_full = gather(qkv_weight)
    out_full = gather(out_weight)
    gate_up_full = gather(gate_up_weight)
    down_full = gather(down_weight)

    qkv_bounds = (0, QW, QW + KW, QW + 2 * KW)
    inputs = hidden.astype(F32)
    normed, norm_pull = jax.vjp(lambda operand: rms_norm(operand, attn_gain), inputs)
    normed_low = normed.astype(BF16)
    reduced_qkv = contract_cols(normed_low, chosen[0]).astype(BF16)
    projected = matmul(normed_low, qkv_full) + rank_apply(reduced_qkv, chosen[1], qkv_bounds)
    (grouped, keyvals), head_pull = jax.vjp(
        lambda operand: prepare_heads(operand, positions, query_gain, key_gain), projected
    )
    sent = jnp.concatenate([grouped * QSCALE, keyvals], axis=-1).astype(BF16).transpose(1, 0, 2)
    arrived = swap(sent).reshape(span, 2 * PAIR)
    queries = arrived[:, :PAIR]
    keyval_rows = arrived[:, PAIR:]
    if halo:
        keyval_rows = jnp.concatenate([shifted(keyval_rows[span - halo :], members), keyval_rows], axis=0)
    mixed, logs = forward_attention(bounds, starts, queries, keyval_rows)
    mixture_tok = swap(mixed.reshape(members, rows, PAIR)).transpose(1, 0, 2).reshape(rows, QW)

    reduced_out = contract_cols(mixture_tok, chosen[2]).astype(BF16)
    branch = matmul(mixture_tok, out_full) + rank_apply(reduced_out, chosen[3], (0, D))
    middle = inputs + branch
    normed_two, norm_two_pull = jax.vjp(lambda operand: rms_norm(operand, ffn_gain), middle)
    normed_two_low = normed_two.astype(BF16)
    reduced_mlp = contract_cols(normed_two_low, chosen[4]).astype(BF16)
    gate_up = matmul(normed_two_low, gate_up_full) + rank_apply(reduced_mlp, chosen[5], (0, FF, 2 * FF))
    hidden_units, unit_pull = jax.vjp(
        lambda operand: jax.nn.silu(operand[:, :FF]) * operand[:, FF:], gate_up
    )
    units_low = hidden_units.astype(BF16)
    reduced_down = contract_cols(units_low, chosen[6]).astype(BF16)
    branch_two = matmul(units_low, down_full) + rank_apply(reduced_down, chosen[7], (0, D))
    output = (middle + branch_two).astype(BF16)

    ffd_up_grad, reduced_down_grad = rank_back(cotangent, reduced_down, chosen[7], (0, D))
    reduced_down_low = reduced_down_grad.astype(BF16)
    ffd_down_grad = contract_rows(reduced_down_low, units_low)
    units_grad = contract_cols(cotangent, down_full) + matmul(reduced_down_low, chosen[6])
    gate_up_grad = unit_pull(units_grad)[0].astype(BF16)
    mlp_up_grad, reduced_mlp_grad = rank_back(gate_up_grad, reduced_mlp, chosen[5], (0, FF, 2 * FF))
    reduced_mlp_low = reduced_mlp_grad.astype(BF16)
    mlp_down_grad = contract_rows(reduced_mlp_low, normed_two_low)
    normed_two_grad = contract_cols(gate_up_grad, gate_up_full) + matmul(reduced_mlp_low, chosen[4])
    middle_grad = cotangent.astype(F32) + norm_two_pull(normed_two_grad)[0]
    branch_grad = middle_grad.astype(BF16)
    out_up_grad, reduced_out_grad = rank_back(branch_grad, reduced_out, chosen[3], (0, D))
    reduced_out_low = reduced_out_grad.astype(BF16)
    out_down_grad = contract_rows(reduced_out_low, mixture_tok)
    mixture_grad = (contract_cols(branch_grad, out_full) + matmul(reduced_out_low, chosen[2])).astype(BF16)
    grad_rows = swap(mixture_grad.reshape(rows, members, PAIR).transpose(1, 0, 2)).reshape(span, PAIR)

    early = [out_down_grad, out_up_grad, mlp_down_grad, mlp_up_grad, ffd_down_grad, ffd_up_grad]
    early_slabs = lax.all_to_all(pack_grads(early, devices), AXES, 0, 0, tiled=True)
    early_owned = reduce_grads(adapter_ids, early_slabs, shapes[2:])

    query_grads, keyval_grads = backward_attention(
        bounds, starts, queries, keyval_rows, mixed, logs, grad_rows
    )
    if halo:
        returned = shifted(keyval_grads[:halo].astype(BF16), -members).astype(F32)
        keyval_grads = jnp.concatenate(
            [keyval_grads[halo : halo + span - halo], keyval_grads[span:] + returned], axis=0
        ).astype(BF16)
    back = jnp.concatenate([query_grads, keyval_grads], axis=1).reshape(members, rows, 2 * PAIR)
    back = swap(back).transpose(1, 0, 2).astype(F32)
    projected_grad = head_pull((back[..., :PAIR], back[..., PAIR:]))[0].astype(BF16)
    qkv_up_grad, reduced_qkv_grad = rank_back(projected_grad, reduced_qkv, chosen[1], qkv_bounds)
    reduced_qkv_low = reduced_qkv_grad.astype(BF16)
    qkv_down_grad = contract_rows(reduced_qkv_low, normed_low)
    late_slabs = lax.all_to_all(pack_grads([qkv_down_grad, qkv_up_grad], devices), AXES, 0, 0, tiled=True)
    late_owned = reduce_grads(adapter_ids, late_slabs, shapes[:2])
    normed_grad = contract_cols(projected_grad, qkv_full) + matmul(reduced_qkv_low, chosen[0])
    input_grad = middle_grad + norm_pull(normed_grad)[0]
    return (output, input_grad, *late_owned, *early_owned)


def solution(mesh):
    by_rows = P(AXES, None)
    by_cols = P(None, None, AXES)
    placed = (by_rows, by_rows) + (P(),) * 6 + (by_rows,) * 4 + (by_cols,) * 8
    return jax.shard_map(
        local,
        mesh=mesh,
        in_specs=placed,
        out_specs=(by_rows, by_rows) + (by_cols,) * 8,
        check_vma=False,
    )
```

time: 2130 us -> 661 us (0.31)
  blocking collectives: 710 us -> 0 us
  local copies, waits for them, and re-layouts: 296 us -> 32.6 us
  matrix products: 355 us -> 138 us
  waiting for transfers between devices: 539 us -> 328 us
  other arithmetic: 138 us -> 23.7 us
  Pallas kernels: 0 us -> 76.6 us
  loops' own time: 37.2 us -> 0 us
    all_gather x6 -> x0, blocking collectives: 710 us -> none  [the longest x1 169 us: local(): lax.all_gather(qkv_up, ('ctx', 'head'), axis=2, tiled=True)]
    unnamed x21 -> x4, waiting for transfers between devices: 326 us -> 2.58 us
    dot_general x43 -> x15, matrix products: 294 us -> 79.3 us  [matmul(): return jnp.dot(left_side, right_side, preferred_element_type=F32)]
    all_gather x6 -> x4, waiting for transfers between devices: 0.03 us -> 159 us  [gather(): return lax.all_gather(value, AXES, axis=0, tiled=True)]
    reduce_scatter x1 -> x0, waiting for transfers between devices: 145 us -> none  [local(): lax.psum_scatter(spread[0], ('ctx', 'head'), scatter_dimension=2, tiled=T...]
    unnamed x217 -> x130, local copies, waits for them, and re-layouts: 157 us -> 15.2 us
    all_to_all x6 -> x7, waiting for transfers between devices: 64.6 us -> 167 us  [the longest x4 139 us: swap(): lax.all_to_all(value, AXES, 0, 0, axis_index_groups=groups, tiled=True)]
    pallas_call x0 -> x8, Pallas kernels: none -> 76.6 us  [the longest x1 37.2 us: backward_attention(): pl.pallas_call(kernel, grid_spec=pltpu.PrefetchScalarGridSpec(num_scalar_...]
  transfers between devices with their start and end apart: 22 -> 11, of which waited for: 8 -> 9; matrix products, arithmetic and copies ran while one was open for 32% -> 13% of each run, Pallas kernels for 0% -> 11%
where the time goes in v1:
time: 661 us; the launch traced here: 653 us
  waiting for transfers between devices  328 us (50%)
  matrix products  138 us (21%)
  Pallas kernels  76.6 us (12%)
  starting transfers between devices  38.4 us (6%)
  local copies, waits for them, and re-layouts  32.6 us (5%)
  other arithmetic  23.7 us (4%)
  between operations  15.2 us (2%)
    all_gather x4, waiting for transfers between devices, gather(): return lax.all_gather(value, AXES, axis=0, tiled=True)  159 us
    all_to_all x4, waiting for transfers between devices, swap(): lax.all_to_all(value, AXES, 0, 0, axis_index_groups=groups, tiled=True)  139 us
    dot_general x15, matrix products, matmul(): return jnp.dot(left_side, right_side, preferred_element_type=F32)  79.3 us
    dot_general x15, matrix products, contract_cols(): lax.dot_general(left_side, right_side, (((1,), (1,)), ((), ())), preferre...  42.9 us
    pallas_call x1, Pallas kernels, backward_attention(): pl.pallas_call(kernel, grid_spec=pltpu.PrefetchScalarGridSpec(num_scalar_...  37.2 us
    pallas_call x1, Pallas kernels, forward_attention(): pl.pallas_call(kernel, grid_spec=pltpu.PrefetchScalarGridSpec(num_scalar_...  25.7 us
    all_to_all x1, waiting for transfers between devices, local(): lax.all_to_all(pack_adapters(adapter_ids, adapters, devices), AXES, 0, 0,...  21.1 us
    all_to_all x4, starting transfers between devices, swap(): lax.all_to_all(value, AXES, 0, 0, axis_index_groups=groups, tiled=True)  17.9 us
  transfers between devices with their start and end apart: 11, of which 9 were waited for; matrix products, arithmetic and copies ran while one was open for 13% of the time, Pallas kernels for 11%

profile of v1, /device:TPU:0, one launch (start us, length us, event | category | flops | bytes accessed | tf_op | source)
XLA Modules:
  0.0 652.6 jit_solution(11875923206673748584)
XLA Ops:
  10.0 1.6 copy.50.refs_0_
  11.6 2.7 pack_adapters.1
  14.3 7.3 %all-to-all-start = ((bf16[32,16,768]{2,1,0:T(8,128)(2,1)}), bf16[32,16,768]{2,1,0:T(8,128)(2,1)S(1)}, u32[]{:S(2)}, u32[]{:S(2)}) async-start(bf16[32,16,768]{2,1,0:T(8,128)(2,1)} %pack_adapters.1), calls=%async_computation | async-start | bytes 1572864 | tf_op jit(solution)/shard_map/all_to_all | solution.py:462
  22.9 21.1 %all-to-all-done.source = bf16[32,16,768]{2,1,0:T(8,128)(2,1)S(1)} async-done(((bf16[32,16,768]{2,1,0:T(8,128)(2,1)}), bf16[32,16,768]{2,1,0:T(8,128)(2,1)S(1)}, u32[]{:S(2)}, u32[]{:S(2)}) %all-to-all-start) | async-done | bytes 786464 | tf_op jit(solution)/shard_map/all_to_all | solution.py:462
  44.9 2.5 unpack_adapters.1
  47.4 1.4 convolution_convert_fusion
  48.8 2.0 fusion.49
  50.9 1.3 fusion.53
  52.6 26.6 %all-gather.5.cloned.1.call-done = bf16[1024,2048]{1,0:T(8,128)(2,1)} async-done(((bf16[32,2048]{1,0:T(8,128)(2,1)}), bf16[1024,2048]{1,0:T(8,128)(2,1)}) %all-gather.5.cloned.1.call-update) | async-done | bytes 4194320 | tf_op jit(solution)/shard_map/all_gather | solution.py:459
  79.2 5.2 maximum_add_fusion.1
  85.6 1.6 slice.140
  88.2 1.9 copy.53
  90.1 2.3 copy.54
  96.1 1.5 maximum_bitcast_fusion
  97.5 3.7 all-to-all-start.1
  101.9 54.9 %all-to-all-done.1 = bf16[8,512,256]{1,2,0:T(8,128)(2,1)S(1)} async-done(((bf16[8,512,256]{1,2,0:T(8,128)(2,1)}), bf16[8,512,256]{1,2,0:T(8,128)(2,1)S(1)}, u32[]{:S(2)}, u32[]{:S(2)}) %all-to-all-start.1) | async-done | bytes 2097184 | tf_op jit(solution)/shard_map/all_to_all | solution.py:452
  156.8 2.4 copy.56
  159.2 1.7 fusion.75
  160.9 25.7 %forward_attention.1 = (bf16[4096,128]{1,0:T(8,128)(2,1)S(1)}, f32[16,8,512]{2,1,0:T(8,128)S(1)}) custom-call(s32[2,16]{1,0:T(2,128)S(1)} %pad_add_fusion.bound_ref, s32[1,4096]{1,0:T(1,128)S(1)} %bitcast.86, bf16[4096,128]{1,0:T(8,128)(2,1)S(1)} %get-tuple-element.94.query_ref, bf16[4096,128]{1,0:T(8,128)(2,1)S(1)} %get-tuple-element.93.keyval_ref), custom_call_target="tpu_custom_call" | custom-call | flops 8589934592 | bytes 4194304 | tf_op jit(solution)/shard_map/forward_attention/pallas_call | solution.py:293
  186.6 1.3 copy.57
  187.9 4.8 all-to-all-start.2
  192.7 1.6 convolution_convert_fusion.5
  194.3 33.9 %all-to-all-done.2 = bf16[8,512,128]{1,2,0:T(8,128)(2,1)} async-done(((bf16[8,512,128]{1,2,0:T(8,128)(2,1)}), bf16[8,512,128]{1,2,0:T(8,128)(2,1)}, u32[]{:S(2)}, u32[]{:S(2)}) %all-to-all-start.2) | async-done | bytes 1048608 | tf_op jit(solution)/shard_map/all_to_all | solution.py:452
  228.2 1.8 convolution_convert_fusion.3
  230.0 3.3 fusion.76
  235.3 4.9 fusion.30
  240.2 5.0 fusion.33
  245.2 16.2 %all-gather.11.cloned.1.call-done = bf16[4608,1024]{1,0:T(8,128)(2,1)} async-done(((bf16[144,1024]{1,0:T(8,128)(2,1)}), bf16[4608,1024]{1,0:T(8,128)(2,1)}) %all-gather.11.cloned.1.call-update) | async-done | bytes 9437200 | tf_op jit(solution)/shard_map/all_gather | solution.py:459
  261.3 10.2 %fusion.78 = f32[512,4608]{1,0:T(8,128)} fusion(bf16[512,1024]{1,0:T(8,128)(2,1)} %param.21, bf16[4608,1024]{1,0:T(8,128)(2,1)} %all-gather.11.cloned.1.call-done), kind=kOutput, calls=%fused_computation.160 | convolution fusion | flops 4831838208 | bytes 19922944 | tf_op jit(solution)/shard_map/dot_general | solution.py:43
  271.5 115.8 %all-gather.9.cloned.1.call-done = bf16[1024,9216]{1,0:T(8,128)(2,1)} async-done(((bf16[32,9216]{1,0:T(8,128)(2,1)}), bf16[1024,9216]{1,0:T(8,128)(2,1)}) %all-gather.9.cloned.1.call-update) | async-done | bytes 18874384 | tf_op jit(solution)/shard_map/all_gather | solution.py:459
  387.3 24.8 %maximum_add_fusion = f32[512,9216]{1,0:T(8,128)} fusion(f32[512,4608]{1,0:T(8,128)} %fusion.30, f32[512,4608]{1,0:T(8,128)} %fusion.33, bf16[512,1024]{1,0:T(8,128)(2,1)} %copy-done.12, bf16[1024,9216]{1,0:T(8,128)(2,1)} %all-gather.9.cloned.1.call-done), kind=kOutput, calls=%fused_computation | convolution fusion | flops 9673113600 | bytes 57671680 | tf_op jit(solution)/shard_map/dot_general | solution.py:35
  412.0 17.1 %fusion.25 = (f32[512,4608]{1,0:T(8,128)}, f32[512,4608]{1,0:T(8,128)}, bf16[512,4608]{1,0:T(8,128)(2,1)}) fusion(f32[512,9216]{1,0:T(8,128)} %maximum_add_fusion, f32[512,4608]{1,0:T(8,128)} %fusion.78, bf16[16,512]{1,0:T(8,128)(2,1)S(1)} %convolution_convert_fusion.5, bf16[16,4608]{1,0:T(8,128)(2,1)} %get-tuple-element.37), kind=kOutput, calls=%fused_computation.62 | convolution fusion | flops 110886912 | bytes 52068352 | tf_op jit(solution)/shard_map/dot_general | solution.py:35
  429.1 7.4 %add_convert_fusion = bf16[512,9216]{1,0:T(8,128)(2,1)S(1)} fusion(f32[512,4608]{1,0:T(8,128)} %get-tuple-element.83, f32[512,4608]{1,0:T(8,128)} %get-tuple-element.82), kind=kLoop, calls=%fused_computation.1 | loop fusion | flops 9437184 | bytes 28311552 | tf_op jit(solution)/shard_map/convert_element_type | solution.py:507
  436.6 1.3 fusion.22
  437.9 1.3 fusion.19
  439.2 2.1 copy-done.2
  442.3 1.3 convolution_convert_fusion.6
  443.6 1.5 fusion.81.refs_4_
  446.1 1.8 fusion.40
  447.9 18.9 %multiply_reduce_fusion.1 = (f32[512]{0:T(512)S(1)}, f32[512,1024]{1,0:T(8,128)}) fusion(f32[512,1024]{1,0:T(8,128)} %copy-done.5, f32[1024]{0:T(1024)S(1)} %copy-done.58, f32[512,1024]{1,0:T(8,128)} %fusion.40, bf16[512,9216]{1,0:T(8,128)(2,1)} %copy-done.2, bf16[1024,9216]{1,0:T(8,128)(2,1)} %all-gather.9.cloned.1.call-done), kind=kOutput, calls=%fused_computation.42 | convolution fusion | flops 9665773568 | bytes 34609152 | tf_op jit(solution)/shard_map/dot_general | solution.py:43
  466.8 3.0 fusion.11
  471.4 2.2 fusion.80.refs_0_
  476.6 4.2 all-to-all-start.3
  480.9 2.1 fusion.82.refs_5_
  483.0 3.1 fusion.7
  486.0 3.1 fusion.3
  489.9 2.6 pack_grads.3
  492.5 14.5 %all-to-all-done.3 = bf16[8,512,128]{2,1,0:T(8,128)(2,1)} async-done(((bf16[8,512,128]{2,1,0:T(8,128)(2,1)}), bf16[8,512,128]{2,1,0:T(8,128)(2,1)}, u32[]{:S(2)}, u32[]{:S(2)}) %all-to-all-start.3) | async-done | bytes 1048608 | tf_op jit(solution)/shard_map/all_to_all | solution.py:452
  507.0 3.3 all-to-all-start.6
  510.3 37.2 %backward_attention.1 = (bf16[4096,128]{1,0:T(8,128)(2,1)S(1)}, bf16[4096,128]{1,0:T(8,128)(2,1)S(1)}) custom-call(s32[2,16]{1,0:T(2,128)S(1)} %pad_add_fusion.bound_ref, s32[1,4096]{1,0:T(1,128)S(1)} %bitcast.87, bf16[4096,128]{1,0:T(8,128)(2,1)S(1)} %get-tuple-element.94.query_ref, bf16[4096,128]{1,0:T(8,128)(2,1)S(1)} %get-tuple-element.93.keyval_ref, ...), custom_call_target="tpu_custom_call" | custom-call | flops 21474836480 | bytes 8388608 | tf_op jit(solution)/shard_map/backward_attention/pallas_call | solution.py:384
  547.8 2.4 copy.59
  550.2 5.1 all-to-all-start.4
  555.3 9.1 %fusion.77 = f32[512,1024]{1,0:T(8,128)S(1)} fusion(bf16[512,4608]{1,0:T(8,128)(2,1)} %get-tuple-element.84, bf16[4608,1024]{1,0:T(8,128)(2,1)} %all-gather.11.cloned.1.call-done), kind=kOutput, calls=%fused_computation.159 | convolution fusion | flops 4831838208 | bytes 16252928 | tf_op jit(solution)/shard_map/dot_general | solution.py:35
  564.5 1.4 add_convert_fusion.3
  565.9 2.1 reduce_grads.3
  568.0 35.8 %all-to-all-done.4 = bf16[8,512,256]{1,2,0:T(8,128)(2,1)S(1)} async-done(((bf16[8,512,256]{1,2,0:T(8,128)(2,1)}), bf16[8,512,256]{1,2,0:T(8,128)(2,1)S(1)}, u32[]{:S(2)}, u32[]{:S(2)}) %all-to-all-start.4) | async-done | bytes 2097184 | tf_op jit(solution)/shard_map/all_to_all | solution.py:452
  614.5 2.4 fusion.79
  617.0 1.8 fusion.16
  619.5 2.0 pack_grads.2
  621.5 9.7 %all-to-all-start.5 = ((bf16[32,16,256]{2,1,0:T(8,128)(2,1)}), bf16[32,16,256]{2,1,0:T(8,128)(2,1)S(1)}, u32[]{:S(2)}, u32[]{:S(2)}) async-start(bf16[32,16,256]{2,1,0:T(8,128)(2,1)} %pack_grads.2), calls=%async_computation.5 | async-start | bytes 524288 | tf_op jit(solution)/shard_map/all_to_all | solution.py:538
  631.3 3.4 fusion.12
  634.7 6.8 %all-to-all-done.5.source = bf16[32,16,256]{2,1,0:T(8,128)(2,1)S(1)} async-done(((bf16[32,16,256]{2,1,0:T(8,128)(2,1)}), bf16[32,16,256]{2,1,0:T(8,128)(2,1)S(1)}, u32[]{:S(2)}, u32[]{:S(2)}) %all-to-all-start.5) | async-done | bytes 262176 | tf_op jit(solution)/shard_map/all_to_all | solution.py:538
  642.1 1.8 reduce_grads.2
  644.0 1.7 copy.60
  (199 shorter events, 32.9 us)
Async XLA Ops:
  7.2 14.5 %copy-start.9 = (bf16[512,1024]{1,0:T(8,128)(2,1)S(1)}, bf16[512,1024]{1,0:T(8,128)(2,1)}, u32[]{:S(2)}) copy-start(bf16[512,1024]{1,0:T(8,128)(2,1)} %param.20) | copy-start | bytes 3145732
  7.2 72.0 %all-gather.5.cloned.1.call-start = ((), (), s32[]{:S(2)}) async-start(), calls=%async_computation.7 | async-start | bytes 4325376 | tf_op jit(solution)/shard_map/all_gather | solution.py:459
  7.9 222.1 %all-gather.7.cloned.1.call-start = ((), (), s32[]{:S(2)}) async-start(), calls=%async_computation.8 | async-start | bytes 2162688 | tf_op jit(solution)/shard_map/all_gather | solution.py:459
  8.7 252.7 %all-gather.11.cloned.1.call-start = ((), (), s32[]{:S(2)}) async-start(), calls=%async_computation.10 | async-start | bytes 9732096 | tf_op jit(solution)/shard_map/all_gather | solution.py:459
  9.4 377.9 %all-gather.9.cloned.1.call-start = ((), (), s32[]{:S(2)}) async-start(), calls=%async_computation.9 | async-start | bytes 19464192 | tf_op jit(solution)/shard_map/all_gather | solution.py:459
  14.3 33.1 %copy-start.59 = (f32[1024]{0:T(1024)S(1)}, f32[1024]{0:T(1024)}, u32[]{:S(2)}) copy-start(f32[1024]{0:T(1024)} %param.24) | copy-start | bytes 12292
  14.3 29.7 %all-to-all-start = ((bf16[32,16,768]{2,1,0:T(8,128)(2,1)}), bf16[32,16,768]{2,1,0:T(8,128)(2,1)S(1)}, u32[]{:S(2)}, u32[]{:S(2)}) async-start(bf16[32,16,768]{2,1,0:T(8,128)(2,1)} %pack_adapters.1), calls=%async_computation | async-start | bytes 1572864 | tf_op jit(solution)/shard_map/all_to_all | solution.py:462
  22.6 56.6 %copy-start.52 = (f32[512]{0:T(512)}, f32[512]{0:T(512)S(1)}, u32[]{:S(2)}) copy-start(f32[512]{0:T(512)S(1)} %fusion.61) | copy-start | bytes 6148
  22.9 72.6 %copy-start.17 = (f32[512,32]{0,1:T(8,128)}, f32[512,32]{0,1:T(8,128)S(1)}, u32[]{:S(2)}) copy-start(f32[512,32]{0,1:T(8,128)S(1)} %get-tuple-element.97) | copy-start | bytes 196612
  22.9 72.6 %copy-start.19 = (f32[512,32]{0,1:T(8,128)}, f32[512,32]{0,1:T(8,128)S(1)}, u32[]{:S(2)}) copy-start(f32[512,32]{0,1:T(8,128)S(1)} %get-tuple-element.98) | copy-start | bytes 196612
  44.0 0.9 copy-start.14
  47.4 3.5 copy-start.28
  48.8 3.3 copy-start.31
  90.1 3.4 copy-start
  90.1 3.4 copy-start.54
  92.5 2.6 copy-start.7
  95.0 2.5 copy-start.37
  95.0 1.0 copy-start.16
  95.2 2.3 copy-start.35
  97.5 3.8 copy-start.46
  97.5 59.3 %all-to-all-start.1 = ((bf16[8,512,256]{1,2,0:T(8,128)(2,1)}), bf16[8,512,256]{1,2,0:T(8,128)(2,1)S(1)}, u32[]{:S(2)}, u32[]{:S(2)}) async-start(bf16[8,512,256]{1,2,0:T(8,128)(2,1)} %maximum_bitcast_fusion), calls=%async_computation.1 | async-start | bytes 4194304 | tf_op jit(solution)/shard_map/all_to_all | solution.py:452
  186.5 6.2 copy-start.42
  187.9 40.3 %copy-start.44 = (bf16[16,1024]{1,0:T(8,128)(2,1)S(1)}, bf16[16,1024]{1,0:T(8,128)(2,1)}, u32[]{:S(2)}) copy-start(bf16[16,1024]{1,0:T(8,128)(2,1)} %get-tuple-element.33) | copy-start | bytes 98308
  187.9 40.3 %all-to-all-start.2 = ((bf16[8,512,128]{1,2,0:T(8,128)(2,1)}), bf16[8,512,128]{1,2,0:T(8,128)(2,1)}, u32[]{:S(2)}, u32[]{:S(2)}) async-start(bf16[8,512,128]{1,2,0:T(8,128)(2,1)} %copy.57), calls=%async_computation.2 | async-start | bytes 2097152 | tf_op jit(solution)/shard_map/all_to_all | solution.py:452
  194.3 217.7 %copy-start.48 = (bf16[16,512]{1,0:T(8,128)(2,1)}, bf16[16,512]{1,0:T(8,128)(2,1)S(1)}, u32[]{:S(2)}) copy-start(bf16[16,512]{1,0:T(8,128)(2,1)S(1)} %convolution_convert_fusion.5) | copy-start | bytes 49156
  230.0 3.3 copy-start.33
  230.0 3.3 copy-start.40
  230.0 3.3 copy-start.10
  233.9 1.3 copy-start.5
  233.9 0.9 copy-start.30
  234.0 1.3 copy-start.22
  234.3 6.0 copy-start.12
  429.1 7.4 %copy-start.23 = (bf16[16,9216]{1,0:T(8,128)(2,1)S(1)}, bf16[16,9216]{1,0:T(8,128)(2,1)}, u32[]{:S(2)}) copy-start(bf16[16,9216]{1,0:T(8,128)(2,1)} %get-tuple-element.36) | copy-start | bytes 884740
  436.6 4.8 copy-start.2
  436.6 5.3 slice-start
  437.9 4.4 slice-start.1
  437.9 4.4 copy-start.39
  442.3 1.3 copy-start.49
  443.6 1.5 copy-start.13
  466.8 3.0 copy-start.41
  469.8 3.9 copy-start.3
  470.6 3.1 copy-start.15
  473.7 1.3 copy-start.45
  476.6 30.4 %all-to-all-start.3 = ((bf16[8,512,128]{2,1,0:T(8,128)(2,1)}), bf16[8,512,128]{2,1,0:T(8,128)(2,1)}, u32[]{:S(2)}, u32[]{:S(2)}) async-start(bf16[8,512,128]{2,1,0:T(8,128)(2,1)} %bitcast.99), calls=%async_computation.3 | async-start | bytes 2097152 | tf_op jit(solution)/shard_map/all_to_all | solution.py:452
  507.0 43.2 %all-to-all-start.6 = ((bf16[32,16,640]{2,1,0:T(8,128)(2,1)}), bf16[32,16,640]{2,1,0:T(8,128)(2,1)}, u32[]{:S(2)}, u32[]{:S(2)}) async-start(bf16[32,16,640]{2,1,0:T(8,128)(2,1)} %pack_grads.3), calls=%async_computation.6 | async-start | bytes 1310720 | tf_op jit(solution)/shard_map/all_to_all | solution.py:521
  550.2 53.7 %all-to-all-start.4 = ((bf16[8,512,256]{1,2,0:T(8,128)(2,1)}), bf16[8,512,256]{1,2,0:T(8,128)(2,1)S(1)}, u32[]{:S(2)}, u32[]{:S(2)}) async-start(bf16[8,512,256]{1,2,0:T(8,128)(2,1)} %copy.59), calls=%async_computation.4 | async-start | bytes 4194304 | tf_op jit(solution)/shard_map/all_to_all | solution.py:452
  555.3 9.2 %copy-start.6 = (f32[512,1024]{1,0:T(8,128)S(1)}, f32[512,1024]{1,0:T(8,128)}, u32[]{:S(2)}) copy-start(f32[512,1024]{1,0:T(8,128)} %copy-done.5) | copy-start | bytes 6291460
  555.3 9.2 %copy-start.43 = (bf16[16,1024]{1,0:T(8,128)(2,1)S(1)}, bf16[16,1024]{1,0:T(8,128)(2,1)}, u32[]{:S(2)}) copy-start(bf16[16,1024]{1,0:T(8,128)(2,1)} %get-tuple-element.38) | copy-start | bytes 98308
  604.4 0.9 copy-start.20
  605.6 1.2 copy-start.8
  605.6 1.2 copy-start.57
  606.0 1.2 copy-start.38
  606.0 1.3 copy-start.36
  607.2 1.6 copy-start.1
  607.2 1.6 copy-start.55
  610.5 1.0 copy-start.32
  611.5 1.4 copy-start.11
  611.5 1.4 copy-start.53
  611.5 1.3 copy-start.60
  612.2 2.4 copy-start.61
  614.5 2.4 copy-start.47
  617.0 14.2 %copy-start.51 = (f32[512]{0:T(512)S(1)}, f32[512]{0:T(512)}, u32[]{:S(2)}) copy-start(f32[512]{0:T(512)} %copy-done.50) | copy-start | bytes 6148
  617.0 14.3 %copy-start.4 = (f32[512,1024]{1,0:T(8,128)S(1)}, f32[512,1024]{1,0:T(8,128)}, u32[]{:S(2)}) copy-start(f32[512,1024]{1,0:T(8,128)} %copy-done.3) | copy-start | bytes 6291460
  621.5 19.9 %all-to-all-start.5 = ((bf16[32,16,256]{2,1,0:T(8,128)(2,1)}), bf16[32,16,256]{2,1,0:T(8,128)(2,1)S(1)}, u32[]{:S(2)}, u32[]{:S(2)}) async-start(bf16[32,16,256]{2,1,0:T(8,128)(2,1)} %pack_grads.2), calls=%async_computation.5 | async-start | bytes 524288 | tf_op jit(solution)/shard_map/all_to_all | solution.py:538
  (11 other events, 7.9 us)
Sparse Core Ops, SparseCore 0:
  11.0 68.1 all-gather.4
  82.1 79.0 all-gather.6
  164.0 97.2 all-gather.10
  264.0 123.2 all-gather.8

commit v2 on v1

--- a/solution.py
+++ b/solution.py
@@ -43,73 +43,271 @@
     return lax.dot_general(left_side, right_side, (((1,), (1,)), ((), ())), preferred_element_type=F32)
 
 
-def rms_norm(values, gain_row):
-    return values * lax.rsqrt(jnp.mean(values * values, axis=-1, keepdims=True) + epsilon) * gain_row
-
-
 def rope_tables(positions):
     middle = HEAD_DIM // 2
     frequency = jnp.power(rope_base, -(2.0 / HEAD_DIM) * jnp.arange(middle, dtype=F32))
     angles = positions.astype(F32)[:, None] * frequency[None, :]
-    return (jnp.cos(angles)[:, None, :], jnp.sin(angles)[:, None, :])
-
-
-def rotate(values, cosine, sine_part):
-    middle = values.shape[-1] // 2
-    leading = values[..., :middle]
-    trailing = values[..., middle:]
-    return jnp.concatenate(
-        [leading * cosine - trailing * sine_part, trailing * cosine + leading * sine_part], axis=-1
-    )
-
-
-def prepare_heads(projected, positions, query_gain, key_gain):
-    length = projected.shape[0]
-    cosine, sine_part = rope_tables(positions)
-    query_rows = projected[:, :QW].reshape(length, HEADS, HEAD_DIM)
-    key_rows = projected[:, QW : QW + KW].reshape(length, KV_HEADS, HEAD_DIM)
-    value_rows = projected[:, QW + KW :].reshape(length, KV_HEADS, HEAD_DIM)
-    query_rows = rotate(rms_norm(query_rows, query_gain), cosine, sine_part)
-    key_rows = rotate(rms_norm(key_rows, key_gain), cosine, sine_part)
-    grouped = query_rows.reshape(length, KV_HEADS, PAIR)
-    return (grouped, jnp.concatenate([key_rows, value_rows], axis=-1))
-
-
-def rank_apply(reduced, up_rows, bounds):
-    return jnp.concatenate(
-        [
-            matmul(
-                reduced[:, RANK * member : RANK * (member + 1)],
-                up_rows[:, bounds[member] : bounds[member + 1]],
+    cosine, sine = jnp.cos(angles), jnp.sin(angles)
+    return jnp.concatenate([cosine] * 4, axis=1), jnp.concatenate([-sine, sine] * 2, axis=1)
+
+
+ANY_SPEC = pl.BlockSpec(memory_space=pl.ANY)
+
+
+class Pieces:
+    def __init__(self, blocks, rows):
+        self.keys = [key for key, _ in blocks]
+        self.blocks = [block for _, block in blocks]
+        self.rows = rows
+
+    def offsets(self):
+        if self.keys[0] is None:
+            return [(0, 0, self.rows)]
+        depth = lax.axis_size("head")
+        ctx, head = lax.axis_index("ctx"), lax.axis_index("head")
+        found = []
+        for flip, steps in self.keys:
+            flips = [flip] if len(steps) == 1 else [flip ^ other for other in (0, 2, 4, 6)]
+            size = self.blocks[0].shape[0] // (len(steps) * len(flips))
+            for place, (flip, step) in enumerate([(flip, step) for flip in flips for step in steps]):
+                device = jnp.bitwise_xor(ctx, flip) * depth + lax.rem(head - step + depth, depth)
+                found.append((place * size, pl.multiple_of(device * size, 8), size))
+        return found
+
+    def copies(self, refs):
+        found, offsets = [], self.offsets()
+        share = len(offsets) // len(refs)
+        for place, (source, target, size) in enumerate(offsets):
+            found.append((refs[place // share], source, target, size))
+        return found
+
+
+def by_axes():
+    return lax.axis_size("ctx") == 8 and lax.axis_size("head") == 4
+
+
+def hop(value, flip, step):
+    depth = lax.axis_size("head")
+    pairs = [
+        (ctx * depth + head, (ctx ^ flip) * depth + (head + step) % depth)
+        for ctx in range(lax.axis_size("ctx"))
+        for head in range(depth)
+    ]
+    return lax.ppermute(value, AXES, pairs)
+
+
+def stack_shard(gate_up_weight, out_weight, down_weight):
+    part, down_part = out_weight.shape[0], down_weight.shape[0]
+    slices = 2 * FF // D
+
+    def kernel(wide_ref, out_ref, down_ref, stacked_ref):
+        for piece in range(slices):
+            stacked_ref[piece * part : (piece + 1) * part, :] = wide_ref[:, piece * D : (piece + 1) * D]
+        stacked_ref[slices * part : (slices + 1) * part, :] = out_ref[...]
+        stacked_ref[(slices + 1) * part :, :] = down_ref[...]
+
+    return pl.pallas_call(
+        kernel,
+        in_specs=[VMEM_SPEC] * 3,
+        out_specs=VMEM_SPEC,
+        out_shape=jax.ShapeDtypeStruct(((slices + 1) * part + down_part, D), BF16),
+        name="stack_shard",
+    )(gate_up_weight, out_weight, down_weight)
+
+
+def whole_gather(value):
+    full = lax.all_gather(value, AXES, axis=0, tiled=True)
+    return Pieces([(None, full)], full.shape[0])
+
+
+def start_loads(pieces, refs, target, sem):
+    for ref, source, where, size in pieces.copies(refs):
+        pltpu.make_async_copy(ref.at[pl.ds(source, size), :], target.at[pl.ds(where, size), :], sem).start()
+
+
+def finish_loads(target, sem, columns=None):
+    region = target if columns is None else target.at[:, columns]
+    pltpu.make_async_copy(region, region, sem).wait()
+
+
+def head_means(values, ones):
+    first = values.astype(BF16)
+    second = (values - first.astype(F32)).astype(BF16)
+    return (matmul(first, ones) + matmul(second, ones)) * (1.0 / HEAD_DIM)
+
+
+def head_ones():
+    row = lax.broadcasted_iota(jnp.int32, (PAIR, PAIR), 0) // HEAD_DIM
+    col = lax.broadcasted_iota(jnp.int32, (PAIR, PAIR), 1) // HEAD_DIM
+    return jnp.where(row == col, 1.0, 0.0).astype(BF16)
+
+
+def swapped_halves(values):
+    lanes = lax.broadcasted_iota(jnp.int32, values.shape, 1)
+    half = HEAD_DIM // 2
+    return jnp.where(lanes % HEAD_DIM < half, pltpu.roll(values, PAIR - half, 1), pltpu.roll(values, half, 1))
+
+
+def row_scale(values):
+    return lax.rsqrt(jnp.mean(values * values, axis=1, keepdims=True) + epsilon)
+
+
+def project_heads(hidden, gain, head_gain, tables, pieces, down, up):
+    rows = hidden.shape[0]
+    count = len(pieces.blocks)
+    width = QW + 2 * KW
+
+    def kernel(*refs):
+        hidden_ref, gain_ref, head_gain_ref, cos_ref, sin_ref, down_ref, up_ref = refs[:7]
+        blocks = refs[7 : 7 + count]
+        sent_ref, low_ref, kept_ref, weight, sem = refs[7 + count :]
+        start_loads(pieces, blocks, weight, sem)
+        inputs = hidden_ref[...].astype(F32)
+        normed = (inputs * row_scale(inputs) * gain_ref[...]).astype(BF16)
+        low = contract_cols(normed, down_ref[...]).astype(BF16)
+        low_ref[...] = low
+        ones = head_ones()
+        cos, sin = cos_ref[...], sin_ref[...]
+        lanes = lax.broadcasted_iota(jnp.int32, (rows, PAIR), 1)
+        finish_loads(weight, sem)
+
+        def columns(start, size, group):
+            return matmul(normed, weight[:, start : start + size]) + matmul(
+                low[:, RANK * group : RANK * (group + 1)], up_ref[:, start : start + size]
             )
-            for member in range(len(bounds) - 1)
+
+        def turned(values, gains):
+            unit = values * lax.rsqrt(head_means(values * values, ones) + epsilon) * gains
+            return unit * cos + swapped_halves(unit) * sin
+
+        step = 2 * PAIR
+        for start in range(0, QW, step):
+            both = columns(start, step, 0)
+            kept_ref[:, start : start + step] = both.astype(BF16)
+            for side in range(2):
+                query = turned(both[:, side * PAIR : (side + 1) * PAIR], head_gain_ref[0:1, :]) * QSCALE
+                sent_ref[start // PAIR + side, :, :PAIR] = query.astype(BF16)
+        for start in range(0, KW, step):
+            both = columns(QW + start, step, 1)
+            values = columns(QW + KW + start, step, 2)
+            kept_ref[:, QW + start : QW + start + step] = both.astype(BF16)
+            for side in range(2):
+                where = slice(side * PAIR, (side + 1) * PAIR)
+                key = turned(both[:, where], head_gain_ref[1:2, :])
+                value = values[:, where]
+                group = (start + side * PAIR) // HEAD_DIM
+                sent_ref[group, :, PAIR:] = jnp.where(
+                    lanes < HEAD_DIM, key, pltpu.roll(value, HEAD_DIM, 1)
+                ).astype(BF16)
+                sent_ref[group + 1, :, PAIR:] = jnp.where(
+                    lanes < HEAD_DIM, pltpu.roll(key, HEAD_DIM, 1), value
+                ).astype(BF16)
+
+    return pl.pallas_call(
+        kernel,
+        in_specs=[VMEM_SPEC] * 7 + [ANY_SPEC] * count,
+        out_specs=[VMEM_SPEC] * 3,
+        out_shape=[
+            jax.ShapeDtypeStruct((KV_HEADS, rows, 2 * PAIR), BF16),
+            jax.ShapeDtypeStruct((rows, 3 * RANK), BF16),
+            jax.ShapeDtypeStruct((rows, QW + KW), BF16),
         ],
-        axis=1,
-    )
-
-
-def rank_back(grad_low, reduced, up_rows, bounds):
-    up_grad = jnp.concatenate(
-        [
-            contract_rows(
-                reduced[:, RANK * member : RANK * (member + 1)],
-                grad_low[:, bounds[member] : bounds[member + 1]],
-            )
-            for member in range(len(bounds) - 1)
+        scratch_shapes=[pltpu.VMEM((D, width), BF16), pltpu.SemaphoreType.DMA],
+        compiler_params=pltpu.CompilerParams(vmem_limit_bytes=40 << 20),
+        cost_estimate=pl.CostEstimate(flops=2 * rows * D * width, bytes_accessed=10 << 20, transcendentals=0),
+        name="project_heads",
+    )(hidden, gain[None, :], head_gain, *tables, down, up, *pieces.blocks)
+
+
+def project_back(back, kept, head_gain, tables, hidden, gain, low, up):
+    rows = hidden.shape[0]
+    width = QW + 2 * KW
+
+    def kernel(
+        back_ref, kept_ref, head_gain_ref, cos_ref, sin_ref, hidden_ref, gain_ref, low_ref, up_ref,
+        grad_ref, low_grad_ref, up_grad_ref, down_grad_ref,
+    ):
+        ones = head_ones()
+        cos, sin = cos_ref[...], sin_ref[...]
+        lanes = lax.broadcasted_iota(jnp.int32, (rows, PAIR), 1)
+
+        def through(grads, values, gains):
+            slope = (grads * cos - swapped_halves(grads) * sin) * gains
+            scale = lax.rsqrt(head_means(values * values, ones) + epsilon)
+            unit = values * scale
+            return scale * (slope - unit * head_means(slope * unit, ones))
+
+        for group in range(KV_HEADS):
+            where = slice(group * PAIR, (group + 1) * PAIR)
+            grads = back_ref[group, :, :PAIR].astype(F32)
+            grad_ref[:, where] = through(grads, kept_ref[:, where].astype(F32), head_gain_ref[0:1, :]).astype(BF16)
+        for group in range(0, KV_HEADS, 2):
+            even = back_ref[group, :, PAIR:].astype(F32)
+            odd = back_ref[group + 1, :, PAIR:].astype(F32)
+            keys = jnp.where(lanes < HEAD_DIM, even, pltpu.roll(odd, HEAD_DIM, 1))
+            values = jnp.where(lanes < HEAD_DIM, pltpu.roll(even, HEAD_DIM, 1), odd)
+            start = QW + group * HEAD_DIM
+            where = slice(start, start + PAIR)
+            grad_ref[:, where] = through(keys, kept_ref[:, where].astype(F32), head_gain_ref[1:2, :]).astype(BF16)
+            grad_ref[:, start + KW : start + KW + PAIR] = values.astype(BF16)
+        low = low_ref[...]
+        turned = low.astype(F32).T.astype(BF16)
+        edges = (0, QW, QW + KW, width)
+        parts = []
+        for group in range(3):
+            where = slice(edges[group], edges[group + 1])
+            grads = grad_ref[:, where]
+            up_grad_ref[:, where] = matmul(turned[RANK * group : RANK * (group + 1), :], grads)
+            parts.append(contract_cols(grads, up_ref[:, where]))
+        low_grad = jnp.concatenate(parts, axis=1)
+        low_grad_ref[...] = low_grad.astype(BF16)
+        inputs = hidden_ref[...].astype(F32)
+        normed = (inputs * row_scale(inputs) * gain_ref[...]).astype(BF16)
+        down_grad_ref[...] = matmul(low_grad.T.astype(BF16), normed)
+
+    return pl.pallas_call(
+        kernel,
+        in_specs=[VMEM_SPEC] * 9,
+        out_specs=[VMEM_SPEC] * 4,
+        out_shape=[
+            jax.ShapeDtypeStruct((rows, width), BF16),
+            jax.ShapeDtypeStruct((rows, 3 * RANK), BF16),
+            jax.ShapeDtypeStruct((RANK, width), F32),
+            jax.ShapeDtypeStruct((3 * RANK, D), F32),
         ],
-        axis=1,
-    )
-    reduced_grad = jnp.concatenate(
-        [
-            contract_cols(
-                grad_low[:, bounds[member] : bounds[member + 1]],
-                up_rows[:, bounds[member] : bounds[member + 1]],
-            )
-            for member in range(len(bounds) - 1)
-        ],
-        axis=1,
-    )
-    return (up_grad, reduced_grad)
+        compiler_params=pltpu.CompilerParams(vmem_limit_bytes=40 << 20),
+        name="project_back",
+    )(back, kept, head_gain, *tables, hidden, gain[None, :], low, up)
+
+
+def input_back(grad, low_grad, pieces, down, hidden, gain, middle_grad):
+    rows = hidden.shape[0]
+    count = len(pieces.blocks)
+
+    def kernel(*refs):
+        grad_ref, low_ref, down_ref, hidden_ref, gain_ref, middle_ref = refs[:6]
+        blocks = refs[6 : 6 + count]
+        out_ref, weight, sem = refs[6 + count :]
+        start_loads(pieces, blocks, weight, sem)
+        inputs = hidden_ref[...].astype(F32)
+        scale = row_scale(inputs)
+        slope = matmul(low_ref[...], down_ref[...])
+        finish_loads(weight, sem)
+        slope = (slope + contract_cols(grad_ref[...], weight[...])) * gain_ref[...]
+        unit = inputs * scale
+        inner = jnp.mean(slope * unit, axis=1, keepdims=True)
+        out_ref[...] = middle_ref[...] + scale * (slope - unit * inner)
+
+    return pl.pallas_call(
+        kernel,
+        in_specs=[VMEM_SPEC] * 6 + [ANY_SPEC] * count,
+        out_specs=VMEM_SPEC,
+        out_shape=jax.ShapeDtypeStruct((rows, D), F32),
+        scratch_shapes=[pltpu.VMEM((D, QW + 2 * KW), BF16), pltpu.SemaphoreType.DMA],
+        compiler_params=pltpu.CompilerParams(vmem_limit_bytes=40 << 20),
+        cost_estimate=pl.CostEstimate(flops=2 * rows * D * 2048, bytes_accessed=10 << 20, transcendentals=0),
+        name="input_back",
+    )(grad, low_grad, down, hidden, gain[None, :], middle_grad, *pieces.blocks)
 
 
 VMEM_SPEC = pl.BlockSpec(memory_space=pltpu.VMEM)
@@ -431,6 +629,208 @@
     return bounds, start[None, :]
 
 
+TILE = 512
+
+
+def silu_parts(gate):
+    share = 1.0 / (1.0 + jnp.exp(-gate))
+    return share, gate * share
+
+
+def feed_forward(mixed, hidden, cotangent, gain, weights, chosen):
+    members, rows, _ = mixed.shape
+    tiles = FF // TILE
+    packed = isinstance(weights, Pieces)
+    arrays = weights.blocks if packed else weights
+    count = len(arrays)
+    slices = 2 * FF // D
+
+    def kernel(*refs):
+        (
+            mixed_ref, hidden_ref, cot_ref, gain_ref,
+            out_down_ref, out_up_ref, mlp_down_ref, mlp_up_ref, ffd_down_ref, ffd_up_ref,
+        ) = refs[:10]
+        weight_refs = refs[10 : 10 + count]
+        (
+            output_ref, middle_grad_ref, mixed_grad_ref,
+            out_down_grad, out_up_grad, mlp_down_grad, mlp_up_grad, ffd_down_grad, ffd_up_grad,
+            wide_scr, down_scr, mix_scr, middle_scr, normed_scr, branch_scr, slope_scr,
+            low_scr, low_turned, back_scr, back_turned, out_low_scr, down_sum, gate_sum, up_sum, sems,
+        ) = refs[10 + count :]
+        out_columns = slice(2 * FF, 2 * FF + D)
+
+        def column_piece(piece):
+            return slice(piece * D, (piece + 1) * D)
+
+        if packed:
+            blocks = weights.copies(weight_refs)
+            devices = len(blocks)
+            part, down_part = D // devices, FF // devices
+
+            def start_piece(piece):
+                for ref, source, where, size in blocks:
+                    row = pl.multiple_of(where // size * part, 8)
+                    pltpu.make_async_copy(
+                        ref.at[pl.ds(source + piece * part, part), :],
+                        wide_scr.at[pl.ds(row, part), column_piece(piece)],
+                        sems.at[piece],
+                    ).start()
+
+            def start_down():
+                for ref, source, where, size in blocks:
+                    row = pl.multiple_of(where // size * down_part, 8)
+                    pltpu.make_async_copy(
+                        ref.at[pl.ds(source + (slices + 1) * part, down_part), :],
+                        down_scr.at[pl.ds(row, down_part), :],
+                        sems.at[slices + 1],
+                    ).start()
+        else:
+
+            def start_piece(piece):
+                columns = column_piece(piece)
+                pltpu.make_async_copy(
+                    weight_refs[0].at[:, columns], wide_scr.at[:, columns], sems.at[piece]
+                ).start()
+
+            def start_down():
+                pltpu.make_async_copy(weight_refs[1], down_scr, sems.at[slices + 1]).start()
+
+        def finish_piece(piece):
+            region = wide_scr.at[:, column_piece(piece)]
+            pltpu.make_async_copy(region, region, sems.at[piece]).wait()
+
+        per_piece = D // TILE
+        first_use = {}
+        for piece in range(slices):
+            uses = [c // TILE % tiles for c in range(piece * D, (piece + 1) * D, TILE)]
+            first_use.setdefault(min(uses), []).append(piece)
+        start_piece(slices)
+        for piece in first_use[0]:
+            start_piece(piece)
+        start_down()
+
+        cot = cot_ref[...]
+        for member in range(members):
+            mix_scr[:, member * PAIR : (member + 1) * PAIR] = mixed_ref[member]
+        out_low = contract_cols(mix_scr[...], out_down_ref[...]).astype(BF16)
+        out_low_scr[...] = out_low
+        back = contract_cols(cot, ffd_up_ref[...])
+        back_scr[...] = back.astype(BF16)
+        back_turned[...] = back.T.astype(BF16)
+        branch_scr[...] = jnp.zeros_like(branch_scr)
+        slope_scr[...] = jnp.zeros_like(slope_scr)
+        down_sum[...] = jnp.zeros_like(down_sum)
+        gate_sum[...] = jnp.zeros_like(gate_sum)
+        up_sum[...] = jnp.zeros_like(up_sum)
+        finish_piece(slices)
+        middle = (
+            hidden_ref[...].astype(F32)
+            + matmul(mix_scr[...], wide_scr[:, out_columns])
+            + matmul(out_low, out_up_ref[...])
+        )
+        middle_scr[...] = middle
+        normed = (middle * row_scale(middle) * gain_ref[...]).astype(BF16)
+        normed_scr[...] = normed
+        low = contract_cols(normed, mlp_down_ref[...])
+        low_scr[...] = low.astype(BF16)
+        low_turned[...] = low.T.astype(BF16)
+        pltpu.make_async_copy(down_scr, down_scr, sems.at[slices + 1]).wait()
+
+        def tile(index, carry):
+            base = pl.multiple_of(index * TILE, TILE)
+            gate_at, up_at = pl.ds(base, TILE), pl.ds(base + FF, TILE)
+            for use, group in sorted(first_use.items()):
+
+                @pl.when(index == use)
+                def _(group=group):
+                    for piece in group:
+                        finish_piece(piece)
+
+                if use > 0:
+
+                    @pl.when(index == max(use - per_piece, 0))
+                    def _(group=group):
+                        for piece in group:
+                            start_piece(piece)
+
+            normed = normed_scr[...]
+            low = low_scr[...]
+            gate = matmul(normed, wide_scr[:, gate_at]) + matmul(low[:, :RANK], mlp_up_ref[:, gate_at])
+            up = matmul(normed, wide_scr[:, up_at]) + matmul(low[:, RANK:], mlp_up_ref[:, up_at])
+            share, active = silu_parts(gate)
+            units = (active * up).astype(BF16)
+            down = down_scr[gate_at, :]
+            branch_scr[...] += matmul(units, down)
+            down_sum[...] += contract_cols(units, ffd_down_ref[:, gate_at])
+            ffd_down_grad[:, gate_at] = matmul(back_turned[...], units)
+            units_grad = contract_cols(cot_ref[...], down) + matmul(back_scr[...], ffd_down_ref[:, gate_at])
+            gate_grad = (units_grad * up * (share * (1.0 + gate * (1.0 - share)))).astype(BF16)
+            up_grad = (units_grad * active).astype(BF16)
+            slope_scr[...] += contract_cols(gate_grad, wide_scr[:, gate_at]) + contract_cols(
+                up_grad, wide_scr[:, up_at]
+            )
+            gate_sum[...] += contract_cols(gate_grad, mlp_up_ref[:, gate_at])
+            up_sum[...] += contract_cols(up_grad, mlp_up_ref[:, up_at])
+            mlp_up_grad[:, gate_at] = matmul(low_turned[:RANK, :], gate_grad)
+            mlp_up_grad[:, up_at] = matmul(low_turned[RANK:, :], up_grad)
+            return carry
+
+        lax.fori_loop(0, tiles, tile, 0)
+
+        middle = middle_scr[...]
+        cot = cot_ref[...]
+        down_low = down_sum[...].astype(BF16)
+        output_ref[...] = (middle + branch_scr[...] + matmul(down_low, ffd_up_ref[...])).astype(BF16)
+        ffd_up_grad[...] = contract_rows(down_low, cot)
+        low_grad = jnp.concatenate([gate_sum[...], up_sum[...]], axis=1).astype(BF16)
+        mlp_down_grad[...] = contract_rows(low_grad, normed_scr[...])
+        slope = gain_ref[...] * (slope_scr[...] + matmul(low_grad, mlp_down_ref[...]))
+        scale = row_scale(middle)
+        inner = jnp.mean(slope * middle, axis=1, keepdims=True)
+        middle_grad = cot.astype(F32) + scale * slope - middle * (scale * scale * scale * inner)
+        middle_grad_ref[...] = middle_grad
+        branch_grad = middle_grad.astype(BF16)
+        out_up_grad[...] = contract_rows(out_low_scr[...], branch_grad)
+        out_low_grad = contract_cols(branch_grad, out_up_ref[...]).astype(BF16)
+        out_down_grad[...] = contract_rows(out_low_grad, mix_scr[...])
+        mixed_grad = contract_cols(branch_grad, wide_scr[:, out_columns]) + matmul(out_low_grad, out_down_ref[...])
+        for member in range(members):
+            mixed_grad_ref[member] = mixed_grad[:, member * PAIR : (member + 1) * PAIR].astype(BF16)
+
+    results = pl.pallas_call(
+        kernel,
+        in_specs=[VMEM_SPEC] * 10 + [ANY_SPEC] * count,
+        out_specs=[VMEM_SPEC] * 9,
+        out_shape=[
+            jax.ShapeDtypeStruct((rows, D), BF16),
+            jax.ShapeDtypeStruct((rows, D), F32),
+            jax.ShapeDtypeStruct((members, rows, PAIR), BF16),
+            jax.ShapeDtypeStruct((RANK, QW), F32),
+            jax.ShapeDtypeStruct((RANK, D), F32),
+            jax.ShapeDtypeStruct((2 * RANK, D), F32),
+            jax.ShapeDtypeStruct((RANK, 2 * FF), F32),
+            jax.ShapeDtypeStruct((RANK, FF), F32),
+            jax.ShapeDtypeStruct((RANK, D), F32),
+        ],
+        scratch_shapes=[
+            pltpu.VMEM((D, 2 * FF + D), BF16), pltpu.VMEM((FF, D), BF16),
+            pltpu.VMEM((rows, QW), BF16), pltpu.VMEM((rows, D), F32), pltpu.VMEM((rows, D), BF16),
+            pltpu.VMEM((rows, D), F32), pltpu.VMEM((rows, D), F32),
+            pltpu.VMEM((rows, 2 * RANK), BF16), pltpu.VMEM((2 * RANK, rows), BF16),
+            pltpu.VMEM((rows, RANK), BF16), pltpu.VMEM((RANK, rows), BF16), pltpu.VMEM((rows, RANK), BF16),
+            pltpu.VMEM((rows, RANK), F32), pltpu.VMEM((rows, RANK), F32), pltpu.VMEM((rows, RANK), F32),
+            pltpu.SemaphoreType.DMA((2 + slices,)),
+        ],
+        compiler_params=pltpu.CompilerParams(vmem_limit_bytes=60 << 20),
+        cost_estimate=pl.CostEstimate(
+            flops=rows * (12 * D * FF + 4 * D * QW), bytes_accessed=6 * D * FF + 16 * rows * D,
+            transcendentals=rows * FF,
+        ),
+        name="feed_forward",
+    )(mixed, hidden, cotangent, gain[None, :], *chosen, *arrays)
+    return results[0], results[1], results[2], list(results[3:])
+
+
 def local(
     hidden, cotangent, segment_ids, adapter_ids, attn_gain, query_gain, key_gain, ffn_gain,
     qkv_weight, out_weight, gate_up_weight, down_weight, *adapters,
@@ -459,65 +859,77 @@
         return lax.all_gather(value, AXES, axis=0, tiled=True)
 
     shapes = [member.shape[1:] for member in adapters]
-    slabs = lax.all_to_all(pack_adapters(adapter_ids, adapters, devices), AXES, 0, 0, tiled=True)
-    chosen = unpack_adapters(slabs, shapes)
-
-    qkv_full = gather(qkv_weight)
-    out_full = gather(out_weight)
-    gate_up_full = gather(gate_up_weight)
-    down_full = gather(down_weight)
-
-    qkv_bounds = (0, QW, QW + KW, QW + 2 * KW)
-    inputs = hidden.astype(F32)
-    normed, norm_pull = jax.vjp(lambda operand: rms_norm(operand, attn_gain), inputs)
-    normed_low = normed.astype(BF16)
-    reduced_qkv = contract_cols(normed_low, chosen[0]).astype(BF16)
-    projected = matmul(normed_low, qkv_full) + rank_apply(reduced_qkv, chosen[1], qkv_bounds)
-    (grouped, keyvals), head_pull = jax.vjp(
-        lambda operand: prepare_heads(operand, positions, query_gain, key_gain), projected
-    )
-    sent = jnp.concatenate([grouped * QSCALE, keyvals], axis=-1).astype(BF16).transpose(1, 0, 2)
+    def exchange_adapters(members):
+        return lax.all_to_all(pack_adapters(adapter_ids, members, devices), AXES, 0, 0, tiled=True)
+
+    spread = by_axes()
+    if spread:
+        found = {(0, 0): stack_shard(gate_up_weight, out_weight, down_weight)}
+        pending = []
+
+        def move(*keys, extra=()):
+            hops = [(found[key[0] ^ key[2], key[1] - key[3]], key[2], key[3]) for key in keys]
+            hops += extra
+            held = lax.optimization_barrier((*[value for value, _, _ in hops], *pending))
+            results = [hop(value, flip, step) for value, (_, flip, step) in zip(held, hops)]
+            found.update(zip([key[:2] for key in keys], results))
+            pending[:] = results
+            return results[len(keys) :]
+
+        def cores(*keys):
+            return [(flip, step, 1, 0) for flip, step in keys]
+
+        def then(value):
+            return lax.optimization_barrier((value, *pending))[0]
+
+        line = move(extra=[(qkv_weight, 0, step) for step in range(1, 4)])
+        slabs = exchange_adapters(adapters[:2])
+        line = jnp.concatenate([qkv_weight] + line, axis=0)
+        plane = move((0, 1, 0, 1), extra=[(line, flip, 0) for flip in (2, 4, 6)])
+        pending.append(slabs)
+        plane = jnp.concatenate([line] + plane, axis=0)
+        (across,) = move((0, 2, 0, 1), (2, 0, 2, 0), (4, 0, 4, 0), extra=[(plane, 1, 0)])
+        qkv = Pieces([((0, (0, 1, 2, 3)), plane), ((1, (0, 1, 2, 3)), across)], D)
+        hidden_then = hidden
+    else:
+        qkv = whole_gather(qkv_weight)
+        weights = [gather(jnp.concatenate([gate_up_weight, out_weight], axis=1)), gather(down_weight)]
+        hidden_then = hidden
+        slabs = exchange_adapters(adapters[:2])
+    chosen = list(unpack_adapters(slabs, shapes[:2]))
+
+    head_gain = jnp.stack([jnp.tile(query_gain, 2), jnp.tile(key_gain, 2)])
+    tables = rope_tables(positions)
+    sent, low_qkv, kept = project_heads(hidden_then, attn_gain, head_gain, tables, qkv, chosen[0], chosen[1])
     arrived = swap(sent).reshape(span, 2 * PAIR)
     queries = arrived[:, :PAIR]
     keyval_rows = arrived[:, PAIR:]
     if halo:
         keyval_rows = jnp.concatenate([shifted(keyval_rows[span - halo :], members), keyval_rows], axis=0)
+    if spread:
+        move((2, 1, 2, 0), (6, 0, 4, 0), *cores((1, 0)))
+        first = pending[:]
+        move((0, 3, 0, 1))
+        pending[:] = first
+        move((2, 2, 2, 0), (4, 1, 4, 0), *cores((1, 1), (3, 0)))
+        move((6, 1, 2, 0), (4, 2, 4, 0), *cores((5, 0), (7, 0)))
+        queries = then(queries)
+        move((2, 3, 2, 0), (4, 3, 4, 0), *cores((1, 2), (3, 1), (5, 1)))
+        slabs = exchange_adapters(lax.optimization_barrier((*adapters[2:], arrived))[:-1])
+    else:
+        slabs = exchange_adapters(adapters[2:])
     mixed, logs = forward_attention(bounds, starts, queries, keyval_rows)
-    mixture_tok = swap(mixed.reshape(members, rows, PAIR)).transpose(1, 0, 2).reshape(rows, QW)
-
-    reduced_out = contract_cols(mixture_tok, chosen[2]).astype(BF16)
-    branch = matmul(mixture_tok, out_full) + rank_apply(reduced_out, chosen[3], (0, D))
-    middle = inputs + branch
-    normed_two, norm_two_pull = jax.vjp(lambda operand: rms_norm(operand, ffn_gain), middle)
-    normed_two_low = normed_two.astype(BF16)
-    reduced_mlp = contract_cols(normed_two_low, chosen[4]).astype(BF16)
-    gate_up = matmul(normed_two_low, gate_up_full) + rank_apply(reduced_mlp, chosen[5], (0, FF, 2 * FF))
-    hidden_units, unit_pull = jax.vjp(
-        lambda operand: jax.nn.silu(operand[:, :FF]) * operand[:, FF:], gate_up
+    chosen += list(unpack_adapters(slabs, shapes[2:]))
+    if spread:
+        pending.append(logs)
+        move((6, 3, 2, 0), (6, 2, 4, 0), *cores((3, 2), (5, 2), (1, 3), (7, 1)))
+        move(*cores((3, 3), (5, 3), (7, 3), (7, 2)))
+        weights = Pieces([((flip, (step,)), block) for (flip, step), block in found.items()], D)
+    mixture_tok = swap(mixed.reshape(members, rows, PAIR))
+    output, middle_grad, mixture_grad, early = feed_forward(
+        mixture_tok, hidden, cotangent, ffn_gain, weights, chosen[2:]
     )
-    units_low = hidden_units.astype(BF16)
-    reduced_down = contract_cols(units_low, chosen[6]).astype(BF16)
-    branch_two = matmul(units_low, down_full) + rank_apply(reduced_down, chosen[7], (0, D))
-    output = (middle + branch_two).astype(BF16)
-
-    ffd_up_grad, reduced_down_grad = rank_back(cotangent, reduced_down, chosen[7], (0, D))
-    reduced_down_low = reduced_down_grad.astype(BF16)
-    ffd_down_grad = contract_rows(reduced_down_low, units_low)
-    units_grad = contract_cols(cotangent, down_full) + matmul(reduced_down_low, chosen[6])
-    gate_up_grad = unit_pull(units_grad)[0].astype(BF16)
-    mlp_up_grad, reduced_mlp_grad = rank_back(gate_up_grad, reduced_mlp, chosen[5], (0, FF, 2 * FF))
-    reduced_mlp_low = reduced_mlp_grad.astype(BF16)
-    mlp_down_grad = contract_rows(reduced_mlp_low, normed_two_low)
-    normed_two_grad = contract_cols(gate_up_grad, gate_up_full) + matmul(reduced_mlp_low, chosen[4])
-    middle_grad = cotangent.astype(F32) + norm_two_pull(normed_two_grad)[0]
-    branch_grad = middle_grad.astype(BF16)
-    out_up_grad, reduced_out_grad = rank_back(branch_grad, reduced_out, chosen[3], (0, D))
-    reduced_out_low = reduced_out_grad.astype(BF16)
-    out_down_grad = contract_rows(reduced_out_low, mixture_tok)
-    mixture_grad = (contract_cols(branch_grad, out_full) + matmul(reduced_out_low, chosen[2])).astype(BF16)
-    grad_rows = swap(mixture_grad.reshape(rows, members, PAIR).transpose(1, 0, 2)).reshape(span, PAIR)
-
-    early = [out_down_grad, out_up_grad, mlp_down_grad, mlp_up_grad, ffd_down_grad, ffd_up_grad]
+    grad_rows = swap(mixture_grad).reshape(span, PAIR)
     early_slabs = lax.all_to_all(pack_grads(early, devices), AXES, 0, 0, tiled=True)
     early_owned = reduce_grads(adapter_ids, early_slabs, shapes[2:])
 
@@ -530,15 +942,12 @@
             [keyval_grads[halo : halo + span - halo], keyval_grads[span:] + returned], axis=0
         ).astype(BF16)
     back = jnp.concatenate([query_grads, keyval_grads], axis=1).reshape(members, rows, 2 * PAIR)
-    back = swap(back).transpose(1, 0, 2).astype(F32)
-    projected_grad = head_pull((back[..., :PAIR], back[..., PAIR:]))[0].astype(BF16)
-    qkv_up_grad, reduced_qkv_grad = rank_back(projected_grad, reduced_qkv, chosen[1], qkv_bounds)
-    reduced_qkv_low = reduced_qkv_grad.astype(BF16)
-    qkv_down_grad = contract_rows(reduced_qkv_low, normed_low)
+    projected_grad, low_grad, qkv_up_grad, qkv_down_grad = project_back(
+        swap(back), kept, head_gain, tables, hidden, attn_gain, low_qkv, chosen[1]
+    )
     late_slabs = lax.all_to_all(pack_grads([qkv_down_grad, qkv_up_grad], devices), AXES, 0, 0, tiled=True)
     late_owned = reduce_grads(adapter_ids, late_slabs, shapes[:2])
-    normed_grad = contract_cols(projected_grad, qkv_full) + matmul(reduced_qkv_low, chosen[0])
-    input_grad = middle_grad + norm_pull(normed_grad)[0]
+    input_grad = input_back(projected_grad, low_grad, qkv, chosen[0], hidden, attn_gain, middle_grad)
     return (output, input_grad, *late_owned, *early_owned)
 
 

time: 661 us -> 483 us (0.73)
  waiting for transfers between devices: 328 us -> 166 us
  matrix products: 138 us -> 0 us
  Pallas kernels: 76.6 us -> 159 us
  starting transfers between devices: 38.4 us -> 87.9 us
  blocking collectives: 0 us -> 30.7 us
  other arithmetic: 23.7 us -> 4.2 us
  between operations: 15.2 us -> 1.54 us
    all_gather x4 -> x0, waiting for transfers between devices: 159 us -> none  [gather(): return lax.all_gather(value, AXES, axis=0, tiled=True)]
    dot_general x41 -> x0, matrix products: 138 us -> none  [the longest x15 79.3 us: matmul(): return jnp.dot(left_side, right_side, preferred_element_type=F32)]
    ppermute x0 -> x38, waiting for transfers between devices: none -> 97.4 us  [hop(): return lax.ppermute(value, AXES, pairs)]
    pallas_call x0 -> x5, Pallas kernels: none -> 81.9 us  [the longest x1 54.5 us: feed_forward(): pl.pallas_call(kernel, in_specs=[VMEM_SPEC] * 10 + [ANY_SPEC] * count, ou...]
    all_to_all x4 -> x3, waiting for transfers between devices: 139 us -> 65.7 us  [swap(): lax.all_to_all(value, AXES, 0, 0, axis_index_groups=groups, tiled=True)]
    ppermute x0 -> x38, starting transfers between devices: none -> 41.2 us  [hop(): return lax.ppermute(value, AXES, pairs)]
    all_to_all x0 -> x1, blocking collectives: none -> 30.7 us  [swap(): lax.all_to_all(value, AXES, 0, 0, axis_index_groups=groups, tiled=True)]
    all_to_all x1 -> x2, waiting for transfers between devices: 21.1 us -> 0.01 us  [exchange_adapters(): lax.all_to_all(pack_adapters(adapter_ids, members, devices), AXES, 0, 0,...]
  transfers between devices with their start and end apart: 11 -> 45, of which waited for: 9 -> 18; matrix products, arithmetic and copies ran while one was open for 13% -> 1% of each run, Pallas kernels for 11% -> 14%
where the time goes in v2:
time: 483 us; the launch traced here: 476 us
  waiting for transfers between devices  166 us (34%)
  Pallas kernels  159 us (33%)
  starting transfers between devices  87.9 us (18%)
  blocking collectives  30.7 us (6%)
  local copies, waits for them, and re-layouts  26.5 us (5%)
    ppermute x38, waiting for transfers between devices, hop(): return lax.ppermute(value, AXES, pairs)  97.4 us
    all_to_all x3, waiting for transfers between devices, swap(): lax.all_to_all(value, AXES, 0, 0, axis_index_groups=groups, tiled=True)  65.7 us
    pallas_call x1, Pallas kernels, feed_forward(): pl.pallas_call(kernel, in_specs=[VMEM_SPEC] * 10 + [ANY_SPEC] * count, ou...  54.5 us
    ppermute x38, starting transfers between devices, hop(): return lax.ppermute(value, AXES, pairs)  41.2 us
    pallas_call x1, Pallas kernels, backward_attention(): pl.pallas_call(kernel, grid_spec=pltpu.PrefetchScalarGridSpec(num_scalar_...  35 us
    all_to_all x1, blocking collectives, swap(): lax.all_to_all(value, AXES, 0, 0, axis_index_groups=groups, tiled=True)  30.7 us
    unnamed x74, local copies, waits for them, and re-layouts  24.4 us
    pallas_call x1, Pallas kernels, forward_attention(): pl.pallas_call(kernel, grid_spec=pltpu.PrefetchScalarGridSpec(num_scalar_...  24.4 us
  transfers between devices with their start and end apart: 45, of which 18 were waited for; matrix products, arithmetic and copies ran while one was open for 1% of the time, Pallas kernels for 14%

profile of v2, /device:TPU:0, one launch (start us, length us, event | category | flops | bytes accessed | tf_op | source)
XLA Modules:
  0.0 476.0 jit_solution(12424695726639903066)
XLA Ops:
  0.7 3.1 collective-permute-start
  3.7 2.6 collective-permute-start.1
  6.3 1.3 collective-permute-start.2
  7.7 1.6 copy.35.refs_0_
  9.2 2.4 pack_adapters.2
  11.7 2.9 all-to-all-start
  14.6 2.2 stack_shard.1.refs_10_
  16.9 1.8 collective-permute-start.3
  18.7 1.5 collective-permute-start.4
  20.5 1.8 collective-permute-start.6
  22.3 10.5 %collective-permute-done.3 = bf16[128,2048]{1,0:T(8,128)(2,1)S(1)} collective-permute-done((bf16[128,2048]{1,0:T(8,128)(2,1)S(1)}, bf16[128,2048]{1,0:T(8,128)(2,1)S(1)}, u32[]{:S(2)}, u32[]{:S(2)}) %collective-permute-start.3) | collective-permute-done | bytes 524320 | tf_op jit(solution)/shard_map/ppermute | solution.py:96
  32.9 10.5 %collective-permute-done.4 = bf16[128,2048]{1,0:T(8,128)(2,1)S(1)} collective-permute-done((bf16[128,2048]{1,0:T(8,128)(2,1)S(1)}, bf16[128,2048]{1,0:T(8,128)(2,1)S(1)}, u32[]{:S(2)}, u32[]{:S(2)}) %collective-permute-start.4) | collective-permute-done | bytes 524320 | tf_op jit(solution)/shard_map/ppermute | solution.py:96
  43.4 1.2 collective-permute-done.5
  46.5 1.2 pad_maximum_fusion.2
  47.7 1.9 unpack_adapters.2
  49.6 1.5 collective-permute-start.8
  51.1 1.1 collective-permute-start.9
  55.5 11.1 %project_heads.1 = (bf16[8,512,256]{2,1,0:T(8,128)(2,1)S(1)}, bf16[512,48]{1,0:T(8,128)(2,1)S(1)}, bf16[512,1536]{1,0:T(8,128)(2,1)S(1)}) custom-call(bf16[512,1024]{1,0:T(8,128)(2,1)S(1)} %copy-done, f32[1,1024]{1,0:T(1,128)S(1)} %bitcast.10, f32[2,128]{1,0:T(2,128)S(1)} %pad_maximum_fusion.4.refs_2_.head_gain_ref, ...), custom_call_target="tpu_custom_call" | custom-call | flops 2147483648 | bytes 10485760 | tf_op jit(solution)/shard_map/project_heads/pallas_call | solution.py:206
  66.6 1.3 copy-done.4
  67.9 1.2 copy-done.8
  69.8 4.8 %all-to-all-start.1 = ((bf16[8,512,256]{2,1,0:T(8,128)(2,1)}), bf16[8,512,256]{2,1,0:T(8,128)(2,1)S(1)}, u32[]{:S(2)}, u32[]{:S(2)}) async-start(bf16[8,512,256]{2,1,0:T(8,128)(2,1)} %copy-done.4), calls=%async_computation.1 | async-start | bytes 4194304 | tf_op jit(solution)/shard_map/all_to_all | solution.py:852
  74.9 1.6 collective-permute-start.11
  76.5 1.5 collective-permute-start.12
  77.9 20.4 %collective-permute-done.11.refs_15_ = bf16[464,1024]{1,0:T(8,128)(2,1)S(1)} collective-permute-done((bf16[464,1024]{1,0:T(8,128)(2,1)}, bf16[464,1024]{1,0:T(8,128)(2,1)S(1)}, u32[]{:S(2)}, u32[]{:S(2)}) %collective-permute-start.11) | collective-permute-done | bytes 950304 | tf_op jit(solution)/shard_map/ppermute | solution.py:96
  99.3 1.5 collective-permute-start.14
  100.7 1.1 collective-permute-start.15
  103.3 18.8 %collective-permute-done.14.refs_20_ = bf16[464,1024]{1,0:T(8,128)(2,1)} collective-permute-done((bf16[464,1024]{1,0:T(8,128)(2,1)}, bf16[464,1024]{1,0:T(8,128)(2,1)}, u32[]{:S(2)}, u32[]{:S(2)}) %collective-permute-start.14) | collective-permute-done | bytes 950304 | tf_op jit(solution)/shard_map/ppermute | solution.py:96
  123.8 1.2 collective-permute-start.19
  126.2 7.7 %collective-permute-done.22.refs_18_ = bf16[464,1024]{1,0:T(8,128)(2,1)} collective-permute-done((bf16[464,1024]{1,0:T(8,128)(2,1)}, bf16[464,1024]{1,0:T(8,128)(2,1)}, u32[]{:S(2)}, u32[]{:S(2)}) %collective-permute-start.22) | collective-permute-done | bytes 950304 | tf_op jit(solution)/shard_map/ppermute | solution.py:96
  133.8 10.6 %collective-permute-done.18.refs_23_ = bf16[464,1024]{1,0:T(8,128)(2,1)} collective-permute-done((bf16[464,1024]{1,0:T(8,128)(2,1)}, bf16[464,1024]{1,0:T(8,128)(2,1)}, u32[]{:S(2)}, u32[]{:S(2)}) %collective-permute-start.18) | collective-permute-done | bytes 950304 | tf_op jit(solution)/shard_map/ppermute | solution.py:96
  144.6 1.7 collective-permute-start.23
  147.5 1.3 copy-done.21
  148.8 1.7 fusion.1
  150.5 2.7 pack_adapters.3
  153.1 5.3 %all-to-all-start.3 = ((bf16[32,16,640]{2,1,0:T(8,128)(2,1)}), bf16[32,16,640]{2,1,0:T(8,128)(2,1)S(1)}, u32[]{:S(2)}, u32[]{:S(2)}) async-start(bf16[32,16,640]{2,1,0:T(8,128)(2,1)} %pack_adapters.3), calls=%async_computation.3 | async-start | bytes 1310720 | tf_op jit(solution)/shard_map/all_to_all | solution.py:863
  158.4 24.4 %forward_attention.1 = (bf16[4096,128]{1,0:T(8,128)(2,1)}, f32[16,8,512]{2,1,0:T(8,128)S(1)}) custom-call(s32[2,16]{1,0:T(2,128)S(1)} %pad_add_fusion.bound_ref, s32[1,4096]{1,0:T(1,128)S(1)} %bitcast.13, bf16[4096,128]{1,0:T(8,128)(2,1)S(1)} %get-tuple-element.116.query_ref, bf16[4096,128]{1,0:T(8,128)(2,1)S(1)} %get-tuple-element.204.keyval_ref), custom_call_target="tpu_custom_call" | custom-call | flops 8589934592 | bytes 4194304 | tf_op jit(solution)/shard_map/forward_attention/pallas_call | solution.py:491
  182.8 2.7 collective-permute-start.28
  185.5 8.8 %collective-permute-start.29 = (bf16[464,1024]{1,0:T(8,128)(2,1)}, bf16[464,1024]{1,0:T(8,128)(2,1)}, u32[]{:S(2)}, u32[]{:S(2)}) collective-permute-start(bf16[464,1024]{1,0:T(8,128)(2,1)} %collective-permute-done.15.refs_19_), channel_id=1, source_target_pairs={{0,16},{1,17},{2,18},{3,19},{4,20},{5,21},{6,22},{7,23},{8,24},{9,... | collective-permute-start | bytes 2850824 | tf_op jit(solution)/shard_map/ppermute | solution.py:96
  194.9 12.2 %collective-permute-done.28.refs_32_ = bf16[464,1024]{1,0:T(8,128)(2,1)S(1)} collective-permute-done((bf16[464,1024]{1,0:T(8,128)(2,1)}, bf16[464,1024]{1,0:T(8,128)(2,1)S(1)}, u32[]{:S(2)}, u32[]{:S(2)}) %collective-permute-start.28) | collective-permute-done | bytes 950304 | tf_op jit(solution)/shard_map/ppermute | solution.py:96
  208.0 4.7 all-to-all-start.2
  212.8 3.0 collective-permute-done.29.refs_33_
  216.9 2.3 unpack_adapters.3
  219.1 19.9 %all-to-all-done.2.refs_0_ = bf16[8,512,128]{2,1,0:T(8,128)(2,1)} async-done(((bf16[8,512,128]{2,1,0:T(8,128)(2,1)}), bf16[8,512,128]{2,1,0:T(8,128)(2,1)}, u32[]{:S(2)}, u32[]{:S(2)}) %all-to-all-start.2) | async-done | bytes 1048608 | tf_op jit(solution)/shard_map/all_to_all | solution.py:852
  239.0 54.5 %feed_forward.1 = (bf16[512,1024]{1,0:T(8,128)(2,1)}, f32[512,1024]{1,0:T(8,128)}, bf16[8,512,128]{2,1,0:T(8,128)(2,1)}, f32[16,1024]{1,0:T(8,128)}, f32[16,1024...) custom-call(bf16[8,512,128]{2,1,0:T(8,128)(2,1)} %all-to-all-done.2.refs_0_, ...), custom_call_target="tpu_custom_call" | custom-call | flops 31138512896 | bytes 36700160 | tf_op jit(solution)/shard_map/feed_forward/pallas_call | solution.py:800
  293.6 30.7 %all_to_all.40 = bf16[8,512,128]{2,1,0:T(8,128)(2,1)} all-to-all(bf16[8,512,128]{2,1,0:T(8,128)(2,1)} %get-tuple-element.148), channel_id=1, replica_groups={{0,1,2,3,4,5,6,7},{8,9,10,11,12,13,14,15},{16,17,18,19,20,21,22,23},{24..., dimensions={0} | all-to-all | bytes 2097152 | tf_op jit(solution)/shard_map/all_to_all | solution.py:852
  324.2 35.0 %backward_attention.1 = (bf16[4096,128]{1,0:T(8,128)(2,1)S(1)}, bf16[4096,128]{1,0:T(8,128)(2,1)S(1)}) custom-call(s32[2,16]{1,0:T(2,128)S(1)} %pad_add_fusion.bound_ref, s32[1,4096]{1,0:T(1,128)S(1)} %bitcast.14, bf16[4096,128]{1,0:T(8,128)(2,1)S(1)} %get-tuple-element.116.query_ref, bf16[4096,128]{1,0:T(8,128)(2,1)S(1)} %get-tuple-element.204.keyval_ref, ...), custom_call_target="tpu_custom_call" | custom-call | flops 21474836480 | bytes 8388608 | tf_op jit(solution)/shard_map/backward_attention/pallas_call | solution.py:582
  359.2 1.6 pad_maximum_fusion
  360.8 3.6 all-to-all-start.5
  364.4 2.6 pack_grads.3
  367.0 45.8 %all-to-all-done.5.back_ref = bf16[8,512,256]{2,1,0:T(8,128)(2,1)S(1)} async-done(((bf16[8,512,256]{2,1,0:T(8,128)(2,1)}), bf16[8,512,256]{2,1,0:T(8,128)(2,1)S(1)}, u32[]{:S(2)}, u32[]{:S(2)}) %all-to-all-start.5) | async-done | bytes 2097184 | tf_op jit(solution)/shard_map/all_to_all | solution.py:852
  412.9 20.7 %all-to-all-start.7 = ((bf16[32,16,640]{2,1,0:T(8,128)(2,1)}), bf16[32,16,640]{2,1,0:T(8,128)(2,1)}, u32[]{:S(2)}, u32[]{:S(2)}) async-start(bf16[32,16,640]{2,1,0:T(8,128)(2,1)} %pack_grads.3), calls=%async_computation.7 | async-start | bytes 1310720 | tf_op jit(solution)/shard_map/all_to_all | solution.py:933
  433.6 1.4 copy-done.9
  437.7 5.1 %project_back.1 = (bf16[512,2048]{1,0:T(8,128)(2,1)S(1)}, bf16[512,48]{1,0:T(8,128)(2,1)S(1)}, f32[16,2048]{1,0:T(8,128)S(1)}, f32[48,1024]{1,0:T(8,128)S(1)}) custom-call(bf16[8,512,256]{2,1,0:T(8,128)(2,1)S(1)} %all-to-all-done.5.back_ref, bf16[512,1536]{1,0:T(8,128)(2,1)S(1)} %copy-done.9, f32[2,128]{1,0:T(2,128)S(1)} %pad_maximum_fusion.4.refs_2_.head_gain_ref, ...), custom_call_target="tpu_custom_call" | custom-call | tf_op jit(solution)/shard_map/project_back/pallas_call | solution.py:268
  442.8 1.3 copy-done.6
  445.5 2.0 pack_grads.2
  447.5 3.0 all-to-all-done.7.source
  450.5 4.7 all-to-all-start.6
  455.2 2.1 reduce_grads.3
  457.3 1.6 copy-done.3
  458.9 1.6 copy-done.5
  460.5 1.6 copy-done.7
  463.0 9.0 %input_back.1 = f32[512,1024]{1,0:T(8,128)} custom-call(bf16[512,2048]{1,0:T(8,128)(2,1)S(1)} %copy-done.7, bf16[512,48]{1,0:T(8,128)(2,1)S(1)} %get-tuple-element.154.refs_1_, bf16[48,1024]{1,0:T(8,128)(2,1)S(1)} %copy-done.17, bf16[512,1024]{1,0:T(8,128)(2,1)S(1)} %copy-done.1, f32[1,1024]{1,0:T(1,128)S(1)} %bitcast.12, f32[512,1024]{1,0:T(8,128)S(1)} %copy-done.5, ...), custom_call_target="tpu_custom_call" | custom-call | flops 2147483648 | bytes 10485760 | tf_op jit(solution)/shard_map/input_back/pallas_call | solution.py:301
  472.0 1.8 reduce_grads.2
  473.9 1.7 copy.36
  (137 shorter events, 20.8 us)
Async XLA Ops:
  0.6 16.2 %copy-start.25 = (bf16[32,2048]{1,0:T(8,128)(2,1)S(1)}, bf16[32,2048]{1,0:T(8,128)(2,1)}, u32[]{:S(2)}) copy-start(bf16[32,2048]{1,0:T(8,128)(2,1)} %param.28) | copy-start | bytes 393220
  0.7 16.2 %collective-permute-start = (bf16[32,2048]{1,0:T(8,128)(2,1)}, bf16[32,2048]{1,0:T(8,128)(2,1)S(1)}, u32[]{:S(2)}, u32[]{:S(2)}) collective-permute-start(bf16[32,2048]{1,0:T(8,128)(2,1)} %param.28), channel_id=1, source_target_pairs={{0,1},{1,2},{2,3},{3,0},{4,5},{5,6},{6,7},{7,4},{8,9},{9,10},{10,1... | collective-permute-start | bytes 393224 | tf_op jit(solution)/shard_map/ppermute | solution.py:96
  3.7 13.1 %collective-permute-start.1 = (bf16[32,2048]{1,0:T(8,128)(2,1)}, bf16[32,2048]{1,0:T(8,128)(2,1)S(1)}, u32[]{:S(2)}, u32[]{:S(2)}) collective-permute-start(bf16[32,2048]{1,0:T(8,128)(2,1)} %param.28), channel_id=1, source_target_pairs={{0,2},{1,3},{2,0},{3,1},{4,6},{5,7},{6,4},{7,5},{8,10},{9,11},{10,... | collective-permute-start | bytes 393224 | tf_op jit(solution)/shard_map/ppermute | solution.py:96
  6.3 10.5 %collective-permute-start.2 = (bf16[32,2048]{1,0:T(8,128)(2,1)}, bf16[32,2048]{1,0:T(8,128)(2,1)S(1)}, u32[]{:S(2)}, u32[]{:S(2)}) collective-permute-start(bf16[32,2048]{1,0:T(8,128)(2,1)} %param.28), channel_id=1, source_target_pairs={{0,3},{1,0},{2,1},{3,2},{4,7},{5,4},{6,5},{7,6},{8,11},{9,8},{10,9... | collective-permute-start | bytes 393224 | tf_op jit(solution)/shard_map/ppermute | solution.py:96
  11.7 33.0 %all-to-all-start = ((bf16[32,16,256]{2,1,0:T(8,128)(2,1)}), bf16[32,16,256]{2,1,0:T(8,128)(2,1)S(1)}, u32[]{:S(2)}, u32[]{:S(2)}) async-start(bf16[32,16,256]{2,1,0:T(8,128)(2,1)} %pack_adapters.2), calls=%async_computation | async-start | bytes 524288 | tf_op jit(solution)/shard_map/all_to_all | solution.py:863
  16.9 28.1 %copy-start.31 = (f32[64]{0:T(128)S(1)}, f32[64]{0:T(128)}, u32[]{:S(2)}) copy-start(f32[64]{0:T(128)} %param.25) | copy-start | bytes 772
  16.9 28.1 %copy-start.32 = (f32[64]{0:T(128)S(1)}, f32[64]{0:T(128)}, u32[]{:S(2)}) copy-start(f32[64]{0:T(128)} %param.26) | copy-start | bytes 772
  16.9 15.9 %collective-permute-start.3 = (bf16[128,2048]{1,0:T(8,128)(2,1)S(1)}, bf16[128,2048]{1,0:T(8,128)(2,1)S(1)}, u32[]{:S(2)}, u32[]{:S(2)}) collective-permute-start(bf16[128,2048]{1,0:T(8,128)(2,1)S(1)} %pad_maximum_fusion.1), channel_id=1, source_target_pairs={{0,8},{1,9},{2,10},{3,11},{4,12},{5,13},{6,14},{7,15},{8,0},{9,1},... | collective-permute-start | bytes 1572872 | tf_op jit(solution)/shard_map/ppermute | solution.py:96
  18.7 24.6 %collective-permute-start.4 = (bf16[128,2048]{1,0:T(8,128)(2,1)S(1)}, bf16[128,2048]{1,0:T(8,128)(2,1)S(1)}, u32[]{:S(2)}, u32[]{:S(2)}) collective-permute-start(bf16[128,2048]{1,0:T(8,128)(2,1)S(1)} %pad_maximum_fusion.1), channel_id=1, source_target_pairs={{0,16},{1,17},{2,18},{3,19},{4,20},{5,21},{6,22},{7,23},{8,24},{9,... | collective-permute-start | bytes 1572872 | tf_op jit(solution)/shard_map/ppermute | solution.py:96
  20.2 24.4 %collective-permute-start.5 = (bf16[128,2048]{1,0:T(8,128)(2,1)S(1)}, bf16[128,2048]{1,0:T(8,128)(2,1)S(1)}, u32[]{:S(2)}, u32[]{:S(2)}) collective-permute-start(bf16[128,2048]{1,0:T(8,128)(2,1)S(1)} %pad_maximum_fusion.1), channel_id=1, source_target_pairs={{0,24},{1,25},{2,26},{3,27},{4,28},{5,29},{6,30},{7,31},{8,16},{9,... | collective-permute-start | bytes 1572872 | tf_op jit(solution)/shard_map/ppermute | solution.py:96
  20.5 24.5 %collective-permute-start.6 = (bf16[464,1024]{1,0:T(8,128)(2,1)}, bf16[464,1024]{1,0:T(8,128)(2,1)}, u32[]{:S(2)}, u32[]{:S(2)}) collective-permute-start(bf16[464,1024]{1,0:T(8,128)(2,1)} %stack_shard.1.refs_10_), channel_id=1, source_target_pairs={{0,1},{1,2},{2,3},{3,0},{4,5},{5,6},{6,7},{7,4},{8,9},{9,10},{10,1... | collective-permute-start | bytes 2850824 | tf_op jit(solution)/shard_map/ppermute | solution.py:96
  32.8 20.0 %copy-start = (bf16[512,1024]{1,0:T(8,128)(2,1)S(1)}, bf16[512,1024]{1,0:T(8,128)(2,1)}, u32[]{:S(2)}) copy-start(bf16[512,1024]{1,0:T(8,128)(2,1)} %refs_3_.2) | copy-start | bytes 3145732
  32.9 20.0 %copy-start.20 = (f32[1024]{0:T(1024)S(1)}, f32[1024]{0:T(1024)}, u32[]{:S(2)}) copy-start(f32[1024]{0:T(1024)} %param.24) | copy-start | bytes 12292
  44.6 21.9 %copy-start.2 = (bf16[512,2048]{1,0:T(8,128)(2,1)}, bf16[512,2048]{1,0:T(8,128)(2,1)S(1)}, u32[]{:S(2)}) copy-start(bf16[512,2048]{1,0:T(8,128)(2,1)S(1)} %constant_dynamic-update-slice_fusion.refs_7_.refs_6_) | copy-start | bytes 6291460
  45.0 7.9 %collective-permute-start.7 = (bf16[512,2048]{1,0:T(8,128)(2,1)S(1)}, bf16[512,2048]{1,0:T(8,128)(2,1)}, u32[]{:S(2)}, u32[]{:S(2)}) collective-permute-start(bf16[512,2048]{1,0:T(8,128)(2,1)S(1)} %constant_dynamic-update-slice_fusion.refs_7_.refs_6_), channel_id=1, source_target_pairs={{0,4},{1,5},{2,6},{3,7},{4,0},{5,1},{6,2},{7,3},{8,12},{9,13},{10,... | collective-permute-start | bytes 6291464 | tf_op jit(solution)/shard_map/ppermute | solution.py:96
  49.6 25.2 %collective-permute-start.8 = (bf16[464,1024]{1,0:T(8,128)(2,1)}, bf16[464,1024]{1,0:T(8,128)(2,1)}, u32[]{:S(2)}, u32[]{:S(2)}) collective-permute-start(bf16[464,1024]{1,0:T(8,128)(2,1)} %collective-permute-done.6.refs_11_), channel_id=1, source_target_pairs={{0,1},{1,2},{2,3},{3,0},{4,5},{5,6},{6,7},{7,4},{8,9},{9,10},{10,1... | collective-permute-start | bytes 2850824 | tf_op jit(solution)/shard_map/ppermute | solution.py:96
  51.1 23.7 %collective-permute-start.9 = (bf16[464,1024]{1,0:T(8,128)(2,1)}, bf16[464,1024]{1,0:T(8,128)(2,1)}, u32[]{:S(2)}, u32[]{:S(2)}) collective-permute-start(bf16[464,1024]{1,0:T(8,128)(2,1)} %stack_shard.1.refs_10_), channel_id=1, source_target_pairs={{0,8},{1,9},{2,10},{3,11},{4,12},{5,13},{6,14},{7,15},{8,0},{9,1},... | collective-permute-start | bytes 2850824 | tf_op jit(solution)/shard_map/ppermute | solution.py:96
  52.2 22.7 %collective-permute-start.10 = (bf16[464,1024]{1,0:T(8,128)(2,1)}, bf16[464,1024]{1,0:T(8,128)(2,1)}, u32[]{:S(2)}, u32[]{:S(2)}) collective-permute-start(bf16[464,1024]{1,0:T(8,128)(2,1)} %stack_shard.1.refs_10_), channel_id=1, source_target_pairs={{0,16},{1,17},{2,18},{3,19},{4,20},{5,21},{6,22},{7,23},{8,24},{9,... | collective-permute-start | bytes 2850824 | tf_op jit(solution)/shard_map/ppermute | solution.py:96
  66.6 1.3 copy-start.4
  69.8 8.2 %copy-start.24 = (bf16[464,1024]{1,0:T(8,128)(2,1)S(1)}, bf16[464,1024]{1,0:T(8,128)(2,1)}, u32[]{:S(2)}) copy-start(bf16[464,1024]{1,0:T(8,128)(2,1)} %stack_shard.1.refs_10_) | copy-start | bytes 2850820
  69.8 55.8 %copy-start.26 = (s32[16384]{0:T(1024)S(1)}, s32[16384]{0:T(1024)}, u32[]{:S(2)}) copy-start(s32[16384]{0:T(1024)} %param.22) | copy-start | bytes 196612
  69.8 77.7 %all-to-all-start.1 = ((bf16[8,512,256]{2,1,0:T(8,128)(2,1)}), bf16[8,512,256]{2,1,0:T(8,128)(2,1)S(1)}, u32[]{:S(2)}, u32[]{:S(2)}) async-start(bf16[8,512,256]{2,1,0:T(8,128)(2,1)} %copy-done.4), calls=%async_computation.1 | async-start | bytes 4194304 | tf_op jit(solution)/shard_map/all_to_all | solution.py:852
  74.9 23.4 %collective-permute-start.11 = (bf16[464,1024]{1,0:T(8,128)(2,1)}, bf16[464,1024]{1,0:T(8,128)(2,1)S(1)}, u32[]{:S(2)}, u32[]{:S(2)}) collective-permute-start(bf16[464,1024]{1,0:T(8,128)(2,1)} %collective-permute-done.6.refs_11_), channel_id=1, source_target_pairs={{0,8},{1,9},{2,10},{3,11},{4,12},{5,13},{6,14},{7,15},{8,0},{9,1},... | collective-permute-start | bytes 2850824 | tf_op jit(solution)/shard_map/ppermute | solution.py:96
  76.5 22.7 %collective-permute-start.12 = (bf16[464,1024]{1,0:T(8,128)(2,1)}, bf16[464,1024]{1,0:T(8,128)(2,1)}, u32[]{:S(2)}, u32[]{:S(2)}) collective-permute-start(bf16[464,1024]{1,0:T(8,128)(2,1)} %collective-permute-done.9.refs_13_), channel_id=1, source_target_pairs={{0,16},{1,17},{2,18},{3,19},{4,20},{5,21},{6,22},{7,23},{8,24},{9,... | collective-permute-start | bytes 2850824 | tf_op jit(solution)/shard_map/ppermute | solution.py:96
  77.9 21.3 %collective-permute-start.13 = (bf16[464,1024]{1,0:T(8,128)(2,1)S(1)}, bf16[464,1024]{1,0:T(8,128)(2,1)S(1)}, u32[]{:S(2)}, u32[]{:S(2)}) collective-permute-start(bf16[464,1024]{1,0:T(8,128)(2,1)S(1)} %copy-done.24), channel_id=1, source_target_pairs={{0,4},{1,5},{2,6},{3,7},{4,0},{5,1},{6,2},{7,3},{8,12},{9,13},{10,... | collective-permute-start | bytes 2850824 | tf_op jit(solution)/shard_map/ppermute | solution.py:96
  99.3 1.5 copy-start.28
  99.3 22.8 %collective-permute-start.14 = (bf16[464,1024]{1,0:T(8,128)(2,1)}, bf16[464,1024]{1,0:T(8,128)(2,1)}, u32[]{:S(2)}, u32[]{:S(2)}) collective-permute-start(bf16[464,1024]{1,0:T(8,128)(2,1)} %collective-permute-done.6.refs_11_), channel_id=1, source_target_pairs={{0,16},{1,17},{2,18},{3,19},{4,20},{5,21},{6,22},{7,23},{8,24},{9,... | collective-permute-start | bytes 2850824 | tf_op jit(solution)/shard_map/ppermute | solution.py:96
  100.7 22.3 %collective-permute-start.15 = (bf16[464,1024]{1,0:T(8,128)(2,1)}, bf16[464,1024]{1,0:T(8,128)(2,1)}, u32[]{:S(2)}, u32[]{:S(2)}) collective-permute-start(bf16[464,1024]{1,0:T(8,128)(2,1)} %collective-permute-done.8.refs_12_), channel_id=1, source_target_pairs={{0,8},{1,9},{2,10},{3,11},{4,12},{5,13},{6,14},{7,15},{8,0},{9,1},... | collective-permute-start | bytes 2850824 | tf_op jit(solution)/shard_map/ppermute | solution.py:96
  101.8 21.2 %collective-permute-start.16 = (bf16[464,1024]{1,0:T(8,128)(2,1)}, bf16[464,1024]{1,0:T(8,128)(2,1)S(1)}, u32[]{:S(2)}, u32[]{:S(2)}) collective-permute-start(bf16[464,1024]{1,0:T(8,128)(2,1)} %collective-permute-done.6.refs_11_), channel_id=1, source_target_pairs={{0,4},{1,5},{2,6},{3,7},{4,0},{5,1},{6,2},{7,3},{8,12},{9,13},{10,... | collective-permute-start | bytes 2850824 | tf_op jit(solution)/shard_map/ppermute | solution.py:96
  101.8 21.2 %collective-permute-start.17 = (bf16[464,1024]{1,0:T(8,128)(2,1)}, bf16[464,1024]{1,0:T(8,128)(2,1)}, u32[]{:S(2)}, u32[]{:S(2)}) collective-permute-start(bf16[464,1024]{1,0:T(8,128)(2,1)} %collective-permute-done.9.refs_13_), channel_id=1, source_target_pairs={{0,4},{1,5},{2,6},{3,7},{4,0},{5,1},{6,2},{7,3},{8,12},{9,13},{10,... | collective-permute-start | bytes 2850824 | tf_op jit(solution)/shard_map/ppermute | solution.py:96
  102.3 31.5 %collective-permute-start.22 = (bf16[464,1024]{1,0:T(8,128)(2,1)}, bf16[464,1024]{1,0:T(8,128)(2,1)}, u32[]{:S(2)}, u32[]{:S(2)}) collective-permute-start(bf16[464,1024]{1,0:T(8,128)(2,1)} %collective-permute-done.8.refs_12_), channel_id=1, source_target_pairs={{0,1},{1,2},{2,3},{3,0},{4,5},{5,6},{6,7},{7,4},{8,9},{9,10},{10,1... | collective-permute-start | bytes 2850824 | tf_op jit(solution)/shard_map/ppermute | solution.py:96
  123.0 2.5 copy-start.29
  123.0 21.4 %collective-permute-start.18 = (bf16[464,1024]{1,0:T(8,128)(2,1)}, bf16[464,1024]{1,0:T(8,128)(2,1)}, u32[]{:S(2)}, u32[]{:S(2)}) collective-permute-start(bf16[464,1024]{1,0:T(8,128)(2,1)} %collective-permute-done.14.refs_20_), channel_id=1, source_target_pairs={{0,8},{1,9},{2,10},{3,11},{4,12},{5,13},{6,14},{7,15},{8,0},{9,1},... | collective-permute-start | bytes 2850824 | tf_op jit(solution)/shard_map/ppermute | solution.py:96
  123.8 20.7 %collective-permute-start.19 = (bf16[464,1024]{1,0:T(8,128)(2,1)}, bf16[464,1024]{1,0:T(8,128)(2,1)}, u32[]{:S(2)}, u32[]{:S(2)}) collective-permute-start(bf16[464,1024]{1,0:T(8,128)(2,1)} %collective-permute-done.8.refs_12_), channel_id=1, source_target_pairs={{0,16},{1,17},{2,18},{3,19},{4,20},{5,21},{6,22},{7,23},{8,24},{9,... | collective-permute-start | bytes 2850824 | tf_op jit(solution)/shard_map/ppermute | solution.py:96
  125.0 19.5 %collective-permute-start.20 = (bf16[464,1024]{1,0:T(8,128)(2,1)}, bf16[464,1024]{1,0:T(8,128)(2,1)}, u32[]{:S(2)}, u32[]{:S(2)}) collective-permute-start(bf16[464,1024]{1,0:T(8,128)(2,1)} %collective-permute-done.10.refs_14_), channel_id=1, source_target_pairs={{0,4},{1,5},{2,6},{3,7},{4,0},{5,1},{6,2},{7,3},{8,12},{9,13},{10,... | collective-permute-start | bytes 2850824 | tf_op jit(solution)/shard_map/ppermute | solution.py:96
  125.0 19.5 %collective-permute-start.21 = (bf16[464,1024]{1,0:T(8,128)(2,1)}, bf16[464,1024]{1,0:T(8,128)(2,1)}, u32[]{:S(2)}, u32[]{:S(2)}) collective-permute-start(bf16[464,1024]{1,0:T(8,128)(2,1)} %collective-permute-done.12.refs_16_), channel_id=1, source_target_pairs={{0,4},{1,5},{2,6},{3,7},{4,0},{5,1},{6,2},{7,3},{8,12},{9,13},{10,... | collective-permute-start | bytes 2850824 | tf_op jit(solution)/shard_map/ppermute | solution.py:96
  144.6 38.2 %collective-permute-start.23 = (bf16[464,1024]{1,0:T(8,128)(2,1)}, bf16[464,1024]{1,0:T(8,128)(2,1)}, u32[]{:S(2)}, u32[]{:S(2)}) collective-permute-start(bf16[464,1024]{1,0:T(8,128)(2,1)} %collective-permute-done.22.refs_18_), channel_id=1, source_target_pairs={{0,8},{1,9},{2,10},{3,11},{4,12},{5,13},{6,14},{7,15},{8,0},{9,1},... | collective-permute-start | bytes 2850824 | tf_op jit(solution)/shard_map/ppermute | solution.py:96
  146.2 36.6 %collective-permute-start.24 = (bf16[464,1024]{1,0:T(8,128)(2,1)}, bf16[464,1024]{1,0:T(8,128)(2,1)}, u32[]{:S(2)}, u32[]{:S(2)}) collective-permute-start(bf16[464,1024]{1,0:T(8,128)(2,1)} %collective-permute-done.22.refs_18_), channel_id=1, source_target_pairs={{0,16},{1,17},{2,18},{3,19},{4,20},{5,21},{6,22},{7,23},{8,24},{9,... | collective-permute-start | bytes 2850824 | tf_op jit(solution)/shard_map/ppermute | solution.py:96
  146.9 35.9 %collective-permute-start.25 = (bf16[464,1024]{1,0:T(8,128)(2,1)}, bf16[464,1024]{1,0:T(8,128)(2,1)}, u32[]{:S(2)}, u32[]{:S(2)}) collective-permute-start(bf16[464,1024]{1,0:T(8,128)(2,1)} %collective-permute-done.8.refs_12_), channel_id=1, source_target_pairs={{0,4},{1,5},{2,6},{3,7},{4,0},{5,1},{6,2},{7,3},{8,12},{9,13},{10,... | collective-permute-start | bytes 2850824 | tf_op jit(solution)/shard_map/ppermute | solution.py:96
  146.9 35.9 %collective-permute-start.26 = (bf16[464,1024]{1,0:T(8,128)(2,1)}, bf16[464,1024]{1,0:T(8,128)(2,1)}, u32[]{:S(2)}, u32[]{:S(2)}) collective-permute-start(bf16[464,1024]{1,0:T(8,128)(2,1)} %copy-done.27), channel_id=1, source_target_pairs={{0,4},{1,5},{2,6},{3,7},{4,0},{5,1},{6,2},{7,3},{8,12},{9,13},{10,... | collective-permute-start | bytes 2850824 | tf_op jit(solution)/shard_map/ppermute | solution.py:96
  147.5 35.4 %collective-permute-start.27 = (bf16[464,1024]{1,0:T(8,128)(2,1)}, bf16[464,1024]{1,0:T(8,128)(2,1)}, u32[]{:S(2)}, u32[]{:S(2)}) collective-permute-start(bf16[464,1024]{1,0:T(8,128)(2,1)} %collective-permute-done.14.refs_20_), channel_id=1, source_target_pairs={{0,4},{1,5},{2,6},{3,7},{4,0},{5,1},{6,2},{7,3},{8,12},{9,13},{10,... | collective-permute-start | bytes 2850824 | tf_op jit(solution)/shard_map/ppermute | solution.py:96
  147.5 1.3 copy-start.21
  153.1 54.9 %all-to-all-start.3 = ((bf16[32,16,640]{2,1,0:T(8,128)(2,1)}), bf16[32,16,640]{2,1,0:T(8,128)(2,1)S(1)}, u32[]{:S(2)}, u32[]{:S(2)}) async-start(bf16[32,16,640]{2,1,0:T(8,128)(2,1)} %pack_adapters.3), calls=%async_computation.3 | async-start | bytes 1310720 | tf_op jit(solution)/shard_map/all_to_all | solution.py:863
  182.8 24.3 %collective-permute-start.28 = (bf16[464,1024]{1,0:T(8,128)(2,1)}, bf16[464,1024]{1,0:T(8,128)(2,1)S(1)}, u32[]{:S(2)}, u32[]{:S(2)}) collective-permute-start(bf16[464,1024]{1,0:T(8,128)(2,1)} %collective-permute-done.24.refs_28_), channel_id=1, source_target_pairs={{0,8},{1,9},{2,10},{3,11},{4,12},{5,13},{6,14},{7,15},{8,0},{9,1},... | collective-permute-start | bytes 2850824 | tf_op jit(solution)/shard_map/ppermute | solution.py:96
  185.5 30.2 %collective-permute-start.29 = (bf16[464,1024]{1,0:T(8,128)(2,1)}, bf16[464,1024]{1,0:T(8,128)(2,1)}, u32[]{:S(2)}, u32[]{:S(2)}) collective-permute-start(bf16[464,1024]{1,0:T(8,128)(2,1)} %collective-permute-done.15.refs_19_), channel_id=1, source_target_pairs={{0,16},{1,17},{2,18},{3,19},{4,20},{5,21},{6,22},{7,23},{8,24},{9,... | collective-permute-start | bytes 2850824 | tf_op jit(solution)/shard_map/ppermute | solution.py:96
  194.4 21.4 %collective-permute-start.30 = (bf16[464,1024]{1,0:T(8,128)(2,1)}, bf16[464,1024]{1,0:T(8,128)(2,1)}, u32[]{:S(2)}, u32[]{:S(2)}) collective-permute-start(bf16[464,1024]{1,0:T(8,128)(2,1)} %collective-permute-done.15.refs_19_), channel_id=1, source_target_pairs={{0,4},{1,5},{2,6},{3,7},{4,0},{5,1},{6,2},{7,3},{8,12},{9,13},{10,... | collective-permute-start | bytes 2850824 | tf_op jit(solution)/shard_map/ppermute | solution.py:96
  194.4 21.4 %collective-permute-start.31 = (bf16[464,1024]{1,0:T(8,128)(2,1)}, bf16[464,1024]{1,0:T(8,128)(2,1)}, u32[]{:S(2)}, u32[]{:S(2)}) collective-permute-start(bf16[464,1024]{1,0:T(8,128)(2,1)} %collective-permute-done.19.refs_24_), channel_id=1, source_target_pairs={{0,4},{1,5},{2,6},{3,7},{4,0},{5,1},{6,2},{7,3},{8,12},{9,13},{10,... | collective-permute-start | bytes 2850824 | tf_op jit(solution)/shard_map/ppermute | solution.py:96
  194.9 20.9 %collective-permute-start.32 = (bf16[464,1024]{1,0:T(8,128)(2,1)}, bf16[464,1024]{1,0:T(8,128)(2,1)}, u32[]{:S(2)}, u32[]{:S(2)}) collective-permute-start(bf16[464,1024]{1,0:T(8,128)(2,1)} %collective-permute-done.22.refs_18_), channel_id=1, source_target_pairs={{0,4},{1,5},{2,6},{3,7},{4,0},{5,1},{6,2},{7,3},{8,12},{9,13},{10,... | collective-permute-start | bytes 2850824 | tf_op jit(solution)/shard_map/ppermute | solution.py:96
  208.0 7.7 %collective-permute-start.33 = (bf16[464,1024]{1,0:T(8,128)(2,1)}, bf16[464,1024]{1,0:T(8,128)(2,1)}, u32[]{:S(2)}, u32[]{:S(2)}) collective-permute-start(bf16[464,1024]{1,0:T(8,128)(2,1)} %collective-permute-done.18.refs_23_), channel_id=1, source_target_pairs={{0,4},{1,5},{2,6},{3,7},{4,0},{5,1},{6,2},{7,3},{8,12},{9,13},{10,... | collective-permute-start | bytes 2850824 | tf_op jit(solution)/shard_map/ppermute | solution.py:96
  208.0 8.8 %copy-start.22 = (bf16[32,16,640]{2,1,0:T(8,128)(2,1)}, bf16[32,16,640]{2,1,0:T(8,128)(2,1)S(1)}, u32[]{:S(2)}) copy-start(bf16[32,16,640]{2,1,0:T(8,128)(2,1)S(1)} %all-to-all-done.3.source) | copy-start | bytes 1966084
  208.0 31.0 %all-to-all-start.2 = ((bf16[8,512,128]{2,1,0:T(8,128)(2,1)}), bf16[8,512,128]{2,1,0:T(8,128)(2,1)}, u32[]{:S(2)}, u32[]{:S(2)}) async-start(bf16[8,512,128]{2,1,0:T(8,128)(2,1)} %bitcast.5), calls=%async_computation.2 | async-start | bytes 2097152 | tf_op jit(solution)/shard_map/all_to_all | solution.py:852
  215.8 23.2 %collective-permute-start.34 = (bf16[464,1024]{1,0:T(8,128)(2,1)}, bf16[464,1024]{1,0:T(8,128)(2,1)}, u32[]{:S(2)}, u32[]{:S(2)}) collective-permute-start(bf16[464,1024]{1,0:T(8,128)(2,1)} %collective-permute-done.23.refs_27_), channel_id=1, source_target_pairs={{0,4},{1,5},{2,6},{3,7},{4,0},{5,1},{6,2},{7,3},{8,12},{9,13},{10,... | collective-permute-start | bytes 2850824 | tf_op jit(solution)/shard_map/ppermute | solution.py:96
  215.9 23.1 %collective-permute-start.35 = (bf16[464,1024]{1,0:T(8,128)(2,1)}, bf16[464,1024]{1,0:T(8,128)(2,1)}, u32[]{:S(2)}, u32[]{:S(2)}) collective-permute-start(bf16[464,1024]{1,0:T(8,128)(2,1)} %collective-permute-done.24.refs_28_), channel_id=1, source_target_pairs={{0,4},{1,5},{2,6},{3,7},{4,0},{5,1},{6,2},{7,3},{8,12},{9,13},{10,... | collective-permute-start | bytes 2850824 | tf_op jit(solution)/shard_map/ppermute | solution.py:96
  216.3 22.7 %collective-permute-start.36 = (bf16[464,1024]{1,0:T(8,128)(2,1)}, bf16[464,1024]{1,0:T(8,128)(2,1)}, u32[]{:S(2)}, u32[]{:S(2)}) collective-permute-start(bf16[464,1024]{1,0:T(8,128)(2,1)} %copy-done.30), channel_id=1, source_target_pairs={{0,4},{1,5},{2,6},{3,7},{4,0},{5,1},{6,2},{7,3},{8,12},{9,13},{10,... | collective-permute-start | bytes 2850824 | tf_op jit(solution)/shard_map/ppermute | solution.py:96
  216.4 22.6 %collective-permute-start.37 = (bf16[464,1024]{1,0:T(8,128)(2,1)}, bf16[464,1024]{1,0:T(8,128)(2,1)}, u32[]{:S(2)}, u32[]{:S(2)}) collective-permute-start(bf16[464,1024]{1,0:T(8,128)(2,1)} %collective-permute-done.29.refs_33_), channel_id=1, source_target_pairs={{0,4},{1,5},{2,6},{3,7},{4,0},{5,1},{6,2},{7,3},{8,12},{9,13},{10,... | collective-permute-start | bytes 2850824 | tf_op jit(solution)/shard_map/ppermute | solution.py:96
  360.8 52.1 %all-to-all-start.5 = ((bf16[8,512,256]{2,1,0:T(8,128)(2,1)}), bf16[8,512,256]{2,1,0:T(8,128)(2,1)S(1)}, u32[]{:S(2)}, u32[]{:S(2)}) async-start(bf16[8,512,256]{2,1,0:T(8,128)(2,1)} %bitcast.16), calls=%async_computation.5 | async-start | bytes 4194304 | tf_op jit(solution)/shard_map/all_to_all | solution.py:852
  364.4 69.2 %copy-start.1 = (bf16[512,1024]{1,0:T(8,128)(2,1)S(1)}, bf16[512,1024]{1,0:T(8,128)(2,1)}, u32[]{:S(2)}) copy-start(bf16[512,1024]{1,0:T(8,128)(2,1)} %refs_3_.2) | copy-start | bytes 3145732
  412.9 37.6 %all-to-all-start.7 = ((bf16[32,16,640]{2,1,0:T(8,128)(2,1)}), bf16[32,16,640]{2,1,0:T(8,128)(2,1)}, u32[]{:S(2)}, u32[]{:S(2)}) async-start(bf16[32,16,640]{2,1,0:T(8,128)(2,1)} %pack_grads.3), calls=%async_computation.7 | async-start | bytes 1310720 | tf_op jit(solution)/shard_map/all_to_all | solution.py:933
  433.6 1.4 copy-start.9
  442.8 1.3 copy-start.6
  450.5 21.5 %all-to-all-start.6 = ((bf16[32,16,256]{2,1,0:T(8,128)(2,1)}), bf16[32,16,256]{2,1,0:T(8,128)(2,1)}, u32[]{:S(2)}, u32[]{:S(2)}) async-start(bf16[32,16,256]{2,1,0:T(8,128)(2,1)} %pack_grads.2), calls=%async_computation.6 | async-start | bytes 524288 | tf_op jit(solution)/shard_map/all_to_all | solution.py:948
  457.3 1.6 copy-start.3
  458.9 1.6 copy-start.5
  460.5 1.6 copy-start.7
  (14 other events, 12.2 us)

commit v3 on v2

--- a/solution.py
+++ b/solution.py
@@ -152,6 +152,21 @@
     return lax.rsqrt(jnp.mean(values * values, axis=1, keepdims=True) + epsilon)
 
 
+ROWS = 256
+
+
+def in_hbm(value):
+    return pltpu.with_memory_space_constraint(value, pltpu.HBM)
+
+
+def row_block(width):
+    return pl.BlockSpec((ROWS, width), lambda i: (i, 0))
+
+
+def fixed(shape):
+    return pl.BlockSpec(shape, lambda i: (0,) * len(shape))
+
+
 def project_heads(hidden, gain, head_gain, tables, pieces, down, up):
     rows = hidden.shape[0]
     count = len(pieces.blocks)
@@ -161,15 +176,19 @@
         hidden_ref, gain_ref, head_gain_ref, cos_ref, sin_ref, down_ref, up_ref = refs[:7]
         blocks = refs[7 : 7 + count]
         sent_ref, low_ref, kept_ref, weight, sem = refs[7 + count :]
-        start_loads(pieces, blocks, weight, sem)
+
+        @pl.when(pl.program_id(0) == 0)
+        def _():
+            start_loads(pieces, blocks, weight, sem)
+            finish_loads(weight, sem)
+
         inputs = hidden_ref[...].astype(F32)
         normed = (inputs * row_scale(inputs) * gain_ref[...]).astype(BF16)
         low = contract_cols(normed, down_ref[...]).astype(BF16)
         low_ref[...] = low
         ones = head_ones()
         cos, sin = cos_ref[...], sin_ref[...]
-        lanes = lax.broadcasted_iota(jnp.int32, (rows, PAIR), 1)
-        finish_loads(weight, sem)
+        lanes = lax.broadcasted_iota(jnp.int32, (ROWS, PAIR), 1)
 
         def columns(start, size, group):
             return matmul(normed, weight[:, start : start + size]) + matmul(
@@ -180,20 +199,20 @@
             unit = values * lax.rsqrt(head_means(values * values, ones) + epsilon) * gains
             return unit * cos + swapped_halves(unit) * sin
 
-        step = 2 * PAIR
+        step = 4 * PAIR
         for start in range(0, QW, step):
-            both = columns(start, step, 0)
-            kept_ref[:, start : start + step] = both.astype(BF16)
-            for side in range(2):
-                query = turned(both[:, side * PAIR : (side + 1) * PAIR], head_gain_ref[0:1, :]) * QSCALE
+            some = columns(start, step, 0)
+            kept_ref[:, start : start + step] = some.astype(BF16)
+            for side in range(step // PAIR):
+                query = turned(some[:, side * PAIR : (side + 1) * PAIR], head_gain_ref[0:1, :]) * QSCALE
                 sent_ref[start // PAIR + side, :, :PAIR] = query.astype(BF16)
         for start in range(0, KW, step):
-            both = columns(QW + start, step, 1)
+            some = columns(QW + start, step, 1)
             values = columns(QW + KW + start, step, 2)
-            kept_ref[:, QW + start : QW + start + step] = both.astype(BF16)
-            for side in range(2):
+            kept_ref[:, QW + start : QW + start + step] = some.astype(BF16)
+            for side in range(step // PAIR):
                 where = slice(side * PAIR, (side + 1) * PAIR)
-                key = turned(both[:, where], head_gain_ref[1:2, :])
+                key = turned(some[:, where], head_gain_ref[1:2, :])
                 value = values[:, where]
                 group = (start + side * PAIR) // HEAD_DIM
                 sent_ref[group, :, PAIR:] = jnp.where(
@@ -205,8 +224,15 @@
 
     return pl.pallas_call(
         kernel,
-        in_specs=[VMEM_SPEC] * 7 + [ANY_SPEC] * count,
-        out_specs=[VMEM_SPEC] * 3,
+        grid=(rows // ROWS,),
+        in_specs=[
+            row_block(D), fixed((1, D)), fixed((2, PAIR)), row_block(PAIR), row_block(PAIR),
+            fixed((3 * RANK, D)), fixed((RANK, width)),
+        ]
+        + [ANY_SPEC] * count,
+        out_specs=[
+            pl.BlockSpec((KV_HEADS, ROWS, 2 * PAIR), lambda i: (0, i, 0)), row_block(3 * RANK), row_block(QW + KW),
+        ],
         out_shape=[
             jax.ShapeDtypeStruct((KV_HEADS, rows, 2 * PAIR), BF16),
             jax.ShapeDtypeStruct((rows, 3 * RANK), BF16),
@@ -219,17 +245,23 @@
     )(hidden, gain[None, :], head_gain, *tables, down, up, *pieces.blocks)
 
 
-def project_back(back, kept, head_gain, tables, hidden, gain, low, up):
+def project_back(back, kept, head_gain, tables, hidden, gain, low, up, devices):
     rows = hidden.shape[0]
     width = QW + 2 * KW
+    places, slab = layout_of([(3 * RANK, D // devices), (RANK, width // devices)])
 
     def kernel(
         back_ref, kept_ref, head_gain_ref, cos_ref, sin_ref, hidden_ref, gain_ref, low_ref, up_ref,
-        grad_ref, low_grad_ref, up_grad_ref, down_grad_ref,
+        grad_ref, low_grad_ref, packed_ref, down_sum, up_sum,
     ):
         ones = head_ones()
         cos, sin = cos_ref[...], sin_ref[...]
-        lanes = lax.broadcasted_iota(jnp.int32, (rows, PAIR), 1)
+        lanes = lax.broadcasted_iota(jnp.int32, (ROWS, PAIR), 1)
+
+        @pl.when(pl.program_id(0) == 0)
+        def _():
+            down_sum[...] = jnp.zeros_like(down_sum)
+            up_sum[...] = jnp.zeros_like(up_sum)
 
         def through(grads, values, gains):
             slope = (grads * cos - swapped_halves(grads) * sin) * gains
@@ -250,34 +282,45 @@
             where = slice(start, start + PAIR)
             grad_ref[:, where] = through(keys, kept_ref[:, where].astype(F32), head_gain_ref[1:2, :]).astype(BF16)
             grad_ref[:, start + KW : start + KW + PAIR] = values.astype(BF16)
-        low = low_ref[...]
-        turned = low.astype(F32).T.astype(BF16)
+        turned = low_ref[...].astype(F32).T.astype(BF16)
         edges = (0, QW, QW + KW, width)
         parts = []
         for group in range(3):
             where = slice(edges[group], edges[group + 1])
             grads = grad_ref[:, where]
-            up_grad_ref[:, where] = matmul(turned[RANK * group : RANK * (group + 1), :], grads)
+            up_sum[:, where] += matmul(turned[RANK * group : RANK * (group + 1), :], grads)
             parts.append(contract_cols(grads, up_ref[:, where]))
         low_grad = jnp.concatenate(parts, axis=1)
         low_grad_ref[...] = low_grad.astype(BF16)
         inputs = hidden_ref[...].astype(F32)
         normed = (inputs * row_scale(inputs) * gain_ref[...]).astype(BF16)
-        down_grad_ref[...] = matmul(low_grad.T.astype(BF16), normed)
+        down_sum[...] += matmul(low_grad.T.astype(BF16), normed)
+
+        @pl.when(pl.program_id(0) == rows // ROWS - 1)
+        def _():
+            for device in range(devices):
+                for index, part, offset, size in places:
+                    packed_ref[device, :, offset : offset + size] = (down_sum, up_sum)[index][
+                        RANK * part : RANK * (part + 1), device * size : (device + 1) * size
+                    ].astype(BF16)
 
     return pl.pallas_call(
         kernel,
-        in_specs=[VMEM_SPEC] * 9,
-        out_specs=[VMEM_SPEC] * 4,
+        grid=(rows // ROWS,),
+        in_specs=[
+            pl.BlockSpec((KV_HEADS, ROWS, 2 * PAIR), lambda i: (0, i, 0)), row_block(QW + KW), fixed((2, PAIR)),
+            row_block(PAIR), row_block(PAIR), row_block(D), fixed((1, D)), row_block(3 * RANK), fixed((RANK, width)),
+        ],
+        out_specs=[row_block(width), row_block(3 * RANK), fixed((devices, RANK, slab))],
         out_shape=[
             jax.ShapeDtypeStruct((rows, width), BF16),
             jax.ShapeDtypeStruct((rows, 3 * RANK), BF16),
-            jax.ShapeDtypeStruct((RANK, width), F32),
-            jax.ShapeDtypeStruct((3 * RANK, D), F32),
+            jax.ShapeDtypeStruct((devices, RANK, slab), BF16),
         ],
+        scratch_shapes=[pltpu.VMEM((3 * RANK, D), F32), pltpu.VMEM((RANK, width), F32)],
         compiler_params=pltpu.CompilerParams(vmem_limit_bytes=40 << 20),
         name="project_back",
-    )(back, kept, head_gain, *tables, hidden, gain[None, :], low, up)
+    )(back, in_hbm(kept), head_gain, *[in_hbm(table) for table in tables], hidden, gain[None, :], in_hbm(low), up)
 
 
 def input_back(grad, low_grad, pieces, down, hidden, gain, middle_grad):
@@ -288,26 +331,34 @@
         grad_ref, low_ref, down_ref, hidden_ref, gain_ref, middle_ref = refs[:6]
         blocks = refs[6 : 6 + count]
         out_ref, weight, sem = refs[6 + count :]
-        start_loads(pieces, blocks, weight, sem)
+
+        @pl.when(pl.program_id(0) == 0)
+        def _():
+            start_loads(pieces, blocks, weight, sem)
+            finish_loads(weight, sem)
+
         inputs = hidden_ref[...].astype(F32)
         scale = row_scale(inputs)
-        slope = matmul(low_ref[...], down_ref[...])
-        finish_loads(weight, sem)
-        slope = (slope + contract_cols(grad_ref[...], weight[...])) * gain_ref[...]
+        slope = matmul(low_ref[...], down_ref[...]) + contract_cols(grad_ref[...], weight[...])
+        slope = slope * gain_ref[...]
         unit = inputs * scale
         inner = jnp.mean(slope * unit, axis=1, keepdims=True)
         out_ref[...] = middle_ref[...] + scale * (slope - unit * inner)
 
     return pl.pallas_call(
         kernel,
-        in_specs=[VMEM_SPEC] * 6 + [ANY_SPEC] * count,
-        out_specs=VMEM_SPEC,
+        grid=(rows // ROWS,),
+        in_specs=[
+            row_block(QW + 2 * KW), row_block(3 * RANK), fixed((3 * RANK, D)), row_block(D), fixed((1, D)), row_block(D),
+        ]
+        + [ANY_SPEC] * count,
+        out_specs=row_block(D),
         out_shape=jax.ShapeDtypeStruct((rows, D), F32),
         scratch_shapes=[pltpu.VMEM((D, QW + 2 * KW), BF16), pltpu.SemaphoreType.DMA],
         compiler_params=pltpu.CompilerParams(vmem_limit_bytes=40 << 20),
         cost_estimate=pl.CostEstimate(flops=2 * rows * D * 2048, bytes_accessed=10 << 20, transcendentals=0),
         name="input_back",
-    )(grad, low_grad, down, hidden, gain[None, :], middle_grad, *pieces.blocks)
+    )(in_hbm(grad), low_grad, down, hidden, gain[None, :], in_hbm(middle_grad), *[in_hbm(block) for block in pieces.blocks])
 
 
 VMEM_SPEC = pl.BlockSpec(memory_space=pltpu.VMEM)
@@ -331,14 +382,20 @@
 def pack_adapters(adapter_ids, members, devices):
     places, width = layout_of([member.shape[1:] for member in members])
     per_seq = devices // NSEQ
+    turned = [member.shape[1] % (2 * RANK) != 0 and member.shape[1] > RANK for member in members]
+    members = [jnp.swapaxes(member, 1, 2) if turn else member for member, turn in zip(members, turned)]
 
     def kernel(ids, *refs):
         sources, out, slab = refs[: len(members)], refs[len(members)], refs[len(members) + 1]
         slab[...] = jnp.zeros_like(slab)
         for index, part, offset, size in places:
-            slab[:, offset : offset + size] = sources[index][
-                ids[pl.program_id(0)], RANK * part : RANK * (part + 1), :
-            ]
+            picked = ids[pl.program_id(0)]
+            rank_rows = slice(RANK * part, RANK * (part + 1))
+            if turned[index]:
+                piece = sources[index][picked, :, rank_rows].astype(F32).T.astype(BF16)
+            else:
+                piece = sources[index][picked, rank_rows, :]
+            slab[:, offset : offset + size] = piece
         for step in range(per_seq):
             out[step] = slab[...]
 
@@ -397,6 +454,7 @@
     devices, _, width = slabs.shape
     places, _ = layout_of(shapes)
     per_seq = devices // NSEQ
+    turned = [rows % (2 * RANK) != 0 and rows > RANK for rows, _ in shapes]
 
     def kernel(ids, source, *refs):
         outs, total = refs[: len(shapes)], refs[len(shapes)]
@@ -405,16 +463,25 @@
             part_sum = jnp.sum(source[seq * per_seq : (seq + 1) * per_seq].astype(F32), axis=0)
             total[ids[seq]] += part_sum
         for index, part, offset, size in places:
-            outs[index][:, RANK * part : RANK * (part + 1), :] = total[:, :, offset : offset + size]
-
-    return pl.pallas_call(
+            rank_rows = slice(RANK * part, RANK * (part + 1))
+            if turned[index]:
+                for adapter in range(ADAPTERS):
+                    outs[index][adapter, :, rank_rows] = total[adapter, :, offset : offset + size].T
+            else:
+                outs[index][:, rank_rows, :] = total[:, :, offset : offset + size]
+
+    sums = pl.pallas_call(
         kernel,
         in_specs=[SMEM_SPEC, VMEM_SPEC],
         out_specs=[VMEM_SPEC] * len(shapes),
-        out_shape=[jax.ShapeDtypeStruct((ADAPTERS, rows, size), F32) for rows, size in shapes],
+        out_shape=[
+            jax.ShapeDtypeStruct((ADAPTERS, *((size, rows) if turn else (rows, size))), F32)
+            for (rows, size), turn in zip(shapes, turned)
+        ],
         scratch_shapes=[pltpu.VMEM((ADAPTERS, RANK, width), F32)],
         name="reduce_grads",
     )(adapter_ids, slabs)
+    return [jnp.swapaxes(value, 1, 2) if turn else value for value, turn in zip(sums, turned)]
 
 
 def split_three(value):
@@ -445,7 +512,7 @@
     return jnp.concatenate([inside, inside], axis=1)
 
 
-def forward_attention(bounds, starts, queries, keyvals):
+def forward_attention(bounds, starts, queries, keyvals, column):
     rows = queries.shape[0]
     length = keyvals.shape[0]
     halo = length - rows
@@ -496,7 +563,7 @@
             in_specs=[
                 pl.BlockSpec((1, BLOCK), lambda i, b: (0, i)),
                 pl.BlockSpec((BLOCK, 128), lambda i, b: (i, 0)),
-                pl.BlockSpec((length, 128), lambda i, b: (0, 0)),
+                pl.BlockSpec((length, 128), lambda i, b: (0, column)),
             ],
             out_specs=[
                 pl.BlockSpec((BLOCK, 128), lambda i, b: (i, 0)),
@@ -516,16 +583,14 @@
     )(bounds, starts, queries, keyvals)
 
 
-def backward_attention(bounds, starts, queries, keyvals, mixed, logs, grads):
+def backward_attention(bounds, starts, queries, keyvals, column, mixed, logs, grads):
     rows = queries.shape[0]
     length = keyvals.shape[0]
     halo = length - rows
     steps = rows // BLOCK
 
-    def kernel(
-        bound_ref, start_ref, query_ref, keyval_ref, mixed_ref, log_ref, grad_ref,
-        query_out, keyval_out, key_scr, value_scr, turned_scr, key_sum, value_sum,
-    ):
+    def kernel(bound_ref, start_ref, query_ref, keyval_ref, mixed_ref, log_ref, grad_ref, *refs):
+        outs, (key_scr, value_scr, turned_scr, key_sum, value_sum) = refs[:-5], refs[-5:]
         step = pl.program_id(0)
 
         @pl.when(step == 0)
@@ -570,14 +635,22 @@
         total = lax.fori_loop(clear, diagonal, lambda i, t: block(i, t, False, False), total)
         total = block(diagonal, total, True, True)
         total = total[:HEAD_DIM] * HEAD_DIM**-0.5
-        query_out[...] = jnp.concatenate([total[:, :BLOCK], total[:, BLOCK:]], axis=0).T.astype(BF16)
+        query_grad = jnp.concatenate([total[:, :BLOCK], total[:, BLOCK:]], axis=0).T.astype(BF16)
+        if halo:
+            outs[0][...] = query_grad
+        else:
+            outs[0][pl.ds(pl.multiple_of(step * BLOCK, BLOCK), BLOCK), :PAIR] = query_grad
 
         @pl.when(step == steps - 1)
         def _():
             whole = lax.broadcasted_iota(jnp.int32, (length, 128), 1)
-            keyval_out[...] = jnp.where(
+            keyval_grad = jnp.where(
                 whole < HEAD_DIM, key_sum[...] * (1.0 / LOG2E), pltpu.roll(value_sum[...], HEAD_DIM, 1)
-            ).astype(keyval_out.dtype)
+            )
+            if halo:
+                outs[1][...] = keyval_grad
+            else:
+                outs[0][:, PAIR:] = keyval_grad.astype(BF16)
 
     return pl.pallas_call(
         kernel,
@@ -587,7 +660,7 @@
             in_specs=[
                 pl.BlockSpec((1, BLOCK), lambda i, b: (0, i)),
                 pl.BlockSpec((BLOCK, 128), lambda i, b: (i, 0)),
-                pl.BlockSpec((length, 128), lambda i, b: (0, 0)),
+                pl.BlockSpec((length, 128), lambda i, b: (0, column)),
                 pl.BlockSpec((BLOCK, 128), lambda i, b: (i, 0)),
                 pl.BlockSpec((1, 8, 2 * BLOCK), lambda i, b: (i, 0, 0)),
                 pl.BlockSpec((BLOCK, 128), lambda i, b: (i, 0)),
@@ -595,7 +668,9 @@
             out_specs=[
                 pl.BlockSpec((BLOCK, 128), lambda i, b: (i, 0)),
                 pl.BlockSpec((length, 128), lambda i, b: (0, 0)),
-            ],
+            ]
+            if halo
+            else [pl.BlockSpec((rows, 2 * PAIR), lambda i, b: (0, 0))],
             scratch_shapes=[
                 pltpu.VMEM((length, 128), BF16),
                 pltpu.VMEM((length, 128), BF16),
@@ -604,10 +679,9 @@
                 pltpu.VMEM((length, 128), F32),
             ],
         ),
-        out_shape=[
-            jax.ShapeDtypeStruct((rows, 128), BF16),
-            jax.ShapeDtypeStruct((length, 128), F32 if halo else BF16),
-        ],
+        out_shape=[jax.ShapeDtypeStruct((rows, 128), BF16), jax.ShapeDtypeStruct((length, 128), F32)]
+        if halo
+        else [jax.ShapeDtypeStruct((rows, 2 * PAIR), BF16)],
         compiler_params=pltpu.CompilerParams(vmem_limit_bytes=48 << 20),
         cost_estimate=pl.CostEstimate(
             flops=10 * rows * 1024 * 256 * 2, bytes_accessed=8 * rows * 256, transcendentals=rows * 2048
@@ -859,8 +933,8 @@
         return lax.all_gather(value, AXES, axis=0, tiled=True)
 
     shapes = [member.shape[1:] for member in adapters]
-    def exchange_adapters(members):
-        return lax.all_to_all(pack_adapters(adapter_ids, members, devices), AXES, 0, 0, tiled=True)
+    def exchange(packed):
+        return lax.all_to_all(packed, AXES, 0, 0, tiled=True)
 
     spread = by_axes()
     if spread:
@@ -882,70 +956,77 @@
         def then(value):
             return lax.optimization_barrier((value, *pending))[0]
 
-        line = move(extra=[(qkv_weight, 0, step) for step in range(1, 4)])
-        slabs = exchange_adapters(adapters[:2])
+        line = move((2, 0, 2, 0), (4, 0, 4, 0), extra=[(qkv_weight, 0, step) for step in range(1, 4)])
+        slabs = exchange(lax.optimization_barrier((pack_adapters(adapter_ids, adapters[:2], devices), *line))[0])
         line = jnp.concatenate([qkv_weight] + line, axis=0)
         plane = move((0, 1, 0, 1), extra=[(line, flip, 0) for flip in (2, 4, 6)])
         pending.append(slabs)
         plane = jnp.concatenate([line] + plane, axis=0)
-        (across,) = move((0, 2, 0, 1), (2, 0, 2, 0), (4, 0, 4, 0), extra=[(plane, 1, 0)])
+        (across,) = move((0, 2, 0, 1), (2, 1, 2, 0), (6, 0, 4, 0), extra=[(plane, 1, 0)])
         qkv = Pieces([((0, (0, 1, 2, 3)), plane), ((1, (0, 1, 2, 3)), across)], D)
         hidden_then = hidden
     else:
         qkv = whole_gather(qkv_weight)
         weights = [gather(jnp.concatenate([gate_up_weight, out_weight], axis=1)), gather(down_weight)]
         hidden_then = hidden
-        slabs = exchange_adapters(adapters[:2])
+        slabs = exchange(pack_adapters(adapter_ids, adapters[:2], devices))
     chosen = list(unpack_adapters(slabs, shapes[:2]))
 
     head_gain = jnp.stack([jnp.tile(query_gain, 2), jnp.tile(key_gain, 2)])
     tables = rope_tables(positions)
     sent, low_qkv, kept = project_heads(hidden_then, attn_gain, head_gain, tables, qkv, chosen[0], chosen[1])
-    arrived = swap(sent).reshape(span, 2 * PAIR)
-    queries = arrived[:, :PAIR]
-    keyval_rows = arrived[:, PAIR:]
+    if spread:
+        sent = then(sent)
+    queries = swap(sent).reshape(span, 2 * PAIR)
+    keyvals, column = queries, 1
     if halo:
-        keyval_rows = jnp.concatenate([shifted(keyval_rows[span - halo :], members), keyval_rows], axis=0)
+        keyvals, column = queries[:, PAIR:], 0
+        keyvals = jnp.concatenate([shifted(keyvals[span - halo :], members), keyvals], axis=0)
     if spread:
-        move((2, 1, 2, 0), (6, 0, 4, 0), *cores((1, 0)))
+        move((2, 2, 2, 0), (4, 1, 4, 0), *cores((1, 0)))
         first = pending[:]
         move((0, 3, 0, 1))
         pending[:] = first
-        move((2, 2, 2, 0), (4, 1, 4, 0), *cores((1, 1), (3, 0)))
-        move((6, 1, 2, 0), (4, 2, 4, 0), *cores((5, 0), (7, 0)))
-        queries = then(queries)
-        move((2, 3, 2, 0), (4, 3, 4, 0), *cores((1, 2), (3, 1), (5, 1)))
-        slabs = exchange_adapters(lax.optimization_barrier((*adapters[2:], arrived))[:-1])
+        late_adapters = then(adapters[2])
+        move((6, 1, 2, 0), (4, 2, 4, 0), *cores((1, 1), (3, 0)))
+        keyvals = queries = then(queries)
+        move((2, 3, 2, 0), (4, 3, 4, 0), *cores((5, 0), (7, 0), (1, 2)))
     else:
-        slabs = exchange_adapters(adapters[2:])
-    mixed, logs = forward_attention(bounds, starts, queries, keyval_rows)
+        late_adapters = adapters[2]
+    packed = pack_adapters(adapter_ids, (late_adapters, *adapters[3:]), devices)
+    slabs = exchange(lax.optimization_barrier((packed, queries))[0])
+    mixed, logs = forward_attention(bounds, starts, queries, keyvals, column)
     chosen += list(unpack_adapters(slabs, shapes[2:]))
     if spread:
         pending.append(logs)
-        move((6, 3, 2, 0), (6, 2, 4, 0), *cores((3, 2), (5, 2), (1, 3), (7, 1)))
-        move(*cores((3, 3), (5, 3), (7, 3), (7, 2)))
+        move((6, 3, 2, 0), (6, 2, 4, 0), *cores((3, 1), (5, 1), (3, 2)))
+    mixed_then = lax.optimization_barrier((mixed, slabs))[0]
+    mixture_tok = swap(mixed_then.reshape(members, rows, PAIR))
+    if spread:
+        move(*cores((5, 2), (7, 1), (1, 3), (3, 3), (5, 3)))
+        pending.append(mixture_tok)
+        move(*cores((7, 2), (7, 3)))
         weights = Pieces([((flip, (step,)), block) for (flip, step), block in found.items()], D)
-    mixture_tok = swap(mixed.reshape(members, rows, PAIR))
     output, middle_grad, mixture_grad, early = feed_forward(
         mixture_tok, hidden, cotangent, ffn_gain, weights, chosen[2:]
     )
     grad_rows = swap(mixture_grad).reshape(span, PAIR)
-    early_slabs = lax.all_to_all(pack_grads(early, devices), AXES, 0, 0, tiled=True)
+    early_packed, grad_rows = lax.optimization_barrier((pack_grads(early, devices), grad_rows))
+    early_slabs = exchange(early_packed)
+    back = backward_attention(bounds, starts, queries, keyvals, column, mixed, logs, grad_rows)
+    if halo:
+        query_grads, keyval_grads = back
+        returned = shifted(keyval_grads[:halo].astype(BF16), -members).astype(F32)
+        keyval_grads = jnp.concatenate([keyval_grads[halo:span], keyval_grads[span:] + returned], axis=0)
+        back = [jnp.concatenate([query_grads, keyval_grads.astype(BF16)], axis=1)]
+    back, early_slabs = lax.optimization_barrier((back[0], early_slabs))
     early_owned = reduce_grads(adapter_ids, early_slabs, shapes[2:])
-
-    query_grads, keyval_grads = backward_attention(
-        bounds, starts, queries, keyval_rows, mixed, logs, grad_rows
+    back = back.reshape(members, rows, 2 * PAIR)
+    arrived_back = swap(back)
+    projected_grad, low_grad, packed = project_back(
+        arrived_back, kept, head_gain, tables, hidden, attn_gain, low_qkv, chosen[1], devices
     )
-    if halo:
-        returned = shifted(keyval_grads[:halo].astype(BF16), -members).astype(F32)
-        keyval_grads = jnp.concatenate(
-            [keyval_grads[halo : halo + span - halo], keyval_grads[span:] + returned], axis=0
-        ).astype(BF16)
-    back = jnp.concatenate([query_grads, keyval_grads], axis=1).reshape(members, rows, 2 * PAIR)
-    projected_grad, low_grad, qkv_up_grad, qkv_down_grad = project_back(
-        swap(back), kept, head_gain, tables, hidden, attn_gain, low_qkv, chosen[1]
-    )
-    late_slabs = lax.all_to_all(pack_grads([qkv_down_grad, qkv_up_grad], devices), AXES, 0, 0, tiled=True)
+    late_slabs = exchange(packed)
     late_owned = reduce_grads(adapter_ids, late_slabs, shapes[:2])
     input_grad = input_back(projected_grad, low_grad, qkv, chosen[0], hidden, attn_gain, middle_grad)
     return (output, input_grad, *late_owned, *early_owned)

time: 483 us -> 441 us (0.913); the launches traced: 476 us -> 441 us
  waiting for transfers between devices: 166 us -> 137 us
  blocking collectives: 30.7 us -> 53.2 us
  starting transfers between devices: 87.9 us -> 69.6 us
  local copies, waits for them, and re-layouts: 26.5 us -> 11.4 us
  Pallas kernels: 159 us -> 166 us
    all_to_all x1, blocking collectives: 30.7 us -> 53.2 us  [swap(): lax.all_to_all(value, AXES, 0, 0, axis_index_groups=groups, tiled=True)]
    all_to_all x3, waiting for transfers between devices: 65.7 us -> 44.8 us  [swap(): lax.all_to_all(value, AXES, 0, 0, axis_index_groups=groups, tiled=True)]
    all_to_all x4, starting transfers between devices: 33.6 us -> 18.8 us  [exchange(): return lax.all_to_all(packed, AXES, 0, 0, tiled=True)]
    unnamed x74 -> x76, local copies, waits for them, and re-layouts: 24.4 us -> 11 us
    ppermute x38, waiting for transfers between devices: 97.4 us -> 92.2 us  [hop(): return lax.ppermute(value, AXES, pairs)]
  transfers between devices with their start and end apart: 45 -> 45, of which waited for: 18 -> 23; matrix products, arithmetic and copies ran while one was open for 1% -> 1% of each run, Pallas kernels for 14% -> 22%
where the time goes in v3:
time: 441 us
  Pallas kernels  166 us (38%)
  waiting for transfers between devices  137 us (31%)
  starting transfers between devices  69.6 us (16%)
  blocking collectives  53.2 us (12%)
  local copies, waits for them, and re-layouts  11.4 us (3%)
    ppermute x38, waiting for transfers between devices, hop(): return lax.ppermute(value, AXES, pairs)  92.2 us
    pallas_call x1, Pallas kernels, feed_forward(): pl.pallas_call(kernel, in_specs=[VMEM_SPEC] * 10 + [ANY_SPEC] * count, ou...  54.7 us
    all_to_all x1, blocking collectives, swap(): lax.all_to_all(value, AXES, 0, 0, axis_index_groups=groups, tiled=True)  53.2 us
    all_to_all x3, waiting for transfers between devices, swap(): lax.all_to_all(value, AXES, 0, 0, axis_index_groups=groups, tiled=True)  44.8 us
    pallas_call x1, Pallas kernels, backward_attention(): pl.pallas_call(kernel, grid_spec=pltpu.PrefetchScalarGridSpec(num_scalar_...  37.4 us
    ppermute x38, starting transfers between devices, hop(): return lax.ppermute(value, AXES, pairs)  36.7 us
    pallas_call x1, Pallas kernels, forward_attention(): pl.pallas_call(kernel, grid_spec=pltpu.PrefetchScalarGridSpec(num_scalar_...  26.5 us
    all_to_all x4, starting transfers between devices, exchange(): return lax.all_to_all(packed, AXES, 0, 0, tiled=True)  18.8 us
  transfers between devices with their start and end apart: 45, of which 23 were waited for; matrix products, arithmetic and copies ran while one was open for 1% of the time, Pallas kernels for 22%

profile of v3, /device:TPU:0, one launch (start us, length us, event | category | flops | bytes accessed | tf_op | source)
XLA Modules:
  0.0 441.3 jit_solution(4194396760615069973)
XLA Ops:
  0.7 2.3 stack_shard.1.refs_10_
  2.9 2.9 collective-permute-start.3
  5.9 1.5 collective-permute-start.4
  7.4 1.6 collective-permute-start
  9.0 2.6 collective-permute-start.1
  11.6 1.3 collective-permute-start.2
  12.9 2.8 pack_adapters.2
  16.0 3.9 collective-permute-done.1
  20.0 4.6 %all-to-all-start = ((bf16[32,16,256]{2,1,0:T(8,128)(2,1)}), bf16[32,16,256]{2,1,0:T(8,128)(2,1)S(1)}, u32[]{:S(2)}, u32[]{:S(2)}) async-start(bf16[32,16,256]{2,1,0:T(8,128)(2,1)} %pack_adapters.2), calls=%async_computation | async-start | bytes 524288 | tf_op jit(solution)/shard_map/all_to_all | solution.py:937
  24.6 2.6 collective-permute-done.3.refs_11_
  27.2 2.3 collective-permute-done.4.refs_12_
  29.7 2.5 collective-permute-start.6
  32.2 1.8 collective-permute-start.8
  34.0 1.6 collective-permute-start.7
  35.6 9.2 %collective-permute-done.5 = bf16[128,2048]{1,0:T(8,128)(2,1)S(1)} collective-permute-done((bf16[128,2048]{1,0:T(8,128)(2,1)S(1)}, bf16[128,2048]{1,0:T(8,128)(2,1)S(1)}, u32[]{:S(2)}, u32[]{:S(2)}) %collective-permute-start.5) | collective-permute-done | bytes 524320 | tf_op jit(solution)/shard_map/ppermute | solution.py:96
  44.9 8.1 %collective-permute-done.6 = bf16[128,2048]{1,0:T(8,128)(2,1)S(1)} collective-permute-done((bf16[128,2048]{1,0:T(8,128)(2,1)S(1)}, bf16[128,2048]{1,0:T(8,128)(2,1)S(1)}, u32[]{:S(2)}, u32[]{:S(2)}) %collective-permute-start.6) | collective-permute-done | bytes 524320 | tf_op jit(solution)/shard_map/ppermute | solution.py:96
  53.0 1.5 collective-permute-done.7
  54.9 1.4 collective-permute-start.10
  57.1 1.2 collective-permute-start.12
  58.5 1.0 fusion
  59.5 1.2 pad_maximum_fusion.1
  60.6 2.0 unpack_adapters.2
  62.6 0.9 copy-done.8
  65.3 11.8 %project_heads.1 = (bf16[8,512,256]{2,1,0:T(8,128)(2,1)S(1)}, bf16[512,48]{1,0:T(8,128)(2,1)S(1)}, bf16[512,1536]{1,0:T(8,128)(2,1)S(1)}) custom-call(bf16[512,1024]{1,0:T(8,128)(2,1)S(1)} %copy-done, f32[1,1024]{1,0:T(1,128)S(1)} %bitcast.18, f32[2,128]{1,0:T(2,128)S(1)} %pad_maximum_fusion.3.refs_2_.head_gain_ref, ...), custom_call_target="tpu_custom_call" | custom-call | flops 2147483648 | bytes 10485760 | tf_op jit(solution)/shard_map/project_heads/pallas_call | solution.py:225
  77.1 1.3 copy-done.4
  78.4 1.2 copy-done.6
  80.6 4.4 all-to-all-start.1
  84.9 1.0 collective-permute-start.13
  86.7 22.0 %collective-permute-done.13.refs_18_ = bf16[464,1024]{1,0:T(8,128)(2,1)} collective-permute-done((bf16[464,1024]{1,0:T(8,128)(2,1)}, bf16[464,1024]{1,0:T(8,128)(2,1)}, u32[]{:S(2)}, u32[]{:S(2)}) %collective-permute-start.13) | collective-permute-done | bytes 950304 | tf_op jit(solution)/shard_map/ppermute | solution.py:96
  110.2 1.1 collective-permute-start.17
  111.8 1.7 collective-permute-start.20
  113.9 2.7 pack_adapters.3
  116.6 15.6 %collective-permute-done.16.refs_21_ = bf16[464,1024]{1,0:T(8,128)(2,1)} collective-permute-done((bf16[464,1024]{1,0:T(8,128)(2,1)}, bf16[464,1024]{1,0:T(8,128)(2,1)}, u32[]{:S(2)}, u32[]{:S(2)}) %collective-permute-start.16) | collective-permute-done | bytes 950304 | tf_op jit(solution)/shard_map/ppermute | solution.py:96
  132.6 21.3 %all-to-all-done.1 = bf16[8,512,256]{2,1,0:T(8,128)(2,1)S(1)} async-done(((bf16[8,512,256]{2,1,0:T(8,128)(2,1)}), bf16[8,512,256]{2,1,0:T(8,128)(2,1)S(1)}, u32[]{:S(2)}, u32[]{:S(2)}) %all-to-all-start.1) | async-done | bytes 2097184 | tf_op jit(solution)/shard_map/all_to_all | solution.py:926
  153.9 2.7 all-to-all-start.2
  156.8 1.7 collective-permute-start.21
  158.5 1.5 collective-permute-start.22
  160.5 26.5 %forward_attention.1 = (bf16[4096,128]{1,0:T(8,128)(2,1)}, f32[16,8,512]{2,1,0:T(8,128)S(1)}) custom-call(s32[2,16]{1,0:T(2,128)S(1)} %pad_add_fusion.bound_ref, s32[1,4096]{1,0:T(1,128)S(1)} %bitcast.21, bf16[4096,256]{1,0:T(8,128)(2,1)S(1)} %bitcast.12, bf16[4096,256]{1,0:T(8,128)(2,1)S(1)} %bitcast.13), custom_call_target="tpu_custom_call" | custom-call | flops 8589934592 | bytes 4194304 | tf_op jit(solution)/shard_map/forward_attention/pallas_call | solution.py:558
  187.3 1.1 collective-permute-start.26
  188.4 4.1 collective-permute-start.27
  193.3 4.9 %all-to-all-start.3 = ((bf16[8,512,128]{2,1,0:T(8,128)(2,1)}), bf16[8,512,128]{2,1,0:T(8,128)(2,1)S(1)}, u32[]{:S(2)}, u32[]{:S(2)}) async-start(bf16[8,512,128]{2,1,0:T(8,128)(2,1)} %bitcast.6), calls=%async_computation.3 | async-start | bytes 2097152 | tf_op jit(solution)/shard_map/all_to_all | solution.py:926
  198.2 12.8 %collective-permute-done.26.refs_30_ = bf16[464,1024]{1,0:T(8,128)(2,1)} collective-permute-done((bf16[464,1024]{1,0:T(8,128)(2,1)}, bf16[464,1024]{1,0:T(8,128)(2,1)}, u32[]{:S(2)}, u32[]{:S(2)}) %collective-permute-start.26) | collective-permute-done | bytes 950304 | tf_op jit(solution)/shard_map/ppermute | solution.py:96
  211.0 3.5 collective-permute-done.27.refs_31_
  215.7 1.6 collective-permute-done.31.refs_35_
  217.3 4.1 collective-permute-done.32.refs_36_
  221.4 1.4 collective-permute-done.33.refs_37_
  222.8 0.9 copy-done.30
  223.7 0.9 copy-done.31
  225.2 2.3 unpack_adapters.3
  227.5 1.4 collective-permute-done.37.refs_41_
  228.9 54.7 %feed_forward.1 = (bf16[512,1024]{1,0:T(8,128)(2,1)}, f32[512,1024]{1,0:T(8,128)}, bf16[8,512,128]{2,1,0:T(8,128)(2,1)}, f32[16,1024]{1,0:T(8,128)}, f32[16,1024...) custom-call(bf16[8,512,128]{2,1,0:T(8,128)(2,1)} %copy-done.18, ...), custom_call_target="tpu_custom_call" | custom-call | flops 31138512896 | bytes 36700160 | tf_op jit(solution)/shard_map/feed_forward/pallas_call | solution.py:874
  283.7 4.8 %all-to-all-start.4 = ((bf16[8,512,128]{2,1,0:T(8,128)(2,1)}), bf16[8,512,128]{2,1,0:T(8,128)(2,1)S(1)}, u32[]{:S(2)}, u32[]{:S(2)}) async-start(bf16[8,512,128]{2,1,0:T(8,128)(2,1)} %get-tuple-element.153), calls=%async_computation.4 | async-start | bytes 2097152 | tf_op jit(solution)/shard_map/all_to_all | solution.py:926
  288.4 2.6 pack_grads.1
  291.0 23.6 %all-to-all-done.4 = bf16[8,512,128]{2,1,0:T(8,128)(2,1)S(1)} async-done(((bf16[8,512,128]{2,1,0:T(8,128)(2,1)}), bf16[8,512,128]{2,1,0:T(8,128)(2,1)S(1)}, u32[]{:S(2)}, u32[]{:S(2)}) %all-to-all-start.4) | async-done | bytes 1048608 | tf_op jit(solution)/shard_map/all_to_all | solution.py:926
  314.6 3.8 all-to-all-start.5
  318.4 0.9 copy-done.16
  319.4 37.4 %backward_attention.1 = bf16[4096,256]{1,0:T(8,128)(2,1)S(1)} custom-call(s32[2,16]{1,0:T(2,128)S(1)} %pad_add_fusion.bound_ref, s32[1,4096]{1,0:T(1,128)S(1)} %bitcast.22, bf16[4096,256]{1,0:T(8,128)(2,1)} %bitcast.14, bf16[4096,256]{1,0:T(8,128)(2,1)} %bitcast.15, bf16[4096,128]{1,0:T(8,128)(2,1)} %get-tuple-element.120.mixed_ref, ...), custom_call_target="tpu_custom_call" | custom-call | flops 21474836480 | bytes 8388608 | tf_op jit(solution)/shard_map/backward_attention/pallas_call | solution.py:655
  356.8 53.2 %all_to_all.40.back_ref = bf16[8,512,256]{2,1,0:T(8,128)(2,1)S(1)} all-to-all(bf16[8,512,256]{2,1,0:T(8,128)(2,1)S(1)} %bitcast.16), channel_id=1, replica_groups={{0,1,2,3,4,5,6,7},{8,9,10,11,12,13,14,15},{16,17,18,19,20,21,22,23},{24..., dimensions={0} | all-to-all | bytes 4194304 | tf_op jit(solution)/shard_map/all_to_all | solution.py:926
  410.1 7.7 %project_back.1 = (bf16[512,2048]{1,0:T(8,128)(2,1)S(1)}, bf16[512,48]{1,0:T(8,128)(2,1)S(1)}, bf16[32,16,256]{2,1,0:T(8,128)(2,1)}) custom-call(bf16[8,512,256]{2,1,0:T(8,128)(2,1)S(1)} %all_to_all.40.back_ref, bf16[512,1536]{1,0:T(8,128)(2,1)} %copy-done.6, f32[2,128]{1,0:T(2,128)S(1)} %pad_maximum_fusion.3.refs_2_.head_gain_ref, f32[512,128]{1,0:T(8,128)} %copy-done.7, ...), custom_call_target="tpu_custom_call" | custom-call | tf_op jit(solution)/shard_map/project_back/pallas_call | solution.py:307
  417.8 1.4 copy-done.5
  419.2 7.8 %all-to-all-start.7 = ((bf16[32,16,256]{2,1,0:T(8,128)(2,1)}), bf16[32,16,256]{2,1,0:T(8,128)(2,1)S(1)}, u32[]{:S(2)}, u32[]{:S(2)}) async-start(bf16[32,16,256]{2,1,0:T(8,128)(2,1)} %get-tuple-element.162), calls=%async_computation.7 | async-start | bytes 524288 | tf_op jit(solution)/shard_map/all_to_all | solution.py:937
  426.9 2.1 reduce_grads.3
  429.1 8.2 %input_back.1 = f32[512,1024]{1,0:T(8,128)} custom-call(bf16[512,2048]{1,0:T(8,128)(2,1)} %copy-done.5, bf16[512,48]{1,0:T(8,128)(2,1)S(1)} %get-tuple-element.160.refs_1_, bf16[48,1024]{1,0:T(8,128)(2,1)S(1)} %copy-done.11, bf16[512,1024]{1,0:T(8,128)(2,1)S(1)} %copy-done.1, f32[1,1024]{1,0:T(1,128)S(1)} %bitcast.20, ...), custom_call_target="tpu_custom_call" | custom-call | flops 2147483648 | bytes 10485760 | tf_op jit(solution)/shard_map/input_back/pallas_call | solution.py:348
  437.9 3.4 reduce_grads.2
  (136 shorter events, 12.6 us)
Async XLA Ops:
  0.6 15.1 %copy-start.21 = (bf16[32,2048]{1,0:T(8,128)(2,1)S(1)}, bf16[32,2048]{1,0:T(8,128)(2,1)}, u32[]{:S(2)}) copy-start(bf16[32,2048]{1,0:T(8,128)(2,1)} %param.28) | copy-start | bytes 393220
  2.9 24.3 %collective-permute-start.3 = (bf16[464,1024]{1,0:T(8,128)(2,1)}, bf16[464,1024]{1,0:T(8,128)(2,1)}, u32[]{:S(2)}, u32[]{:S(2)}) collective-permute-start(bf16[464,1024]{1,0:T(8,128)(2,1)} %stack_shard.1.refs_10_), channel_id=1, source_target_pairs={{0,8},{1,9},{2,10},{3,11},{4,12},{5,13},{6,14},{7,15},{8,0},{9,1},... | collective-permute-start | bytes 2850824 | tf_op jit(solution)/shard_map/ppermute | solution.py:96
  5.9 23.6 %collective-permute-start.4 = (bf16[464,1024]{1,0:T(8,128)(2,1)}, bf16[464,1024]{1,0:T(8,128)(2,1)}, u32[]{:S(2)}, u32[]{:S(2)}) collective-permute-start(bf16[464,1024]{1,0:T(8,128)(2,1)} %stack_shard.1.refs_10_), channel_id=1, source_target_pairs={{0,16},{1,17},{2,18},{3,19},{4,20},{5,21},{6,22},{7,23},{8,24},{9,... | collective-permute-start | bytes 2850824 | tf_op jit(solution)/shard_map/ppermute | solution.py:96
  7.4 8.6 %collective-permute-start = (bf16[32,2048]{1,0:T(8,128)(2,1)}, bf16[32,2048]{1,0:T(8,128)(2,1)S(1)}, u32[]{:S(2)}, u32[]{:S(2)}) collective-permute-start(bf16[32,2048]{1,0:T(8,128)(2,1)} %param.28), channel_id=1, source_target_pairs={{0,1},{1,2},{2,3},{3,0},{4,5},{5,6},{6,7},{7,4},{8,9},{9,10},{10,1... | collective-permute-start | bytes 393224 | tf_op jit(solution)/shard_map/ppermute | solution.py:96
  9.0 10.9 %collective-permute-start.1 = (bf16[32,2048]{1,0:T(8,128)(2,1)}, bf16[32,2048]{1,0:T(8,128)(2,1)S(1)}, u32[]{:S(2)}, u32[]{:S(2)}) collective-permute-start(bf16[32,2048]{1,0:T(8,128)(2,1)} %param.28), channel_id=1, source_target_pairs={{0,2},{1,3},{2,0},{3,1},{4,6},{5,7},{6,4},{7,5},{8,10},{9,11},{10,... | collective-permute-start | bytes 393224 | tf_op jit(solution)/shard_map/ppermute | solution.py:96
  11.6 8.4 %collective-permute-start.2 = (bf16[32,2048]{1,0:T(8,128)(2,1)}, bf16[32,2048]{1,0:T(8,128)(2,1)S(1)}, u32[]{:S(2)}, u32[]{:S(2)}) collective-permute-start(bf16[32,2048]{1,0:T(8,128)(2,1)} %param.28), channel_id=1, source_target_pairs={{0,3},{1,0},{2,1},{3,2},{4,7},{5,4},{6,5},{7,6},{8,11},{9,8},{10,9... | collective-permute-start | bytes 393224 | tf_op jit(solution)/shard_map/ppermute | solution.py:96
  20.0 34.5 %all-to-all-start = ((bf16[32,16,256]{2,1,0:T(8,128)(2,1)}), bf16[32,16,256]{2,1,0:T(8,128)(2,1)S(1)}, u32[]{:S(2)}, u32[]{:S(2)}) async-start(bf16[32,16,256]{2,1,0:T(8,128)(2,1)} %pack_adapters.2), calls=%async_computation | async-start | bytes 524288 | tf_op jit(solution)/shard_map/all_to_all | solution.py:937
  24.6 33.6 %copy-start.33 = (f32[64]{0:T(128)S(1)}, f32[64]{0:T(128)}, u32[]{:S(2)}) copy-start(f32[64]{0:T(128)} %param.25) | copy-start | bytes 772
  24.6 33.7 %copy-start.34 = (f32[64]{0:T(128)S(1)}, f32[64]{0:T(128)}, u32[]{:S(2)}) copy-start(f32[64]{0:T(128)} %param.26) | copy-start | bytes 772
  29.5 15.3 %collective-permute-start.5 = (bf16[128,2048]{1,0:T(8,128)(2,1)S(1)}, bf16[128,2048]{1,0:T(8,128)(2,1)S(1)}, u32[]{:S(2)}, u32[]{:S(2)}) collective-permute-start(bf16[128,2048]{1,0:T(8,128)(2,1)S(1)} %pad_maximum_fusion), channel_id=1, source_target_pairs={{0,8},{1,9},{2,10},{3,11},{4,12},{5,13},{6,14},{7,15},{8,0},{9,1},... | collective-permute-start | bytes 1572872 | tf_op jit(solution)/shard_map/ppermute | solution.py:96
  29.7 23.2 %collective-permute-start.6 = (bf16[128,2048]{1,0:T(8,128)(2,1)S(1)}, bf16[128,2048]{1,0:T(8,128)(2,1)S(1)}, u32[]{:S(2)}, u32[]{:S(2)}) collective-permute-start(bf16[128,2048]{1,0:T(8,128)(2,1)S(1)} %pad_maximum_fusion), channel_id=1, source_target_pairs={{0,16},{1,17},{2,18},{3,19},{4,20},{5,21},{6,22},{7,23},{8,24},{9,... | collective-permute-start | bytes 1572872 | tf_op jit(solution)/shard_map/ppermute | solution.py:96
  32.2 22.5 %collective-permute-start.8 = (bf16[464,1024]{1,0:T(8,128)(2,1)}, bf16[464,1024]{1,0:T(8,128)(2,1)}, u32[]{:S(2)}, u32[]{:S(2)}) collective-permute-start(bf16[464,1024]{1,0:T(8,128)(2,1)} %stack_shard.1.refs_10_), channel_id=1, source_target_pairs={{0,1},{1,2},{2,3},{3,0},{4,5},{5,6},{6,7},{7,4},{8,9},{9,10},{10,1... | collective-permute-start | bytes 2850824 | tf_op jit(solution)/shard_map/ppermute | solution.py:96
  34.0 20.4 %collective-permute-start.7 = (bf16[128,2048]{1,0:T(8,128)(2,1)S(1)}, bf16[128,2048]{1,0:T(8,128)(2,1)S(1)}, u32[]{:S(2)}, u32[]{:S(2)}) collective-permute-start(bf16[128,2048]{1,0:T(8,128)(2,1)S(1)} %pad_maximum_fusion), channel_id=1, source_target_pairs={{0,24},{1,25},{2,26},{3,27},{4,28},{5,29},{6,30},{7,31},{8,16},{9,... | collective-permute-start | bytes 1572872 | tf_op jit(solution)/shard_map/ppermute | solution.py:96
  44.8 17.8 %copy-start = (bf16[512,1024]{1,0:T(8,128)(2,1)S(1)}, bf16[512,1024]{1,0:T(8,128)(2,1)}, u32[]{:S(2)}) copy-start(bf16[512,1024]{1,0:T(8,128)(2,1)} %refs_3_.3) | copy-start | bytes 3145732
  44.9 17.8 %copy-start.14 = (f32[1024]{0:T(1024)S(1)}, f32[1024]{0:T(1024)}, u32[]{:S(2)}) copy-start(f32[1024]{0:T(1024)} %param.24) | copy-start | bytes 12292
  54.5 22.6 %copy-start.2 = (bf16[512,2048]{1,0:T(8,128)(2,1)}, bf16[512,2048]{1,0:T(8,128)(2,1)S(1)}, u32[]{:S(2)}) copy-start(bf16[512,2048]{1,0:T(8,128)(2,1)S(1)} %constant_dynamic-update-slice_fusion.refs_7_.refs_6_) | copy-start | bytes 6291460
  54.7 7.9 %collective-permute-start.9 = (bf16[512,2048]{1,0:T(8,128)(2,1)S(1)}, bf16[512,2048]{1,0:T(8,128)(2,1)}, u32[]{:S(2)}, u32[]{:S(2)}) collective-permute-start(bf16[512,2048]{1,0:T(8,128)(2,1)S(1)} %constant_dynamic-update-slice_fusion.refs_7_.refs_6_), channel_id=1, source_target_pairs={{0,4},{1,5},{2,6},{3,7},{4,0},{5,1},{6,2},{7,3},{8,12},{9,13},{10,... | collective-permute-start | bytes 6291464 | tf_op jit(solution)/shard_map/ppermute | solution.py:96
  54.9 25.7 %collective-permute-start.10 = (bf16[464,1024]{1,0:T(8,128)(2,1)}, bf16[464,1024]{1,0:T(8,128)(2,1)}, u32[]{:S(2)}, u32[]{:S(2)}) collective-permute-start(bf16[464,1024]{1,0:T(8,128)(2,1)} %collective-permute-done.8.refs_13_), channel_id=1, source_target_pairs={{0,1},{1,2},{2,3},{3,0},{4,5},{5,6},{6,7},{7,4},{8,9},{9,10},{10,1... | collective-permute-start | bytes 2850824 | tf_op jit(solution)/shard_map/ppermute | solution.py:96
  56.3 24.3 %collective-permute-start.11 = (bf16[464,1024]{1,0:T(8,128)(2,1)}, bf16[464,1024]{1,0:T(8,128)(2,1)}, u32[]{:S(2)}, u32[]{:S(2)}) collective-permute-start(bf16[464,1024]{1,0:T(8,128)(2,1)} %collective-permute-done.8.refs_13_), channel_id=1, source_target_pairs={{0,8},{1,9},{2,10},{3,11},{4,12},{5,13},{6,14},{7,15},{8,0},{9,1},... | collective-permute-start | bytes 2850824 | tf_op jit(solution)/shard_map/ppermute | solution.py:96
  57.1 23.5 %collective-permute-start.12 = (bf16[464,1024]{1,0:T(8,128)(2,1)}, bf16[464,1024]{1,0:T(8,128)(2,1)}, u32[]{:S(2)}, u32[]{:S(2)}) collective-permute-start(bf16[464,1024]{1,0:T(8,128)(2,1)} %collective-permute-done.3.refs_11_), channel_id=1, source_target_pairs={{0,16},{1,17},{2,18},{3,19},{4,20},{5,21},{6,22},{7,23},{8,24},{9,... | collective-permute-start | bytes 2850824 | tf_op jit(solution)/shard_map/ppermute | solution.py:96
  60.6 16.5 %copy-start.7 = (f32[512,128]{1,0:T(8,128)}, f32[512,128]{1,0:T(8,128)S(1)}, u32[]{:S(2)}) copy-start(f32[512,128]{1,0:T(8,128)S(1)} %get-tuple-element.177.refs_3_.cos_ref) | copy-start | bytes 786436
  80.6 32.9 %copy-start.22 = (s32[16384]{0:T(1024)S(1)}, s32[16384]{0:T(1024)}, u32[]{:S(2)}) copy-start(s32[16384]{0:T(1024)} %param.22) | copy-start | bytes 196612
  80.6 73.3 %all-to-all-start.1 = ((bf16[8,512,256]{2,1,0:T(8,128)(2,1)}), bf16[8,512,256]{2,1,0:T(8,128)(2,1)S(1)}, u32[]{:S(2)}, u32[]{:S(2)}) async-start(bf16[8,512,256]{2,1,0:T(8,128)(2,1)} %copy-done.4), calls=%async_computation.1 | async-start | bytes 4194304 | tf_op jit(solution)/shard_map/all_to_all | solution.py:926
  84.9 23.8 %collective-permute-start.13 = (bf16[464,1024]{1,0:T(8,128)(2,1)}, bf16[464,1024]{1,0:T(8,128)(2,1)}, u32[]{:S(2)}, u32[]{:S(2)}) collective-permute-start(bf16[464,1024]{1,0:T(8,128)(2,1)} %collective-permute-done.8.refs_13_), channel_id=1, source_target_pairs={{0,16},{1,17},{2,18},{3,19},{4,20},{5,21},{6,22},{7,23},{8,24},{9,... | collective-permute-start | bytes 2850824 | tf_op jit(solution)/shard_map/ppermute | solution.py:96
  86.0 23.5 %collective-permute-start.14 = (bf16[464,1024]{1,0:T(8,128)(2,1)}, bf16[464,1024]{1,0:T(8,128)(2,1)}, u32[]{:S(2)}, u32[]{:S(2)}) collective-permute-start(bf16[464,1024]{1,0:T(8,128)(2,1)} %collective-permute-done.10.refs_14_), channel_id=1, source_target_pairs={{0,8},{1,9},{2,10},{3,11},{4,12},{5,13},{6,14},{7,15},{8,0},{9,1},... | collective-permute-start | bytes 2850824 | tf_op jit(solution)/shard_map/ppermute | solution.py:96
  86.7 22.8 %collective-permute-start.15 = (bf16[464,1024]{1,0:T(8,128)(2,1)}, bf16[464,1024]{1,0:T(8,128)(2,1)}, u32[]{:S(2)}, u32[]{:S(2)}) collective-permute-start(bf16[464,1024]{1,0:T(8,128)(2,1)} %stack_shard.1.refs_10_), channel_id=1, source_target_pairs={{0,4},{1,5},{2,6},{3,7},{4,0},{5,1},{6,2},{7,3},{8,12},{9,13},{10,... | collective-permute-start | bytes 2850824 | tf_op jit(solution)/shard_map/ppermute | solution.py:96
  109.5 22.7 %collective-permute-start.16 = (bf16[464,1024]{1,0:T(8,128)(2,1)}, bf16[464,1024]{1,0:T(8,128)(2,1)}, u32[]{:S(2)}, u32[]{:S(2)}) collective-permute-start(bf16[464,1024]{1,0:T(8,128)(2,1)} %collective-permute-done.13.refs_18_), channel_id=1, source_target_pairs={{0,8},{1,9},{2,10},{3,11},{4,12},{5,13},{6,14},{7,15},{8,0},{9,1},... | collective-permute-start | bytes 2850824 | tf_op jit(solution)/shard_map/ppermute | solution.py:96
  110.2 22.4 %collective-permute-start.17 = (bf16[464,1024]{1,0:T(8,128)(2,1)}, bf16[464,1024]{1,0:T(8,128)(2,1)}, u32[]{:S(2)}, u32[]{:S(2)}) collective-permute-start(bf16[464,1024]{1,0:T(8,128)(2,1)} %collective-permute-done.10.refs_14_), channel_id=1, source_target_pairs={{0,16},{1,17},{2,18},{3,19},{4,20},{5,21},{6,22},{7,23},{8,24},{9,... | collective-permute-start | bytes 2850824 | tf_op jit(solution)/shard_map/ppermute | solution.py:96
  111.3 21.3 %collective-permute-start.18 = (bf16[464,1024]{1,0:T(8,128)(2,1)}, bf16[464,1024]{1,0:T(8,128)(2,1)}, u32[]{:S(2)}, u32[]{:S(2)}) collective-permute-start(bf16[464,1024]{1,0:T(8,128)(2,1)} %collective-permute-done.8.refs_13_), channel_id=1, source_target_pairs={{0,4},{1,5},{2,6},{3,7},{4,0},{5,1},{6,2},{7,3},{8,12},{9,13},{10,... | collective-permute-start | bytes 2850824 | tf_op jit(solution)/shard_map/ppermute | solution.py:96
  111.3 21.3 %collective-permute-start.19 = (bf16[464,1024]{1,0:T(8,128)(2,1)}, bf16[464,1024]{1,0:T(8,128)(2,1)}, u32[]{:S(2)}, u32[]{:S(2)}) collective-permute-start(bf16[464,1024]{1,0:T(8,128)(2,1)} %collective-permute-done.3.refs_11_), channel_id=1, source_target_pairs={{0,4},{1,5},{2,6},{3,7},{4,0},{5,1},{6,2},{7,3},{8,12},{9,13},{10,... | collective-permute-start | bytes 2850824 | tf_op jit(solution)/shard_map/ppermute | solution.py:96
  111.8 45.0 %collective-permute-start.20 = (bf16[464,1024]{1,0:T(8,128)(2,1)}, bf16[464,1024]{1,0:T(8,128)(2,1)}, u32[]{:S(2)}, u32[]{:S(2)}) collective-permute-start(bf16[464,1024]{1,0:T(8,128)(2,1)} %collective-permute-done.10.refs_14_), channel_id=1, source_target_pairs={{0,1},{1,2},{2,3},{3,0},{4,5},{5,6},{6,7},{7,4},{8,9},{9,10},{10,1... | collective-permute-start | bytes 2850824 | tf_op jit(solution)/shard_map/ppermute | solution.py:96
  153.9 33.2 %copy-start.3 = (bf16[8,512,256]{2,1,0:T(8,128)(2,1)}, bf16[8,512,256]{2,1,0:T(8,128)(2,1)S(1)}, u32[]{:S(2)}) copy-start(bf16[8,512,256]{2,1,0:T(8,128)(2,1)S(1)} %all-to-all-done.1) | copy-start | bytes 6291460
  153.9 39.4 %all-to-all-start.2 = ((bf16[32,16,640]{2,1,0:T(8,128)(2,1)}), bf16[32,16,640]{2,1,0:T(8,128)(2,1)S(1)}, u32[]{:S(2)}, u32[]{:S(2)}) async-start(bf16[32,16,640]{2,1,0:T(8,128)(2,1)} %pack_adapters.3), calls=%async_computation.2 | async-start | bytes 1310720 | tf_op jit(solution)/shard_map/all_to_all | solution.py:937
  156.8 30.3 %collective-permute-start.21 = (bf16[464,1024]{1,0:T(8,128)(2,1)}, bf16[464,1024]{1,0:T(8,128)(2,1)S(1)}, u32[]{:S(2)}, u32[]{:S(2)}) collective-permute-start(bf16[464,1024]{1,0:T(8,128)(2,1)} %collective-permute-done.20.refs_20_), channel_id=1, source_target_pairs={{0,8},{1,9},{2,10},{3,11},{4,12},{5,13},{6,14},{7,15},{8,0},{9,1},... | collective-permute-start | bytes 2850824 | tf_op jit(solution)/shard_map/ppermute | solution.py:96
  158.5 28.8 %collective-permute-start.22 = (bf16[464,1024]{1,0:T(8,128)(2,1)}, bf16[464,1024]{1,0:T(8,128)(2,1)}, u32[]{:S(2)}, u32[]{:S(2)}) collective-permute-start(bf16[464,1024]{1,0:T(8,128)(2,1)} %collective-permute-done.20.refs_20_), channel_id=1, source_target_pairs={{0,16},{1,17},{2,18},{3,19},{4,20},{5,21},{6,22},{7,23},{8,24},{9,... | collective-permute-start | bytes 2850824 | tf_op jit(solution)/shard_map/ppermute | solution.py:96
  160.0 27.3 %collective-permute-start.23 = (bf16[464,1024]{1,0:T(8,128)(2,1)}, bf16[464,1024]{1,0:T(8,128)(2,1)S(1)}, u32[]{:S(2)}, u32[]{:S(2)}) collective-permute-start(bf16[464,1024]{1,0:T(8,128)(2,1)} %collective-permute-done.4.refs_12_), channel_id=1, source_target_pairs={{0,4},{1,5},{2,6},{3,7},{4,0},{5,1},{6,2},{7,3},{8,12},{9,13},{10,... | collective-permute-start | bytes 2850824 | tf_op jit(solution)/shard_map/ppermute | solution.py:96
  160.0 27.3 %collective-permute-start.24 = (bf16[464,1024]{1,0:T(8,128)(2,1)}, bf16[464,1024]{1,0:T(8,128)(2,1)S(1)}, u32[]{:S(2)}, u32[]{:S(2)}) collective-permute-start(bf16[464,1024]{1,0:T(8,128)(2,1)} %collective-permute-done.12.refs_16_), channel_id=1, source_target_pairs={{0,4},{1,5},{2,6},{3,7},{4,0},{5,1},{6,2},{7,3},{8,12},{9,13},{10,... | collective-permute-start | bytes 2850824 | tf_op jit(solution)/shard_map/ppermute | solution.py:96
  160.5 26.8 %collective-permute-start.25 = (bf16[464,1024]{1,0:T(8,128)(2,1)}, bf16[464,1024]{1,0:T(8,128)(2,1)S(1)}, u32[]{:S(2)}, u32[]{:S(2)}) collective-permute-start(bf16[464,1024]{1,0:T(8,128)(2,1)} %collective-permute-done.10.refs_14_), channel_id=1, source_target_pairs={{0,4},{1,5},{2,6},{3,7},{4,0},{5,1},{6,2},{7,3},{8,12},{9,13},{10,... | collective-permute-start | bytes 2850824 | tf_op jit(solution)/shard_map/ppermute | solution.py:96
  187.1 96.6 %copy-start.15 = (f32[16,8,512]{2,1,0:T(8,128)}, f32[16,8,512]{2,1,0:T(8,128)S(1)}, u32[]{:S(2)}) copy-start(f32[16,8,512]{2,1,0:T(8,128)S(1)} %get-tuple-element.133.log_ref) | copy-start | bytes 786436
  187.1 5.9 %copy-start.23 = (bf16[464,1024]{1,0:T(8,128)(2,1)}, bf16[464,1024]{1,0:T(8,128)(2,1)S(1)}, u32[]{:S(2)}) copy-start(bf16[464,1024]{1,0:T(8,128)(2,1)S(1)} %collective-permute-done.21.refs_25_) | copy-start | bytes 2850820
  187.3 5.7 %copy-start.25 = (bf16[464,1024]{1,0:T(8,128)(2,1)}, bf16[464,1024]{1,0:T(8,128)(2,1)S(1)}, u32[]{:S(2)}) copy-start(bf16[464,1024]{1,0:T(8,128)(2,1)S(1)} %collective-permute-done.23.refs_27_) | copy-start | bytes 2850820
  187.3 5.7 %copy-start.26 = (bf16[464,1024]{1,0:T(8,128)(2,1)}, bf16[464,1024]{1,0:T(8,128)(2,1)S(1)}, u32[]{:S(2)}) copy-start(bf16[464,1024]{1,0:T(8,128)(2,1)S(1)} %collective-permute-done.24.refs_28_) | copy-start | bytes 2850820
  187.3 5.7 %copy-start.27 = (bf16[464,1024]{1,0:T(8,128)(2,1)}, bf16[464,1024]{1,0:T(8,128)(2,1)S(1)}, u32[]{:S(2)}) copy-start(bf16[464,1024]{1,0:T(8,128)(2,1)S(1)} %collective-permute-done.25.refs_29_) | copy-start | bytes 2850820
  187.3 23.7 %collective-permute-start.26 = (bf16[464,1024]{1,0:T(8,128)(2,1)}, bf16[464,1024]{1,0:T(8,128)(2,1)}, u32[]{:S(2)}, u32[]{:S(2)}) collective-permute-start(bf16[464,1024]{1,0:T(8,128)(2,1)} %collective-permute-done.22.refs_26_), channel_id=1, source_target_pairs={{0,8},{1,9},{2,10},{3,11},{4,12},{5,13},{6,14},{7,15},{8,0},{9,1},... | collective-permute-start | bytes 2850824 | tf_op jit(solution)/shard_map/ppermute | solution.py:96
  188.4 26.1 %collective-permute-start.27 = (bf16[464,1024]{1,0:T(8,128)(2,1)}, bf16[464,1024]{1,0:T(8,128)(2,1)}, u32[]{:S(2)}, u32[]{:S(2)}) collective-permute-start(bf16[464,1024]{1,0:T(8,128)(2,1)} %collective-permute-done.14.refs_17_), channel_id=1, source_target_pairs={{0,16},{1,17},{2,18},{3,19},{4,20},{5,21},{6,22},{7,23},{8,24},{9,... | collective-permute-start | bytes 2850824 | tf_op jit(solution)/shard_map/ppermute | solution.py:96
  192.5 22.0 %collective-permute-start.28 = (bf16[464,1024]{1,0:T(8,128)(2,1)}, bf16[464,1024]{1,0:T(8,128)(2,1)}, u32[]{:S(2)}, u32[]{:S(2)}) collective-permute-start(bf16[464,1024]{1,0:T(8,128)(2,1)} %collective-permute-done.11.refs_15_), channel_id=1, source_target_pairs={{0,4},{1,5},{2,6},{3,7},{4,0},{5,1},{6,2},{7,3},{8,12},{9,13},{10,... | collective-permute-start | bytes 2850824 | tf_op jit(solution)/shard_map/ppermute | solution.py:96
  192.7 21.8 %collective-permute-start.29 = (bf16[464,1024]{1,0:T(8,128)(2,1)}, bf16[464,1024]{1,0:T(8,128)(2,1)}, u32[]{:S(2)}, u32[]{:S(2)}) collective-permute-start(bf16[464,1024]{1,0:T(8,128)(2,1)} %collective-permute-done.13.refs_18_), channel_id=1, source_target_pairs={{0,4},{1,5},{2,6},{3,7},{4,0},{5,1},{6,2},{7,3},{8,12},{9,13},{10,... | collective-permute-start | bytes 2850824 | tf_op jit(solution)/shard_map/ppermute | solution.py:96
  193.0 21.5 %collective-permute-start.30 = (bf16[464,1024]{1,0:T(8,128)(2,1)}, bf16[464,1024]{1,0:T(8,128)(2,1)}, u32[]{:S(2)}, u32[]{:S(2)}) collective-permute-start(bf16[464,1024]{1,0:T(8,128)(2,1)} %collective-permute-done.14.refs_17_), channel_id=1, source_target_pairs={{0,4},{1,5},{2,6},{3,7},{4,0},{5,1},{6,2},{7,3},{8,12},{9,13},{10,... | collective-permute-start | bytes 2850824 | tf_op jit(solution)/shard_map/ppermute | solution.py:96
  193.3 21.9 %copy-start.24 = (bf16[464,1024]{1,0:T(8,128)(2,1)S(1)}, bf16[464,1024]{1,0:T(8,128)(2,1)}, u32[]{:S(2)}) copy-start(bf16[464,1024]{1,0:T(8,128)(2,1)} %copy-done.23) | copy-start | bytes 2850820
  193.3 31.9 %copy-start.17 = (bf16[32,16,640]{2,1,0:T(8,128)(2,1)}, bf16[32,16,640]{2,1,0:T(8,128)(2,1)S(1)}, u32[]{:S(2)}) copy-start(bf16[32,16,640]{2,1,0:T(8,128)(2,1)S(1)} %all-to-all-done.2.source) | copy-start | bytes 1966084
  193.3 31.4 %all-to-all-start.3 = ((bf16[8,512,128]{2,1,0:T(8,128)(2,1)}), bf16[8,512,128]{2,1,0:T(8,128)(2,1)S(1)}, u32[]{:S(2)}, u32[]{:S(2)}) async-start(bf16[8,512,128]{2,1,0:T(8,128)(2,1)} %bitcast.6), calls=%async_computation.3 | async-start | bytes 2097152 | tf_op jit(solution)/shard_map/all_to_all | solution.py:926
  214.5 2.8 collective-permute-start.31
  214.6 6.8 %collective-permute-start.32 = (bf16[464,1024]{1,0:T(8,128)(2,1)}, bf16[464,1024]{1,0:T(8,128)(2,1)S(1)}, u32[]{:S(2)}, u32[]{:S(2)}) collective-permute-start(bf16[464,1024]{1,0:T(8,128)(2,1)} %collective-permute-done.16.refs_21_), channel_id=1, source_target_pairs={{0,4},{1,5},{2,6},{3,7},{4,0},{5,1},{6,2},{7,3},{8,12},{9,13},{10,... | collective-permute-start | bytes 2850824 | tf_op jit(solution)/shard_map/ppermute | solution.py:96
  215.1 7.7 %collective-permute-start.33 = (bf16[464,1024]{1,0:T(8,128)(2,1)}, bf16[464,1024]{1,0:T(8,128)(2,1)S(1)}, u32[]{:S(2)}, u32[]{:S(2)}) collective-permute-start(bf16[464,1024]{1,0:T(8,128)(2,1)} %collective-permute-done.20.refs_20_), channel_id=1, source_target_pairs={{0,4},{1,5},{2,6},{3,7},{4,0},{5,1},{6,2},{7,3},{8,12},{9,13},{10,... | collective-permute-start | bytes 2850824 | tf_op jit(solution)/shard_map/ppermute | solution.py:96
  215.2 7.6 %collective-permute-start.34 = (bf16[464,1024]{1,0:T(8,128)(2,1)S(1)}, bf16[464,1024]{1,0:T(8,128)(2,1)S(1)}, u32[]{:S(2)}, u32[]{:S(2)}) collective-permute-start(bf16[464,1024]{1,0:T(8,128)(2,1)S(1)} %copy-done.24), channel_id=1, source_target_pairs={{0,4},{1,5},{2,6},{3,7},{4,0},{5,1},{6,2},{7,3},{8,12},{9,13},{10,... | collective-permute-start | bytes 2850824 | tf_op jit(solution)/shard_map/ppermute | solution.py:96
  215.6 9.0 %collective-permute-start.35 = (bf16[464,1024]{1,0:T(8,128)(2,1)}, bf16[464,1024]{1,0:T(8,128)(2,1)}, u32[]{:S(2)}, u32[]{:S(2)}) collective-permute-start(bf16[464,1024]{1,0:T(8,128)(2,1)} %collective-permute-done.22.refs_26_), channel_id=1, source_target_pairs={{0,4},{1,5},{2,6},{3,7},{4,0},{5,1},{6,2},{7,3},{8,12},{9,13},{10,... | collective-permute-start | bytes 2850824 | tf_op jit(solution)/shard_map/ppermute | solution.py:96
  224.6 2.9 collective-permute-start.36
  224.8 4.1 collective-permute-start.37
  283.7 30.9 %all-to-all-start.4 = ((bf16[8,512,128]{2,1,0:T(8,128)(2,1)}), bf16[8,512,128]{2,1,0:T(8,128)(2,1)S(1)}, u32[]{:S(2)}, u32[]{:S(2)}) async-start(bf16[8,512,128]{2,1,0:T(8,128)(2,1)} %get-tuple-element.153), calls=%async_computation.4 | async-start | bytes 2097152 | tf_op jit(solution)/shard_map/all_to_all | solution.py:926
  314.6 42.2 %all-to-all-start.5 = ((bf16[32,16,640]{2,1,0:T(8,128)(2,1)}), bf16[32,16,640]{2,1,0:T(8,128)(2,1)}, u32[]{:S(2)}, u32[]{:S(2)}) async-start(bf16[32,16,640]{2,1,0:T(8,128)(2,1)} %pack_grads.1), calls=%async_computation.5 | async-start | bytes 1310720 | tf_op jit(solution)/shard_map/all_to_all | solution.py:937
  356.8 53.3 %copy-start.1 = (bf16[512,1024]{1,0:T(8,128)(2,1)S(1)}, bf16[512,1024]{1,0:T(8,128)(2,1)}, u32[]{:S(2)}) copy-start(bf16[512,1024]{1,0:T(8,128)(2,1)} %refs_3_.3) | copy-start | bytes 3145732
  356.8 53.3 %copy-start.13 = (bf16[16,2048]{1,0:T(8,128)(2,1)S(1)}, bf16[16,2048]{1,0:T(8,128)(2,1)}, u32[]{:S(2)}) copy-start(bf16[16,2048]{1,0:T(8,128)(2,1)} %get-tuple-element.96.refs_6_.up_ref) | copy-start | bytes 196612
  410.1 19.0 %copy-start.11 = (bf16[48,1024]{1,0:T(8,128)(2,1)S(1)}, bf16[48,1024]{1,0:T(8,128)(2,1)}, u32[]{:S(2)}) copy-start(bf16[48,1024]{1,0:T(8,128)(2,1)} %get-tuple-element.95.refs_5_.refs_2_) | copy-start | bytes 294916
  419.2 18.1 %all-to-all-start.7 = ((bf16[32,16,256]{2,1,0:T(8,128)(2,1)}), bf16[32,16,256]{2,1,0:T(8,128)(2,1)S(1)}, u32[]{:S(2)}, u32[]{:S(2)}) async-start(bf16[32,16,256]{2,1,0:T(8,128)(2,1)} %get-tuple-element.162), calls=%async_computation.7 | async-start | bytes 524288 | tf_op jit(solution)/shard_map/all_to_all | solution.py:937
  (16 other events, 28.3 us)

commit v4 on v3

--- a/solution.py
+++ b/solution.py
@@ -131,9 +131,7 @@
 
 
 def head_means(values, ones):
-    first = values.astype(BF16)
-    second = (values - first.astype(F32)).astype(BF16)
-    return (matmul(first, ones) + matmul(second, ones)) * (1.0 / HEAD_DIM)
+    return matmul(values.astype(BF16), ones) * (1.0 / HEAD_DIM)
 
 
 def head_ones():
@@ -180,7 +178,6 @@
         @pl.when(pl.program_id(0) == 0)
         def _():
             start_loads(pieces, blocks, weight, sem)
-            finish_loads(weight, sem)
 
         inputs = hidden_ref[...].astype(F32)
         normed = (inputs * row_scale(inputs) * gain_ref[...]).astype(BF16)
@@ -189,6 +186,10 @@
         ones = head_ones()
         cos, sin = cos_ref[...], sin_ref[...]
         lanes = lax.broadcasted_iota(jnp.int32, (ROWS, PAIR), 1)
+
+        @pl.when(pl.program_id(0) == 0)
+        def _():
+            finish_loads(weight, sem)
 
         def columns(start, size, group):
             return matmul(normed, weight[:, start : start + size]) + matmul(
@@ -239,7 +240,7 @@
             jax.ShapeDtypeStruct((rows, QW + KW), BF16),
         ],
         scratch_shapes=[pltpu.VMEM((D, width), BF16), pltpu.SemaphoreType.DMA],
-        compiler_params=pltpu.CompilerParams(vmem_limit_bytes=40 << 20),
+        compiler_params=pltpu.CompilerParams(vmem_limit_bytes=60 << 20),
         cost_estimate=pl.CostEstimate(flops=2 * rows * D * width, bytes_accessed=10 << 20, transcendentals=0),
         name="project_heads",
     )(hidden, gain[None, :], head_gain, *tables, down, up, *pieces.blocks)
@@ -318,7 +319,7 @@
             jax.ShapeDtypeStruct((devices, RANK, slab), BF16),
         ],
         scratch_shapes=[pltpu.VMEM((3 * RANK, D), F32), pltpu.VMEM((RANK, width), F32)],
-        compiler_params=pltpu.CompilerParams(vmem_limit_bytes=40 << 20),
+        compiler_params=pltpu.CompilerParams(vmem_limit_bytes=60 << 20),
         name="project_back",
     )(back, in_hbm(kept), head_gain, *[in_hbm(table) for table in tables], hidden, gain[None, :], in_hbm(low), up)
 
@@ -335,10 +336,14 @@
         @pl.when(pl.program_id(0) == 0)
         def _():
             start_loads(pieces, blocks, weight, sem)
-            finish_loads(weight, sem)
 
         inputs = hidden_ref[...].astype(F32)
         scale = row_scale(inputs)
+
+        @pl.when(pl.program_id(0) == 0)
+        def _():
+            finish_loads(weight, sem)
+
         slope = matmul(low_ref[...], down_ref[...]) + contract_cols(grad_ref[...], weight[...])
         slope = slope * gain_ref[...]
         unit = inputs * scale
@@ -355,7 +360,7 @@
         out_specs=row_block(D),
         out_shape=jax.ShapeDtypeStruct((rows, D), F32),
         scratch_shapes=[pltpu.VMEM((D, QW + 2 * KW), BF16), pltpu.SemaphoreType.DMA],
-        compiler_params=pltpu.CompilerParams(vmem_limit_bytes=40 << 20),
+        compiler_params=pltpu.CompilerParams(vmem_limit_bytes=60 << 20),
         cost_estimate=pl.CostEstimate(flops=2 * rows * D * 2048, bytes_accessed=10 << 20, transcendentals=0),
         name="input_back",
     )(in_hbm(grad), low_grad, down, hidden, gain[None, :], in_hbm(middle_grad), *[in_hbm(block) for block in pieces.blocks])
@@ -499,16 +504,14 @@
     return out
 
 
-def stacked_heads(pair, lanes):
+def stacked_heads(pair):
     return jnp.concatenate([pair, pltpu.roll(pair, HEAD_DIM, 1)], axis=0)
 
 
-def allowed(start_row, key_base, query_base, diagonal):
-    keys = key_base + lax.broadcasted_iota(jnp.int32, (BLOCK, BLOCK), 0)
-    inside = keys >= start_row
-    if diagonal:
-        queries = query_base + lax.broadcasted_iota(jnp.int32, (BLOCK, BLOCK), 1)
-        inside = inside & (keys <= queries)
+def allowed(start_row, key_base, query_base):
+    keys = lax.broadcasted_iota(jnp.int32, (BLOCK, BLOCK), 0)
+    last = query_base - key_base + lax.broadcasted_iota(jnp.int32, (1, BLOCK), 1)
+    inside = (keys >= start_row - key_base) & (keys <= last)
     return jnp.concatenate([inside, inside], axis=1)
 
 
@@ -518,176 +521,248 @@
     halo = length - rows
     steps = rows // BLOCK
 
-    def kernel(bound_ref, start_ref, query_ref, keyval_ref, out_ref, log_ref, key_scr, value_scr):
-        step = pl.program_id(0)
-
-        @pl.when(step == 0)
-        def _():
-            lanes = lax.broadcasted_iota(jnp.int32, (length, 128), 1)
-            both = keyval_ref[...].astype(F32)
-            key_scr[...] = jnp.where(lanes < HEAD_DIM, both, 0.0).astype(BF16)
-            values = jnp.where(lanes < HEAD_DIM, pltpu.roll(both, HEAD_DIM, 1), 1.0)
-            value_scr[...] = values.T.astype(BF16)
-
-        lanes = lax.broadcasted_iota(jnp.int32, (BLOCK, 128), 1)
-        pair = query_ref[...].astype(F32)
-        query = stacked_heads(pair, lanes).astype(BF16)
-        start_row = start_ref[...]
-        diagonal = halo // BLOCK + step
-        first = bound_ref[0, step]
-        clear = jnp.minimum(bound_ref[1, step], diagonal)
-
-        def block(index, total, masked, is_diagonal):
-            base = pl.multiple_of(index * BLOCK, BLOCK)
-            scores = contract_cols(key_scr[pl.ds(base, BLOCK), :], query)
-            weights = jnp.exp2(scores)
-            if masked:
-                keep = allowed(start_row, base, diagonal * BLOCK, is_diagonal)
-                weights = jnp.where(keep, weights, 0.0)
-            return total + matmul(value_scr[:, pl.ds(base, BLOCK)], weights.astype(BF16))
-
-        total = jnp.zeros((128, 2 * BLOCK), F32)
-        total = lax.fori_loop(first, clear, lambda i, t: block(i, t, True, False), total)
-        total = lax.fori_loop(clear, diagonal, lambda i, t: block(i, t, False, False), total)
-        total = block(diagonal, total, True, True)
-        norm = total[HEAD_DIM : HEAD_DIM + 1, :]
-        mixed = total[:HEAD_DIM, :] / norm
-        out_ref[...] = jnp.concatenate([mixed[:, :BLOCK], mixed[:, BLOCK:]], axis=0).T.astype(BF16)
-        log_ref[0] = jnp.broadcast_to(jnp.log2(norm), (8, 2 * BLOCK))
-
+    def kernel(bound_ref, start_ref, *refs):
+        arrays, (out_ref, log_ref, key_scr, value_scr) = refs[:-4], refs[-4:]
+        query_ref, keyval_ref = arrays[0], arrays[-1].at[:, column * PAIR : (column + 1) * PAIR]
+        lanes = lax.broadcasted_iota(jnp.int32, (length, 128), 1)
+        both = keyval_ref[...].astype(F32)
+        key_scr[...] = jnp.where(lanes < HEAD_DIM, both, 0.0).astype(BF16)
+        values = jnp.where(lanes < HEAD_DIM, pltpu.roll(both, HEAD_DIM, 1), 1.0)
+        value_scr[...] = values.T.astype(BF16)
+
+        def one_step(step, carry):
+            own = pl.ds(pl.multiple_of(step * BLOCK, BLOCK), BLOCK)
+            query = stacked_heads(query_ref[own, :PAIR].astype(F32)).astype(BF16)
+            start_row = start_ref[:, own]
+            diagonal = halo // BLOCK + step
+            count = diagonal - bound_ref[0, step] + 1
+
+            def block(index):
+                base = pl.multiple_of(jnp.maximum(index, 0) * BLOCK, BLOCK)
+                scores = contract_cols(key_scr[pl.ds(base, BLOCK), :], query)
+                keep = allowed(start_row, index * BLOCK, diagonal * BLOCK)
+                weights = jnp.where(keep, jnp.exp2(scores), 0.0).astype(BF16)
+                return matmul(value_scr[:, pl.ds(base, BLOCK)], weights)
+
+            def pair_of_blocks(turn, total):
+                index = diagonal - 2 * turn
+                return total + (block(index) + block(index - 1))
+
+            total = lax.fori_loop(0, (count + 1) // 2, pair_of_blocks, jnp.zeros((128, 2 * BLOCK), F32))
+            norm = total[HEAD_DIM : HEAD_DIM + 1, :]
+            mixed = total[:HEAD_DIM, :] / norm
+            out_ref[own, :] = jnp.concatenate([mixed[:, :BLOCK], mixed[:, BLOCK:]], axis=0).T.astype(BF16)
+            log_ref[step] = jnp.broadcast_to(jnp.log2(norm), (8, 2 * BLOCK))
+            return carry
+
+        lax.fori_loop(0, steps, one_step, 0)
+
+    arrays = [queries, keyvals] if halo else [queries]
     return pl.pallas_call(
         kernel,
-        grid_spec=pltpu.PrefetchScalarGridSpec(
-            num_scalar_prefetch=1,
-            grid=(steps,),
-            in_specs=[
-                pl.BlockSpec((1, BLOCK), lambda i, b: (0, i)),
-                pl.BlockSpec((BLOCK, 128), lambda i, b: (i, 0)),
-                pl.BlockSpec((length, 128), lambda i, b: (0, column)),
-            ],
-            out_specs=[
-                pl.BlockSpec((BLOCK, 128), lambda i, b: (i, 0)),
-                pl.BlockSpec((1, 8, 2 * BLOCK), lambda i, b: (i, 0, 0)),
-            ],
-            scratch_shapes=[pltpu.VMEM((length, 128), BF16), pltpu.VMEM((128, length), BF16)],
-        ),
+        in_specs=[SMEM_SPEC] + [VMEM_SPEC] * (1 + len(arrays)),
+        out_specs=[VMEM_SPEC] * 2,
         out_shape=[
             jax.ShapeDtypeStruct((rows, 128), BF16),
             jax.ShapeDtypeStruct((steps, 8, 2 * BLOCK), F32),
         ],
+        scratch_shapes=[pltpu.VMEM((length, 128), BF16), pltpu.VMEM((128, length), BF16)],
         compiler_params=pltpu.CompilerParams(vmem_limit_bytes=40 << 20),
         cost_estimate=pl.CostEstimate(
             flops=4 * rows * 1024 * 256 * 2, bytes_accessed=4 * rows * 256, transcendentals=rows * 2048
         ),
         name="forward_attention",
-    )(bounds, starts, queries, keyvals)
-
-
-def backward_attention(bounds, starts, queries, keyvals, column, mixed, logs, grads):
+    )(bounds, starts, *arrays)
+
+
+TURNS = (SEGMAX // BLOCK + 2) // 2
+
+
+def probabilities(bounds, starts, queries, keyvals, column, logs):
     rows = queries.shape[0]
     length = keyvals.shape[0]
     halo = length - rows
     steps = rows // BLOCK
 
-    def kernel(bound_ref, start_ref, query_ref, keyval_ref, mixed_ref, log_ref, grad_ref, *refs):
-        outs, (key_scr, value_scr, turned_scr, key_sum, value_sum) = refs[:-5], refs[-5:]
-        step = pl.program_id(0)
-
-        @pl.when(step == 0)
-        def _():
-            lanes = lax.broadcasted_iota(jnp.int32, (length, 128), 1)
-            both = keyval_ref[...].astype(F32)
-            ones = jnp.where(lanes < HEAD_DIM + 3, 1.0, 0.0)
-            keys = jnp.where(lanes < HEAD_DIM, both, ones)
-            key_scr[...] = keys.astype(BF16)
-            value_scr[...] = jnp.where(lanes < HEAD_DIM, pltpu.roll(both, HEAD_DIM, 1), ones).astype(BF16)
-            turned_scr[...] = keys.T.astype(BF16)
-            key_sum[...] = jnp.zeros_like(key_sum)
-            value_sum[...] = jnp.zeros_like(value_sum)
-
-        lanes = lax.broadcasted_iota(jnp.int32, (2 * BLOCK, 128), 1)
-        query = stacked_heads(query_ref[...].astype(F32), lanes)
-        grad = stacked_heads(grad_ref[...].astype(F32), lanes)
-        weighed = stacked_heads(mixed_ref[...].astype(F32), lanes)
-        inner = jnp.sum(jnp.where(lanes < HEAD_DIM, grad * weighed, 0.0), axis=1, keepdims=True)
-        log_column = log_ref[0].T[:, :1]
-        query_low = with_columns(query, [part.astype(F32) for part in split_three(-log_column)], lanes).astype(BF16)
-        grad_low = with_columns(grad, [part.astype(F32) for part in split_three(-inner)], lanes).astype(BF16)
-        start_row = start_ref[...]
-        diagonal = halo // BLOCK + step
-        first = bound_ref[0, step]
-        clear = jnp.minimum(bound_ref[1, step], diagonal)
-
-        def block(index, total, masked, is_diagonal):
-            base = pl.multiple_of(index * BLOCK, BLOCK)
-            where = pl.ds(base, BLOCK)
-            weights = jnp.exp2(contract_cols(key_scr[where, :], query_low))
-            if masked:
-                keep = allowed(start_row, base, diagonal * BLOCK, is_diagonal)
-                weights = jnp.where(keep, weights, 0.0)
-            slopes = (weights * contract_cols(value_scr[where, :], grad_low)).astype(BF16)
-            value_sum[where, :] += matmul(weights.astype(BF16), grad_low)
-            key_sum[where, :] += matmul(slopes, query_low)
-            return total + matmul(turned_scr[:, where], slopes)
-
-        total = jnp.zeros((128, 2 * BLOCK), F32)
-        total = lax.fori_loop(first, clear, lambda i, t: block(i, t, True, False), total)
-        total = lax.fori_loop(clear, diagonal, lambda i, t: block(i, t, False, False), total)
-        total = block(diagonal, total, True, True)
-        total = total[:HEAD_DIM] * HEAD_DIM**-0.5
-        query_grad = jnp.concatenate([total[:, :BLOCK], total[:, BLOCK:]], axis=0).T.astype(BF16)
-        if halo:
-            outs[0][...] = query_grad
-        else:
-            outs[0][pl.ds(pl.multiple_of(step * BLOCK, BLOCK), BLOCK), :PAIR] = query_grad
-
-        @pl.when(step == steps - 1)
-        def _():
-            whole = lax.broadcasted_iota(jnp.int32, (length, 128), 1)
-            keyval_grad = jnp.where(
-                whole < HEAD_DIM, key_sum[...] * (1.0 / LOG2E), pltpu.roll(value_sum[...], HEAD_DIM, 1)
-            )
-            if halo:
-                outs[1][...] = keyval_grad
-            else:
-                outs[0][:, PAIR:] = keyval_grad.astype(BF16)
-
+    def kernel(bound_ref, start_ref, log_ref, *refs):
+        arrays, (out_ref, key_scr, buffer, sems) = refs[:-4], refs[-4:]
+        query_ref, keyval_ref = arrays[0], arrays[-1].at[:, column * PAIR : (column + 1) * PAIR]
+        whole = lax.broadcasted_iota(jnp.int32, (length, 128), 1)
+        ones = jnp.where(whole < HEAD_DIM + 3, 1.0, 0.0)
+        key_scr[...] = jnp.where(whole < HEAD_DIM, keyval_ref[...].astype(F32), ones).astype(BF16)
+
+        def turns(step):
+            return (halo // BLOCK + step - bound_ref[0, step] + 2) // 2
+
+        def stored(slot, step, turn):
+            blocks = pl.ds(2 * turn, 2)
+            return pltpu.make_async_copy(buffer.at[slot, blocks], out_ref.at[step, blocks], sems.at[slot])
+
+        def finish(step):
+            def wait(turn, carry):
+                stored(lax.rem(step, 2), step, turn).wait()
+                return carry
+
+            lax.fori_loop(0, turns(step), wait, 0)
+
+        def one_step(step, carry):
+            @pl.when(step >= 2)
+            def _():
+                finish(step - 2)
+
+            slot = lax.rem(step, 2)
+            own = pl.ds(pl.multiple_of(step * BLOCK, BLOCK), BLOCK)
+            lanes = lax.broadcasted_iota(jnp.int32, (2 * BLOCK, 128), 1)
+            query = stacked_heads(query_ref[own, :PAIR].astype(F32))
+            log_column = log_ref[step].T[:, :1]
+            query_low = with_columns(query, [part.astype(F32) for part in split_three(-log_column)], lanes).astype(BF16)
+            start_row = start_ref[:, own]
+            diagonal = halo // BLOCK + step
+
+            def block(index):
+                where = pl.ds(pl.multiple_of(jnp.maximum(index, 0) * BLOCK, BLOCK), BLOCK)
+                weights = jnp.exp2(contract_cols(key_scr[where, :], query_low))
+                keep = allowed(start_row, index * BLOCK, diagonal * BLOCK)
+                return jnp.where(keep, weights, 0.0).astype(BF16)
+
+            def pair_of_blocks(turn, carry):
+                index = diagonal - 2 * turn
+                found = [block(index), block(index - 1)]
+                buffer[slot, 2 * turn] = found[0]
+                buffer[slot, 2 * turn + 1] = found[1]
+                stored(slot, step, turn).start()
+                return carry
+
+            lax.fori_loop(0, turns(step), pair_of_blocks, 0)
+            return carry
+
+        lax.fori_loop(0, steps, one_step, 0)
+        finish(steps - 2)
+        finish(steps - 1)
+
+    arrays = [queries, keyvals] if halo else [queries]
     return pl.pallas_call(
         kernel,
-        grid_spec=pltpu.PrefetchScalarGridSpec(
-            num_scalar_prefetch=1,
-            grid=(steps,),
-            in_specs=[
-                pl.BlockSpec((1, BLOCK), lambda i, b: (0, i)),
-                pl.BlockSpec((BLOCK, 128), lambda i, b: (i, 0)),
-                pl.BlockSpec((length, 128), lambda i, b: (0, column)),
-                pl.BlockSpec((BLOCK, 128), lambda i, b: (i, 0)),
-                pl.BlockSpec((1, 8, 2 * BLOCK), lambda i, b: (i, 0, 0)),
-                pl.BlockSpec((BLOCK, 128), lambda i, b: (i, 0)),
-            ],
-            out_specs=[
-                pl.BlockSpec((BLOCK, 128), lambda i, b: (i, 0)),
-                pl.BlockSpec((length, 128), lambda i, b: (0, 0)),
-            ]
-            if halo
-            else [pl.BlockSpec((rows, 2 * PAIR), lambda i, b: (0, 0))],
-            scratch_shapes=[
-                pltpu.VMEM((length, 128), BF16),
-                pltpu.VMEM((length, 128), BF16),
-                pltpu.VMEM((128, length), BF16),
-                pltpu.VMEM((length, 128), F32),
-                pltpu.VMEM((length, 128), F32),
-            ],
+        in_specs=[SMEM_SPEC] + [VMEM_SPEC] * (2 + len(arrays)),
+        out_specs=ANY_SPEC,
+        out_shape=jax.ShapeDtypeStruct((steps, 2 * TURNS, BLOCK, 2 * BLOCK), BF16),
+        scratch_shapes=[
+            pltpu.VMEM((length, 128), BF16),
+            pltpu.VMEM((2, 2 * TURNS, BLOCK, 2 * BLOCK), BF16),
+            pltpu.SemaphoreType.DMA((2,)),
+        ],
+        compiler_params=pltpu.CompilerParams(vmem_limit_bytes=40 << 20),
+        cost_estimate=pl.CostEstimate(
+            flops=4 * rows * 1024 * 256, bytes_accessed=20 << 20, transcendentals=rows * 2048
         ),
+        name="probabilities",
+    )(bounds, starts, logs, *arrays)
+
+
+def backward_attention(bounds, queries, keyvals, column, mixed, probs, grads):
+    rows = queries.shape[0]
+    length = keyvals.shape[0]
+    halo = length - rows
+    steps = rows // BLOCK
+
+    def kernel(bound_ref, *refs):
+        arrays, refs = refs[: 2 if halo else 1], refs[2 if halo else 1 :]
+        mixed_ref, grad_ref, probs_ref = refs[:3]
+        outs, (value_scr, turned_scr, key_sum, value_sum, buffer, sems) = refs[3:-6], refs[-6:]
+        query_ref, keyval_ref = arrays[0], arrays[-1].at[:, column * PAIR : (column + 1) * PAIR]
+
+        def turns(step):
+            return (halo // BLOCK + step - bound_ref[0, step] + 2) // 2
+
+        def loaded(step, turn):
+            slot, blocks = lax.rem(step, 2), pl.ds(2 * turn, 2)
+            return pltpu.make_async_copy(probs_ref.at[step, blocks], buffer.at[slot, blocks], sems.at[slot])
+
+        def begin(step):
+            def start(turn, carry):
+                loaded(step, turn).start()
+                return carry
+
+            lax.fori_loop(0, turns(step), start, 0)
+
+        begin(0)
+        whole = lax.broadcasted_iota(jnp.int32, (length, 128), 1)
+        both = keyval_ref[...].astype(F32)
+        ones = jnp.where(whole < HEAD_DIM + 3, 1.0, 0.0)
+        value_scr[...] = jnp.where(whole < HEAD_DIM, pltpu.roll(both, HEAD_DIM, 1), ones).astype(BF16)
+        turned_scr[...] = both.T.astype(BF16)
+        key_sum[...] = jnp.zeros_like(key_sum)
+        value_sum[...] = jnp.zeros_like(value_sum)
+
+        def one_step(step, carry):
+            @pl.when(step + 1 < steps)
+            def _():
+                begin(step + 1)
+
+            slot = lax.rem(step, 2)
+            own = pl.ds(pl.multiple_of(step * BLOCK, BLOCK), BLOCK)
+            lanes = lax.broadcasted_iota(jnp.int32, (2 * BLOCK, 128), 1)
+            query_low = stacked_heads(query_ref[own, :PAIR].astype(F32)).astype(BF16)
+            grad = stacked_heads(grad_ref[own, :].astype(F32))
+            weighed = stacked_heads(mixed_ref[own, :].astype(F32))
+            inner = jnp.sum(jnp.where(lanes < HEAD_DIM, grad * weighed, 0.0), axis=1, keepdims=True)
+            grad_low = with_columns(grad, [part.astype(F32) for part in split_three(-inner)], lanes).astype(BF16)
+            diagonal = halo // BLOCK + step
+
+            def wait(turn, carry):
+                loaded(step, turn).wait()
+                return carry
+
+            lax.fori_loop(0, turns(step), wait, 0)
+
+            def block(index, weights):
+                where = pl.ds(pl.multiple_of(jnp.maximum(index, 0) * BLOCK, BLOCK), BLOCK)
+                slopes = (weights.astype(F32) * contract_cols(value_scr[where, :], grad_low)).astype(BF16)
+                value_part = matmul(weights, grad_low)
+                return where, value_part, matmul(slopes, query_low), matmul(turned_scr[:, where], slopes)
+
+            def pair_of_blocks(turn, total):
+                index = diagonal - 2 * turn
+                parts = [block(index, buffer[slot, 2 * turn]), block(index - 1, buffer[slot, 2 * turn + 1])]
+                for where, value_part, key_part, _ in parts:
+                    value_sum[where, :] += value_part
+                    key_sum[where, :] += key_part
+                return total + (parts[0][3] + parts[1][3])
+
+            total = lax.fori_loop(0, turns(step), pair_of_blocks, jnp.zeros((128, 2 * BLOCK), F32))
+            total = total[:HEAD_DIM] * HEAD_DIM**-0.5
+            outs[0][own, :PAIR] = jnp.concatenate([total[:, :BLOCK], total[:, BLOCK:]], axis=0).T.astype(BF16)
+            return carry
+
+        lax.fori_loop(0, steps, one_step, 0)
+        keyval_grad = jnp.where(whole < HEAD_DIM, key_sum[...] * (1.0 / LOG2E), pltpu.roll(value_sum[...], HEAD_DIM, 1))
+        if halo:
+            outs[1][...] = keyval_grad
+        else:
+            outs[0][:, PAIR:] = keyval_grad.astype(BF16)
+
+    arrays = [queries, keyvals] if halo else [queries]
+    return pl.pallas_call(
+        kernel,
+        in_specs=[SMEM_SPEC] + [VMEM_SPEC] * (2 + len(arrays)) + [ANY_SPEC],
+        out_specs=[VMEM_SPEC] * (2 if halo else 1),
         out_shape=[jax.ShapeDtypeStruct((rows, 128), BF16), jax.ShapeDtypeStruct((length, 128), F32)]
         if halo
         else [jax.ShapeDtypeStruct((rows, 2 * PAIR), BF16)],
-        compiler_params=pltpu.CompilerParams(vmem_limit_bytes=48 << 20),
+        scratch_shapes=[
+            pltpu.VMEM((length, 128), BF16),
+            pltpu.VMEM((128, length), BF16),
+            pltpu.VMEM((length, 128), F32),
+            pltpu.VMEM((length, 128), F32),
+            pltpu.VMEM((2, 2 * TURNS, BLOCK, 2 * BLOCK), BF16),
+            pltpu.SemaphoreType.DMA((2,)),
+        ],
+        compiler_params=pltpu.CompilerParams(vmem_limit_bytes=40 << 20),
         cost_estimate=pl.CostEstimate(
-            flops=10 * rows * 1024 * 256 * 2, bytes_accessed=8 * rows * 256, transcendentals=rows * 2048
+            flops=8 * rows * 1024 * 256 * 2, bytes_accessed=20 << 20, transcendentals=0
         ),
         name="backward_attention",
-    )(bounds, starts, queries, keyvals, mixed, logs, grads)
+    )(bounds, *arrays, mixed, grads, probs)
 
 
 def document_bounds(segment_ids, origin, halo, span, seq_start):
@@ -1003,6 +1078,7 @@
     mixed_then = lax.optimization_barrier((mixed, slabs))[0]
     mixture_tok = swap(mixed_then.reshape(members, rows, PAIR))
     if spread:
+        pending.append(chosen[-1])
         move(*cores((5, 2), (7, 1), (1, 3), (3, 3), (5, 3)))
         pending.append(mixture_tok)
         move(*cores((7, 2), (7, 3)))
@@ -1011,9 +1087,11 @@
         mixture_tok, hidden, cotangent, ffn_gain, weights, chosen[2:]
     )
     grad_rows = swap(mixture_grad).reshape(span, PAIR)
+    logs_then = lax.optimization_barrier((logs, mixture_grad))[0]
+    probs = probabilities(bounds, starts, queries, keyvals, column, logs_then)
     early_packed, grad_rows = lax.optimization_barrier((pack_grads(early, devices), grad_rows))
     early_slabs = exchange(early_packed)
-    back = backward_attention(bounds, starts, queries, keyvals, column, mixed, logs, grad_rows)
+    back = backward_attention(bounds, queries, keyvals, column, mixed, probs, grad_rows)
     if halo:
         query_grads, keyval_grads = back
         returned = shifted(keyval_grads[:halo].astype(BF16), -members).astype(F32)

time: 441 us -> 426 us (0.966)
  waiting for transfers between devices: 137 us -> 123 us
  starting transfers between devices: 69.6 us -> 59.2 us
  Pallas kernels: 166 us -> 176 us
  local copies, waits for them, and re-layouts: 11.4 us -> 6.92 us
    all_to_all x3, waiting for transfers between devices: 44.8 us -> 26.1 us  [swap(): lax.all_to_all(value, AXES, 0, 0, axis_index_groups=groups, tiled=True)]
    pallas_call x2 -> x3, Pallas kernels: 63.9 us -> 74.4 us  [the longest x1 31.4 us: backward_attention(): pl.pallas_call(kernel, in_specs=[SMEM_SPEC] + [VMEM_SPEC] * (2 + len(arra...]
    all_to_all x4, starting transfers between devices: 18.8 us -> 13.4 us  [exchange(): return lax.all_to_all(packed, AXES, 0, 0, tiled=True)]
    ppermute x38, waiting for transfers between devices: 92.2 us -> 97 us  [hop(): return lax.ppermute(value, AXES, pairs)]
    unnamed x76 -> x44, local copies, waits for them, and re-layouts: 11 us -> 6.51 us
  transfers between devices with their start and end apart: 45 -> 45, of which waited for: 23 -> 27; matrix products, arithmetic and copies ran while one was open for 1% -> 2% of each run, Pallas kernels for 22% -> 26%
where the time goes in v4:
time: 426 us; the launch traced here: 424 us
  Pallas kernels  176 us (41%)
  waiting for transfers between devices  123 us (29%)
  starting transfers between devices  59.2 us (14%)
  blocking collectives  53.6 us (13%)
  local copies, waits for them, and re-layouts  6.92 us (2%)
  other arithmetic  4.3 us (1%)
    ppermute x38, waiting for transfers between devices, hop(): return lax.ppermute(value, AXES, pairs)  97 us
    pallas_call x1, Pallas kernels, feed_forward(): pl.pallas_call(kernel, in_specs=[VMEM_SPEC] * 10 + [ANY_SPEC] * count, ou...  54.4 us
    all_to_all x1, blocking collectives, swap(): lax.all_to_all(value, AXES, 0, 0, axis_index_groups=groups, tiled=True)  53.6 us
    ppermute x38, starting transfers between devices, hop(): return lax.ppermute(value, AXES, pairs)  33.2 us
    pallas_call x1, Pallas kernels, backward_attention(): pl.pallas_call(kernel, in_specs=[SMEM_SPEC] + [VMEM_SPEC] * (2 + len(arra...  31.4 us
    all_to_all x3, waiting for transfers between devices, swap(): lax.all_to_all(value, AXES, 0, 0, axis_index_groups=groups, tiled=True)  26.1 us
    pallas_call x1, Pallas kernels, forward_attention(): pl.pallas_call(kernel, in_specs=[SMEM_SPEC] + [VMEM_SPEC] * (1 + len(arra...  24.5 us
    pallas_call x1, Pallas kernels, probabilities(): pl.pallas_call(kernel, in_specs=[SMEM_SPEC] + [VMEM_SPEC] * (2 + len(arra...  18.5 us
  transfers between devices with their start and end apart: 45, of which 27 were waited for; matrix products, arithmetic and copies ran while one was open for 2% of the time, Pallas kernels for 26%

profile of v4, /device:TPU:0, one launch (start us, length us, event | category | flops | bytes accessed | tf_op | source)
XLA Modules:
  0.0 424.0 jit_solution(8357587225376497276)
XLA Ops:
  0.7 2.2 stack_shard.1.refs_10_
  2.9 2.9 collective-permute-start.3
  5.8 1.5 collective-permute-start.4
  7.3 1.6 collective-permute-start
  8.9 2.6 collective-permute-start.1
  11.5 1.3 collective-permute-start.2
  12.9 2.8 pack_adapters.2
  16.0 3.8 collective-permute-done.1
  20.6 4.6 %all-to-all-start = ((bf16[32,16,256]{2,1,0:T(8,128)(2,1)}), bf16[32,16,256]{2,1,0:T(8,128)(2,1)S(1)}, u32[]{:S(2)}, u32[]{:S(2)}) async-start(bf16[32,16,256]{2,1,0:T(8,128)(2,1)} %pack_adapters.2), calls=%async_computation | async-start | bytes 524288 | tf_op jit(solution)/shard_map/all_to_all | solution.py:1012
  25.2 1.1 pad_maximum_fusion
  26.3 0.9 collective-permute-done.3.refs_11_
  27.3 1.6 collective-permute-done.4.refs_12_
  30.2 2.2 collective-permute-start.6
  32.4 1.8 collective-permute-start.8
  35.1 1.6 collective-permute-start.7
  37.6 6.9 %collective-permute-done.5 = bf16[128,2048]{1,0:T(8,128)(2,1)S(1)} collective-permute-done((bf16[128,2048]{1,0:T(8,128)(2,1)S(1)}, bf16[128,2048]{1,0:T(8,128)(2,1)S(1)}, u32[]{:S(2)}, u32[]{:S(2)}) %collective-permute-start.5) | collective-permute-done | bytes 524320 | tf_op jit(solution)/shard_map/ppermute | solution.py:96
  44.5 10.6 %collective-permute-done.6 = bf16[128,2048]{1,0:T(8,128)(2,1)S(1)} collective-permute-done((bf16[128,2048]{1,0:T(8,128)(2,1)S(1)}, bf16[128,2048]{1,0:T(8,128)(2,1)S(1)}, u32[]{:S(2)}, u32[]{:S(2)}) %collective-permute-start.6) | collective-permute-done | bytes 524320 | tf_op jit(solution)/shard_map/ppermute | solution.py:96
  55.6 1.1 collective-permute-start.10
  56.8 1.2 collective-permute-start.11
  57.9 1.0 collective-permute-start.12
  59.7 1.0 fusion
  60.7 1.3 pad_maximum_fusion.1
  62.0 1.9 unpack_adapters.2
  63.9 11.1 %project_heads.1 = (bf16[8,512,256]{2,1,0:T(8,128)(2,1)}, bf16[512,48]{1,0:T(8,128)(2,1)}, bf16[512,1536]{1,0:T(8,128)(2,1)}) custom-call(bf16[512,1024]{1,0:T(8,128)(2,1)} %refs_3_.3, f32[1,1024]{1,0:T(1,128)} %bitcast.20, f32[2,128]{1,0:T(2,128)} %pad_maximum_fusion.3.refs_2_.head_gain_ref, f32[512,128]{1,0:T(8,128)} %get-tuple-element.179.refs_3_.cos_ref, ...), custom_call_target="tpu_custom_call" | custom-call | flops 2147483648 | bytes 10485760 | tf_op jit(solution)/shard_map/project_heads/pallas_call | solution.py:226
  74.9 5.9 %collective-permute-done.10.refs_14_ = bf16[464,1024]{1,0:T(8,128)(2,1)} collective-permute-done((bf16[464,1024]{1,0:T(8,128)(2,1)}, bf16[464,1024]{1,0:T(8,128)(2,1)}, u32[]{:S(2)}, u32[]{:S(2)}) %collective-permute-start.10) | collective-permute-done | bytes 950304 | tf_op jit(solution)/shard_map/ppermute | solution.py:96
  81.1 4.0 all-to-all-start.1
  85.1 1.1 collective-permute-start.13
  86.2 1.0 collective-permute-start.14
  87.2 21.7 %collective-permute-done.13.refs_18_ = bf16[464,1024]{1,0:T(8,128)(2,1)} collective-permute-done((bf16[464,1024]{1,0:T(8,128)(2,1)}, bf16[464,1024]{1,0:T(8,128)(2,1)}, u32[]{:S(2)}, u32[]{:S(2)}) %collective-permute-start.13) | collective-permute-done | bytes 950304 | tf_op jit(solution)/shard_map/ppermute | solution.py:96
  109.7 0.9 copy-done.10
  112.9 1.7 collective-permute-start.20
  114.9 2.7 pack_adapters.3
  117.6 15.6 %collective-permute-done.16.refs_21_ = bf16[464,1024]{1,0:T(8,128)(2,1)S(1)} collective-permute-done((bf16[464,1024]{1,0:T(8,128)(2,1)}, bf16[464,1024]{1,0:T(8,128)(2,1)S(1)}, u32[]{:S(2)}, u32[]{:S(2)}) %collective-permute-start.16) | collective-permute-done | bytes 950304 | tf_op jit(solution)/shard_map/ppermute | solution.py:96
  133.9 20.1 %all-to-all-done.1 = bf16[8,512,256]{2,1,0:T(8,128)(2,1)S(1)} async-done(((bf16[8,512,256]{2,1,0:T(8,128)(2,1)}), bf16[8,512,256]{2,1,0:T(8,128)(2,1)S(1)}, u32[]{:S(2)}, u32[]{:S(2)}) %all-to-all-start.1) | async-done | bytes 2097184 | tf_op jit(solution)/shard_map/all_to_all | solution.py:1001
  154.0 2.6 all-to-all-start.2
  156.9 1.7 collective-permute-start.21
  158.6 1.5 collective-permute-start.22
  160.6 24.5 %forward_attention.1 = (bf16[4096,128]{1,0:T(8,128)(2,1)}, f32[16,8,512]{2,1,0:T(8,128)S(1)}) custom-call(s32[2,16]{1,0:T(2,128)S(1)} %pad_add_fusion.bound_ref, s32[1,4096]{1,0:T(1,128)S(1)} %bitcast.17, bf16[4096,256]{1,0:T(8,128)(2,1)S(1)} %bitcast.12), custom_call_target="tpu_custom_call" | custom-call | flops 8589934592 | bytes 4194304 | tf_op jit(solution)/shard_map/forward_attention/pallas_call | solution.py:561
  185.1 1.7 collective-permute-done.21.refs_25_
  187.4 1.1 collective-permute-start.26
  189.6 4.9 %all-to-all-start.3 = ((bf16[8,512,128]{2,1,0:T(8,128)(2,1)}), bf16[8,512,128]{2,1,0:T(8,128)(2,1)}, u32[]{:S(2)}, u32[]{:S(2)}) async-start(bf16[8,512,128]{2,1,0:T(8,128)(2,1)} %bitcast.6), calls=%async_computation.3 | async-start | bytes 2097152 | tf_op jit(solution)/shard_map/all_to_all | solution.py:1001
  194.5 2.3 unpack_adapters.3
  196.8 14.0 %collective-permute-done.26.refs_30_ = bf16[464,1024]{1,0:T(8,128)(2,1)} collective-permute-done((bf16[464,1024]{1,0:T(8,128)(2,1)}, bf16[464,1024]{1,0:T(8,128)(2,1)}, u32[]{:S(2)}, u32[]{:S(2)}) %collective-permute-start.26) | collective-permute-done | bytes 950304 | tf_op jit(solution)/shard_map/ppermute | solution.py:96
  212.5 2.2 collective-permute-done.31.refs_35_
  215.7 1.4 collective-permute-done.33.refs_37_
  217.0 1.4 collective-permute-done.34.refs_38_
  218.4 1.4 collective-permute-done.35.refs_39_
  219.7 1.0 all-to-all-done.3.refs_0_
  221.2 2.4 collective-permute-done.36.refs_40_
  223.6 1.4 collective-permute-done.37.refs_41_
  224.9 54.4 %feed_forward.1 = (bf16[512,1024]{1,0:T(8,128)(2,1)}, f32[512,1024]{1,0:T(8,128)}, bf16[8,512,128]{2,1,0:T(8,128)(2,1)}, f32[16,1024]{1,0:T(8,128)}, f32[16,1024...) custom-call(bf16[8,512,128]{2,1,0:T(8,128)(2,1)} %all-to-all-done.3.refs_0_, ...), custom_call_target="tpu_custom_call" | custom-call | flops 31138512896 | bytes 36700160 | tf_op jit(solution)/shard_map/feed_forward/pallas_call | solution.py:949
  279.3 3.7 all-to-all-start.4
  283.0 2.6 pack_grads.1
  285.6 18.5 %probabilities.1.refs_3_ = bf16[16,10,256,512]{3,2,1,0:T(8,128)(2,1)} custom-call(s32[2,16]{1,0:T(2,128)S(1)} %pad_add_fusion.bound_ref, s32[1,4096]{1,0:T(1,128)S(1)} %bitcast.18, f32[16,8,512]{2,1,0:T(8,128)S(1)} %get-tuple-element.156.log_ref, bf16[4096,256]{1,0:T(8,128)(2,1)S(1)} %bitcast.13), custom_call_target="tpu_custom_call" | custom-call | flops 4294967296 | bytes 20971520 | tf_op jit(solution)/shard_map/probabilities/pallas_call | solution.py:644
  304.1 5.0 %all-to-all-done.4 = bf16[8,512,128]{2,1,0:T(8,128)(2,1)S(1)} async-done(((bf16[8,512,128]{2,1,0:T(8,128)(2,1)}), bf16[8,512,128]{2,1,0:T(8,128)(2,1)S(1)}, u32[]{:S(2)}, u32[]{:S(2)}) %all-to-all-start.4) | async-done | bytes 1048608 | tf_op jit(solution)/shard_map/all_to_all | solution.py:1001
  309.1 3.6 all-to-all-start.5
  312.7 31.4 %backward_attention.1 = bf16[4096,256]{1,0:T(8,128)(2,1)S(1)} custom-call(s32[2,16]{1,0:T(2,128)S(1)} %pad_add_fusion.bound_ref, bf16[4096,256]{1,0:T(8,128)(2,1)S(1)} %bitcast.14, bf16[4096,128]{1,0:T(8,128)(2,1)} %get-tuple-element.121.refs_1_, bf16[4096,128]{1,0:T(8,128)(2,1)S(1)} %bitcast.16, bf16[16,10,256,512]{3,2,1,0:T(8,128)(2,1)} %probabilities.1.refs_3_), custom_call_target="tpu_custom_call" | custom-call | flops 17179869184 | bytes 20971520 | tf_op jit(solution)/shard_map/backward_attention/pallas_call | solution.py:745
  344.1 1.3 copy-done
  345.4 53.6 %all_to_all.40.back_ref = bf16[8,512,256]{2,1,0:T(8,128)(2,1)} all-to-all(bf16[8,512,256]{2,1,0:T(8,128)(2,1)} %bitcast.15), channel_id=1, replica_groups={{0,1,2,3,4,5,6,7},{8,9,10,11,12,13,14,15},{16,17,18,19,20,21,22,23},{24..., dimensions={0} | all-to-all | bytes 4194304 | tf_op jit(solution)/shard_map/all_to_all | solution.py:1001
  399.0 7.6 %project_back.1 = (bf16[512,2048]{1,0:T(8,128)(2,1)}, bf16[512,48]{1,0:T(8,128)(2,1)}, bf16[32,16,256]{2,1,0:T(8,128)(2,1)}) custom-call(bf16[8,512,256]{2,1,0:T(8,128)(2,1)} %all_to_all.40.back_ref, bf16[512,1536]{1,0:T(8,128)(2,1)} %get-tuple-element.159.kept_ref, f32[2,128]{1,0:T(2,128)} %pad_maximum_fusion.3.refs_2_.head_gain_ref, ...), custom_call_target="tpu_custom_call" | custom-call | tf_op jit(solution)/shard_map/project_back/pallas_call | solution.py:308
  406.6 2.6 all-to-all-start.7
  409.2 2.1 reduce_grads.3
  411.3 8.6 %input_back.1 = f32[512,1024]{1,0:T(8,128)} custom-call(bf16[512,2048]{1,0:T(8,128)(2,1)} %get-tuple-element.161.refs_0_, bf16[512,48]{1,0:T(8,128)(2,1)} %get-tuple-element.162.refs_1_, bf16[48,1024]{1,0:T(8,128)(2,1)} %get-tuple-element.96.refs_5_.refs_2_, bf16[512,1024]{1,0:T(8,128)(2,1)} %refs_3_.3, f32[1,1024]{1,0:T(1,128)} %bitcast.22, ...), custom_call_target="tpu_custom_call" | custom-call | flops 2147483648 | bytes 10485760 | tf_op jit(solution)/shard_map/input_back/pallas_call | solution.py:353
  420.6 3.4 reduce_grads.2
  (105 shorter events, 16.3 us)
Async XLA Ops:
  0.6 15.0 %copy-start.6 = (bf16[32,2048]{1,0:T(8,128)(2,1)S(1)}, bf16[32,2048]{1,0:T(8,128)(2,1)}, u32[]{:S(2)}) copy-start(bf16[32,2048]{1,0:T(8,128)(2,1)} %param.28) | copy-start | bytes 393220
  2.9 29.5 %copy-start.5 = (bf16[464,1024]{1,0:T(8,128)(2,1)S(1)}, bf16[464,1024]{1,0:T(8,128)(2,1)}, u32[]{:S(2)}) copy-start(bf16[464,1024]{1,0:T(8,128)(2,1)} %stack_shard.1.refs_10_) | copy-start | bytes 2850820
  2.9 24.4 %collective-permute-start.3 = (bf16[464,1024]{1,0:T(8,128)(2,1)}, bf16[464,1024]{1,0:T(8,128)(2,1)}, u32[]{:S(2)}, u32[]{:S(2)}) collective-permute-start(bf16[464,1024]{1,0:T(8,128)(2,1)} %stack_shard.1.refs_10_), channel_id=1, source_target_pairs={{0,8},{1,9},{2,10},{3,11},{4,12},{5,13},{6,14},{7,15},{8,0},{9,1},... | collective-permute-start | bytes 2850824 | tf_op jit(solution)/shard_map/ppermute | solution.py:96
  5.8 23.0 %collective-permute-start.4 = (bf16[464,1024]{1,0:T(8,128)(2,1)}, bf16[464,1024]{1,0:T(8,128)(2,1)}, u32[]{:S(2)}, u32[]{:S(2)}) collective-permute-start(bf16[464,1024]{1,0:T(8,128)(2,1)} %stack_shard.1.refs_10_), channel_id=1, source_target_pairs={{0,16},{1,17},{2,18},{3,19},{4,20},{5,21},{6,22},{7,23},{8,24},{9,... | collective-permute-start | bytes 2850824 | tf_op jit(solution)/shard_map/ppermute | solution.py:96
  7.3 8.7 %collective-permute-start = (bf16[32,2048]{1,0:T(8,128)(2,1)}, bf16[32,2048]{1,0:T(8,128)(2,1)}, u32[]{:S(2)}, u32[]{:S(2)}) collective-permute-start(bf16[32,2048]{1,0:T(8,128)(2,1)} %param.28), channel_id=1, source_target_pairs={{0,1},{1,2},{2,3},{3,0},{4,5},{5,6},{6,7},{7,4},{8,9},{9,10},{10,1... | collective-permute-start | bytes 393224 | tf_op jit(solution)/shard_map/ppermute | solution.py:96
  8.9 10.9 %collective-permute-start.1 = (bf16[32,2048]{1,0:T(8,128)(2,1)}, bf16[32,2048]{1,0:T(8,128)(2,1)S(1)}, u32[]{:S(2)}, u32[]{:S(2)}) collective-permute-start(bf16[32,2048]{1,0:T(8,128)(2,1)} %param.28), channel_id=1, source_target_pairs={{0,2},{1,3},{2,0},{3,1},{4,6},{5,7},{6,4},{7,5},{8,10},{9,11},{10,... | collective-permute-start | bytes 393224 | tf_op jit(solution)/shard_map/ppermute | solution.py:96
  11.5 8.4 %collective-permute-start.2 = (bf16[32,2048]{1,0:T(8,128)(2,1)}, bf16[32,2048]{1,0:T(8,128)(2,1)S(1)}, u32[]{:S(2)}, u32[]{:S(2)}) collective-permute-start(bf16[32,2048]{1,0:T(8,128)(2,1)} %param.28), channel_id=1, source_target_pairs={{0,3},{1,0},{2,1},{3,2},{4,7},{5,4},{6,5},{7,6},{8,11},{9,8},{10,9... | collective-permute-start | bytes 393224 | tf_op jit(solution)/shard_map/ppermute | solution.py:96
  19.8 0.7 copy-start.8
  20.0 0.7 copy-start.7
  20.6 34.6 %all-to-all-start = ((bf16[32,16,256]{2,1,0:T(8,128)(2,1)}), bf16[32,16,256]{2,1,0:T(8,128)(2,1)S(1)}, u32[]{:S(2)}, u32[]{:S(2)}) async-start(bf16[32,16,256]{2,1,0:T(8,128)(2,1)} %pack_adapters.2), calls=%async_computation | async-start | bytes 524288 | tf_op jit(solution)/shard_map/all_to_all | solution.py:1012
  26.3 32.7 %copy-start.17 = (f32[64]{0:T(128)S(1)}, f32[64]{0:T(128)}, u32[]{:S(2)}) copy-start(f32[64]{0:T(128)} %param.25) | copy-start | bytes 772
  26.3 32.7 %copy-start.18 = (f32[64]{0:T(128)S(1)}, f32[64]{0:T(128)}, u32[]{:S(2)}) copy-start(f32[64]{0:T(128)} %param.26) | copy-start | bytes 772
  28.8 15.6 %collective-permute-start.5 = (bf16[128,2048]{1,0:T(8,128)(2,1)S(1)}, bf16[128,2048]{1,0:T(8,128)(2,1)S(1)}, u32[]{:S(2)}, u32[]{:S(2)}) collective-permute-start(bf16[128,2048]{1,0:T(8,128)(2,1)S(1)} %pad_maximum_fusion), channel_id=1, source_target_pairs={{0,8},{1,9},{2,10},{3,11},{4,12},{5,13},{6,14},{7,15},{8,0},{9,1},... | collective-permute-start | bytes 1572872 | tf_op jit(solution)/shard_map/ppermute | solution.py:96
  30.2 24.9 %collective-permute-start.6 = (bf16[128,2048]{1,0:T(8,128)(2,1)S(1)}, bf16[128,2048]{1,0:T(8,128)(2,1)S(1)}, u32[]{:S(2)}, u32[]{:S(2)}) collective-permute-start(bf16[128,2048]{1,0:T(8,128)(2,1)S(1)} %pad_maximum_fusion), channel_id=1, source_target_pairs={{0,16},{1,17},{2,18},{3,19},{4,20},{5,21},{6,22},{7,23},{8,24},{9,... | collective-permute-start | bytes 1572872 | tf_op jit(solution)/shard_map/ppermute | solution.py:96
  32.4 22.8 %collective-permute-start.8 = (bf16[464,1024]{1,0:T(8,128)(2,1)S(1)}, bf16[464,1024]{1,0:T(8,128)(2,1)}, u32[]{:S(2)}, u32[]{:S(2)}) collective-permute-start(bf16[464,1024]{1,0:T(8,128)(2,1)S(1)} %copy-done.5), channel_id=1, source_target_pairs={{0,1},{1,2},{2,3},{3,0},{4,5},{5,6},{6,7},{7,4},{8,9},{9,10},{10,1... | collective-permute-start | bytes 2850824 | tf_op jit(solution)/shard_map/ppermute | solution.py:96
  35.1 20.0 %collective-permute-start.7 = (bf16[128,2048]{1,0:T(8,128)(2,1)S(1)}, bf16[128,2048]{1,0:T(8,128)(2,1)S(1)}, u32[]{:S(2)}, u32[]{:S(2)}) collective-permute-start(bf16[128,2048]{1,0:T(8,128)(2,1)S(1)} %pad_maximum_fusion), channel_id=1, source_target_pairs={{0,24},{1,25},{2,26},{3,27},{4,28},{5,29},{6,30},{7,31},{8,16},{9,... | collective-permute-start | bytes 1572872 | tf_op jit(solution)/shard_map/ppermute | solution.py:96
  55.2 8.7 %copy-start.2 = (bf16[512,2048]{1,0:T(8,128)(2,1)}, bf16[512,2048]{1,0:T(8,128)(2,1)S(1)}, u32[]{:S(2)}) copy-start(bf16[512,2048]{1,0:T(8,128)(2,1)S(1)} %constant_dynamic-update-slice_fusion.refs_7_.refs_6_) | copy-start | bytes 6291460
  55.2 6.8 %copy-start.3 = (bf16[32,16,256]{2,1,0:T(8,128)(2,1)}, bf16[32,16,256]{2,1,0:T(8,128)(2,1)S(1)}, u32[]{:S(2)}) copy-start(bf16[32,16,256]{2,1,0:T(8,128)(2,1)S(1)} %all-to-all-done.source) | copy-start | bytes 786436
  55.2 8.6 %collective-permute-start.9 = (bf16[512,2048]{1,0:T(8,128)(2,1)S(1)}, bf16[512,2048]{1,0:T(8,128)(2,1)}, u32[]{:S(2)}, u32[]{:S(2)}) collective-permute-start(bf16[512,2048]{1,0:T(8,128)(2,1)S(1)} %constant_dynamic-update-slice_fusion.refs_7_.refs_6_), channel_id=1, source_target_pairs={{0,4},{1,5},{2,6},{3,7},{4,0},{5,1},{6,2},{7,3},{8,12},{9,13},{10,... | collective-permute-start | bytes 6291464 | tf_op jit(solution)/shard_map/ppermute | solution.py:96
  55.6 25.3 %collective-permute-start.10 = (bf16[464,1024]{1,0:T(8,128)(2,1)}, bf16[464,1024]{1,0:T(8,128)(2,1)}, u32[]{:S(2)}, u32[]{:S(2)}) collective-permute-start(bf16[464,1024]{1,0:T(8,128)(2,1)} %collective-permute-done.8.refs_13_), channel_id=1, source_target_pairs={{0,1},{1,2},{2,3},{3,0},{4,5},{5,6},{6,7},{7,4},{8,9},{9,10},{10,1... | collective-permute-start | bytes 2850824 | tf_op jit(solution)/shard_map/ppermute | solution.py:96
  56.8 24.1 %collective-permute-start.11 = (bf16[464,1024]{1,0:T(8,128)(2,1)}, bf16[464,1024]{1,0:T(8,128)(2,1)}, u32[]{:S(2)}, u32[]{:S(2)}) collective-permute-start(bf16[464,1024]{1,0:T(8,128)(2,1)} %collective-permute-done.8.refs_13_), channel_id=1, source_target_pairs={{0,8},{1,9},{2,10},{3,11},{4,12},{5,13},{6,14},{7,15},{8,0},{9,1},... | collective-permute-start | bytes 2850824 | tf_op jit(solution)/shard_map/ppermute | solution.py:96
  57.9 23.2 %collective-permute-start.12 = (bf16[464,1024]{1,0:T(8,128)(2,1)}, bf16[464,1024]{1,0:T(8,128)(2,1)}, u32[]{:S(2)}, u32[]{:S(2)}) collective-permute-start(bf16[464,1024]{1,0:T(8,128)(2,1)} %collective-permute-done.3.refs_11_), channel_id=1, source_target_pairs={{0,16},{1,17},{2,18},{3,19},{4,20},{5,21},{6,22},{7,23},{8,24},{9,... | collective-permute-start | bytes 2850824 | tf_op jit(solution)/shard_map/ppermute | solution.py:96
  81.1 33.5 %copy-start.9 = (s32[16384]{0:T(1024)S(1)}, s32[16384]{0:T(1024)}, u32[]{:S(2)}) copy-start(s32[16384]{0:T(1024)} %param.22) | copy-start | bytes 196612
  81.1 73.0 %all-to-all-start.1 = ((bf16[8,512,256]{2,1,0:T(8,128)(2,1)}), bf16[8,512,256]{2,1,0:T(8,128)(2,1)S(1)}, u32[]{:S(2)}, u32[]{:S(2)}) async-start(bf16[8,512,256]{2,1,0:T(8,128)(2,1)} %get-tuple-element.109), calls=%async_computation.1 | async-start | bytes 4194304 | tf_op jit(solution)/shard_map/all_to_all | solution.py:1001
  85.1 23.8 %collective-permute-start.13 = (bf16[464,1024]{1,0:T(8,128)(2,1)}, bf16[464,1024]{1,0:T(8,128)(2,1)}, u32[]{:S(2)}, u32[]{:S(2)}) collective-permute-start(bf16[464,1024]{1,0:T(8,128)(2,1)} %collective-permute-done.8.refs_13_), channel_id=1, source_target_pairs={{0,16},{1,17},{2,18},{3,19},{4,20},{5,21},{6,22},{7,23},{8,24},{9,... | collective-permute-start | bytes 2850824 | tf_op jit(solution)/shard_map/ppermute | solution.py:96
  86.2 23.5 %collective-permute-start.14 = (bf16[464,1024]{1,0:T(8,128)(2,1)}, bf16[464,1024]{1,0:T(8,128)(2,1)}, u32[]{:S(2)}, u32[]{:S(2)}) collective-permute-start(bf16[464,1024]{1,0:T(8,128)(2,1)} %collective-permute-done.10.refs_14_), channel_id=1, source_target_pairs={{0,8},{1,9},{2,10},{3,11},{4,12},{5,13},{6,14},{7,15},{8,0},{9,1},... | collective-permute-start | bytes 2850824 | tf_op jit(solution)/shard_map/ppermute | solution.py:96
  87.2 22.5 %collective-permute-start.15 = (bf16[464,1024]{1,0:T(8,128)(2,1)S(1)}, bf16[464,1024]{1,0:T(8,128)(2,1)S(1)}, u32[]{:S(2)}, u32[]{:S(2)}) collective-permute-start(bf16[464,1024]{1,0:T(8,128)(2,1)S(1)} %copy-done.5), channel_id=1, source_target_pairs={{0,4},{1,5},{2,6},{3,7},{4,0},{5,1},{6,2},{7,3},{8,12},{9,13},{10,... | collective-permute-start | bytes 2850824 | tf_op jit(solution)/shard_map/ppermute | solution.py:96
  109.7 0.9 copy-start.10
  110.7 22.6 %collective-permute-start.16 = (bf16[464,1024]{1,0:T(8,128)(2,1)}, bf16[464,1024]{1,0:T(8,128)(2,1)S(1)}, u32[]{:S(2)}, u32[]{:S(2)}) collective-permute-start(bf16[464,1024]{1,0:T(8,128)(2,1)} %collective-permute-done.13.refs_18_), channel_id=1, source_target_pairs={{0,8},{1,9},{2,10},{3,11},{4,12},{5,13},{6,14},{7,15},{8,0},{9,1},... | collective-permute-start | bytes 2850824 | tf_op jit(solution)/shard_map/ppermute | solution.py:96
  111.6 22.4 %collective-permute-start.17 = (bf16[464,1024]{1,0:T(8,128)(2,1)}, bf16[464,1024]{1,0:T(8,128)(2,1)}, u32[]{:S(2)}, u32[]{:S(2)}) collective-permute-start(bf16[464,1024]{1,0:T(8,128)(2,1)} %collective-permute-done.10.refs_14_), channel_id=1, source_target_pairs={{0,16},{1,17},{2,18},{3,19},{4,20},{5,21},{6,22},{7,23},{8,24},{9,... | collective-permute-start | bytes 2850824 | tf_op jit(solution)/shard_map/ppermute | solution.py:96
  112.4 21.6 %collective-permute-start.18 = (bf16[464,1024]{1,0:T(8,128)(2,1)}, bf16[464,1024]{1,0:T(8,128)(2,1)}, u32[]{:S(2)}, u32[]{:S(2)}) collective-permute-start(bf16[464,1024]{1,0:T(8,128)(2,1)} %collective-permute-done.8.refs_13_), channel_id=1, source_target_pairs={{0,4},{1,5},{2,6},{3,7},{4,0},{5,1},{6,2},{7,3},{8,12},{9,13},{10,... | collective-permute-start | bytes 2850824 | tf_op jit(solution)/shard_map/ppermute | solution.py:96
  112.4 21.6 %collective-permute-start.19 = (bf16[464,1024]{1,0:T(8,128)(2,1)}, bf16[464,1024]{1,0:T(8,128)(2,1)}, u32[]{:S(2)}, u32[]{:S(2)}) collective-permute-start(bf16[464,1024]{1,0:T(8,128)(2,1)} %collective-permute-done.3.refs_11_), channel_id=1, source_target_pairs={{0,4},{1,5},{2,6},{3,7},{4,0},{5,1},{6,2},{7,3},{8,12},{9,13},{10,... | collective-permute-start | bytes 2850824 | tf_op jit(solution)/shard_map/ppermute | solution.py:96
  112.9 44.0 %collective-permute-start.20 = (bf16[464,1024]{1,0:T(8,128)(2,1)}, bf16[464,1024]{1,0:T(8,128)(2,1)}, u32[]{:S(2)}, u32[]{:S(2)}) collective-permute-start(bf16[464,1024]{1,0:T(8,128)(2,1)} %collective-permute-done.10.refs_14_), channel_id=1, source_target_pairs={{0,1},{1,2},{2,3},{3,0},{4,5},{5,6},{6,7},{7,4},{8,9},{9,10},{10,1... | collective-permute-start | bytes 2850824 | tf_op jit(solution)/shard_map/ppermute | solution.py:96
  133.2 20.8 %copy-start.11 = (bf16[464,1024]{1,0:T(8,128)(2,1)}, bf16[464,1024]{1,0:T(8,128)(2,1)S(1)}, u32[]{:S(2)}) copy-start(bf16[464,1024]{1,0:T(8,128)(2,1)S(1)} %collective-permute-done.16.refs_21_) | copy-start | bytes 2850820
  154.0 35.5 %all-to-all-start.2 = ((bf16[32,16,640]{2,1,0:T(8,128)(2,1)}), bf16[32,16,640]{2,1,0:T(8,128)(2,1)S(1)}, u32[]{:S(2)}, u32[]{:S(2)}) async-start(bf16[32,16,640]{2,1,0:T(8,128)(2,1)} %pack_adapters.3), calls=%async_computation.2 | async-start | bytes 1310720 | tf_op jit(solution)/shard_map/all_to_all | solution.py:1012
  156.9 29.9 %collective-permute-start.21 = (bf16[464,1024]{1,0:T(8,128)(2,1)}, bf16[464,1024]{1,0:T(8,128)(2,1)S(1)}, u32[]{:S(2)}, u32[]{:S(2)}) collective-permute-start(bf16[464,1024]{1,0:T(8,128)(2,1)} %collective-permute-done.20.refs_20_), channel_id=1, source_target_pairs={{0,8},{1,9},{2,10},{3,11},{4,12},{5,13},{6,14},{7,15},{8,0},{9,1},... | collective-permute-start | bytes 2850824 | tf_op jit(solution)/shard_map/ppermute | solution.py:96
  158.6 28.8 %collective-permute-start.22 = (bf16[464,1024]{1,0:T(8,128)(2,1)}, bf16[464,1024]{1,0:T(8,128)(2,1)}, u32[]{:S(2)}, u32[]{:S(2)}) collective-permute-start(bf16[464,1024]{1,0:T(8,128)(2,1)} %collective-permute-done.20.refs_20_), channel_id=1, source_target_pairs={{0,16},{1,17},{2,18},{3,19},{4,20},{5,21},{6,22},{7,23},{8,24},{9,... | collective-permute-start | bytes 2850824 | tf_op jit(solution)/shard_map/ppermute | solution.py:96
  160.1 27.3 %collective-permute-start.23 = (bf16[464,1024]{1,0:T(8,128)(2,1)}, bf16[464,1024]{1,0:T(8,128)(2,1)S(1)}, u32[]{:S(2)}, u32[]{:S(2)}) collective-permute-start(bf16[464,1024]{1,0:T(8,128)(2,1)} %collective-permute-done.4.refs_12_), channel_id=1, source_target_pairs={{0,4},{1,5},{2,6},{3,7},{4,0},{5,1},{6,2},{7,3},{8,12},{9,13},{10,... | collective-permute-start | bytes 2850824 | tf_op jit(solution)/shard_map/ppermute | solution.py:96
  160.1 27.3 %collective-permute-start.24 = (bf16[464,1024]{1,0:T(8,128)(2,1)}, bf16[464,1024]{1,0:T(8,128)(2,1)S(1)}, u32[]{:S(2)}, u32[]{:S(2)}) collective-permute-start(bf16[464,1024]{1,0:T(8,128)(2,1)} %collective-permute-done.12.refs_16_), channel_id=1, source_target_pairs={{0,4},{1,5},{2,6},{3,7},{4,0},{5,1},{6,2},{7,3},{8,12},{9,13},{10,... | collective-permute-start | bytes 2850824 | tf_op jit(solution)/shard_map/ppermute | solution.py:96
  160.6 26.8 %collective-permute-start.25 = (bf16[464,1024]{1,0:T(8,128)(2,1)}, bf16[464,1024]{1,0:T(8,128)(2,1)S(1)}, u32[]{:S(2)}, u32[]{:S(2)}) collective-permute-start(bf16[464,1024]{1,0:T(8,128)(2,1)} %collective-permute-done.10.refs_14_), channel_id=1, source_target_pairs={{0,4},{1,5},{2,6},{3,7},{4,0},{5,1},{6,2},{7,3},{8,12},{9,13},{10,... | collective-permute-start | bytes 2850824 | tf_op jit(solution)/shard_map/ppermute | solution.py:96
  186.8 2.7 copy-start.12
  187.4 2.1 copy-start.13
  187.4 2.1 copy-start.14
  187.4 2.1 copy-start.15
  187.4 23.4 %collective-permute-start.26 = (bf16[464,1024]{1,0:T(8,128)(2,1)}, bf16[464,1024]{1,0:T(8,128)(2,1)}, u32[]{:S(2)}, u32[]{:S(2)}) collective-permute-start(bf16[464,1024]{1,0:T(8,128)(2,1)} %collective-permute-done.22.refs_26_), channel_id=1, source_target_pairs={{0,8},{1,9},{2,10},{3,11},{4,12},{5,13},{6,14},{7,15},{8,0},{9,1},... | collective-permute-start | bytes 2850824 | tf_op jit(solution)/shard_map/ppermute | solution.py:96
  188.5 22.9 %collective-permute-start.27 = (bf16[464,1024]{1,0:T(8,128)(2,1)}, bf16[464,1024]{1,0:T(8,128)(2,1)}, u32[]{:S(2)}, u32[]{:S(2)}) collective-permute-start(bf16[464,1024]{1,0:T(8,128)(2,1)} %collective-permute-done.14.refs_17_), channel_id=1, source_target_pairs={{0,16},{1,17},{2,18},{3,19},{4,20},{5,21},{6,22},{7,23},{8,24},{9,... | collective-permute-start | bytes 2850824 | tf_op jit(solution)/shard_map/ppermute | solution.py:96
  189.0 22.4 %collective-permute-start.28 = (bf16[464,1024]{1,0:T(8,128)(2,1)}, bf16[464,1024]{1,0:T(8,128)(2,1)}, u32[]{:S(2)}, u32[]{:S(2)}) collective-permute-start(bf16[464,1024]{1,0:T(8,128)(2,1)} %collective-permute-done.11.refs_15_), channel_id=1, source_target_pairs={{0,4},{1,5},{2,6},{3,7},{4,0},{5,1},{6,2},{7,3},{8,12},{9,13},{10,... | collective-permute-start | bytes 2850824 | tf_op jit(solution)/shard_map/ppermute | solution.py:96
  189.0 22.4 %collective-permute-start.29 = (bf16[464,1024]{1,0:T(8,128)(2,1)}, bf16[464,1024]{1,0:T(8,128)(2,1)}, u32[]{:S(2)}, u32[]{:S(2)}) collective-permute-start(bf16[464,1024]{1,0:T(8,128)(2,1)} %collective-permute-done.13.refs_18_), channel_id=1, source_target_pairs={{0,4},{1,5},{2,6},{3,7},{4,0},{5,1},{6,2},{7,3},{8,12},{9,13},{10,... | collective-permute-start | bytes 2850824 | tf_op jit(solution)/shard_map/ppermute | solution.py:96
  189.5 21.9 %collective-permute-start.30 = (bf16[464,1024]{1,0:T(8,128)(2,1)}, bf16[464,1024]{1,0:T(8,128)(2,1)}, u32[]{:S(2)}, u32[]{:S(2)}) collective-permute-start(bf16[464,1024]{1,0:T(8,128)(2,1)} %collective-permute-done.14.refs_17_), channel_id=1, source_target_pairs={{0,4},{1,5},{2,6},{3,7},{4,0},{5,1},{6,2},{7,3},{8,12},{9,13},{10,... | collective-permute-start | bytes 2850824 | tf_op jit(solution)/shard_map/ppermute | solution.py:96
  189.6 4.9 %copy-start.1 = (bf16[32,16,640]{2,1,0:T(8,128)(2,1)}, bf16[32,16,640]{2,1,0:T(8,128)(2,1)S(1)}, u32[]{:S(2)}) copy-start(bf16[32,16,640]{2,1,0:T(8,128)(2,1)S(1)} %all-to-all-done.2.source) | copy-start | bytes 1966084
  189.6 31.1 %all-to-all-start.3 = ((bf16[8,512,128]{2,1,0:T(8,128)(2,1)}), bf16[8,512,128]{2,1,0:T(8,128)(2,1)}, u32[]{:S(2)}, u32[]{:S(2)}) async-start(bf16[8,512,128]{2,1,0:T(8,128)(2,1)} %bitcast.6), calls=%async_computation.3 | async-start | bytes 2097152 | tf_op jit(solution)/shard_map/all_to_all | solution.py:1001
  211.4 3.4 collective-permute-start.31
  211.4 4.2 collective-permute-start.32
  211.9 5.1 %collective-permute-start.33 = (bf16[464,1024]{1,0:T(8,128)(2,1)}, bf16[464,1024]{1,0:T(8,128)(2,1)}, u32[]{:S(2)}, u32[]{:S(2)}) collective-permute-start(bf16[464,1024]{1,0:T(8,128)(2,1)} %collective-permute-done.20.refs_20_), channel_id=1, source_target_pairs={{0,4},{1,5},{2,6},{3,7},{4,0},{5,1},{6,2},{7,3},{8,12},{9,13},{10,... | collective-permute-start | bytes 2850824 | tf_op jit(solution)/shard_map/ppermute | solution.py:96
  212.0 6.3 %collective-permute-start.34 = (bf16[464,1024]{1,0:T(8,128)(2,1)}, bf16[464,1024]{1,0:T(8,128)(2,1)}, u32[]{:S(2)}, u32[]{:S(2)}) collective-permute-start(bf16[464,1024]{1,0:T(8,128)(2,1)} %copy-done.12), channel_id=1, source_target_pairs={{0,4},{1,5},{2,6},{3,7},{4,0},{5,1},{6,2},{7,3},{8,12},{9,13},{10,... | collective-permute-start | bytes 2850824 | tf_op jit(solution)/shard_map/ppermute | solution.py:96
  212.5 7.3 %collective-permute-start.35 = (bf16[464,1024]{1,0:T(8,128)(2,1)}, bf16[464,1024]{1,0:T(8,128)(2,1)}, u32[]{:S(2)}, u32[]{:S(2)}) collective-permute-start(bf16[464,1024]{1,0:T(8,128)(2,1)} %collective-permute-done.22.refs_26_), channel_id=1, source_target_pairs={{0,4},{1,5},{2,6},{3,7},{4,0},{5,1},{6,2},{7,3},{8,12},{9,13},{10,... | collective-permute-start | bytes 2850824 | tf_op jit(solution)/shard_map/ppermute | solution.py:96
  214.7 10.2 %copy-start.16 = (bf16[464,1024]{1,0:T(8,128)(2,1)}, bf16[464,1024]{1,0:T(8,128)(2,1)S(1)}, u32[]{:S(2)}) copy-start(bf16[464,1024]{1,0:T(8,128)(2,1)S(1)} %collective-permute-done.31.refs_35_) | copy-start | bytes 2850820
  220.7 2.9 collective-permute-start.36
  221.0 3.9 collective-permute-start.37
  279.3 29.8 %all-to-all-start.4 = ((bf16[8,512,128]{2,1,0:T(8,128)(2,1)}), bf16[8,512,128]{2,1,0:T(8,128)(2,1)S(1)}, u32[]{:S(2)}, u32[]{:S(2)}) async-start(bf16[8,512,128]{2,1,0:T(8,128)(2,1)} %get-tuple-element.154), calls=%async_computation.4 | async-start | bytes 2097152 | tf_op jit(solution)/shard_map/all_to_all | solution.py:1001
  309.1 36.3 %all-to-all-start.5 = ((bf16[32,16,640]{2,1,0:T(8,128)(2,1)}), bf16[32,16,640]{2,1,0:T(8,128)(2,1)}, u32[]{:S(2)}, u32[]{:S(2)}) async-start(bf16[32,16,640]{2,1,0:T(8,128)(2,1)} %pack_grads.1), calls=%async_computation.5 | async-start | bytes 1310720 | tf_op jit(solution)/shard_map/all_to_all | solution.py:1012
  344.1 1.3 copy-start
  406.6 13.3 %all-to-all-start.7 = ((bf16[32,16,256]{2,1,0:T(8,128)(2,1)}), bf16[32,16,256]{2,1,0:T(8,128)(2,1)S(1)}, u32[]{:S(2)}, u32[]{:S(2)}) async-start(bf16[32,16,256]{2,1,0:T(8,128)(2,1)} %get-tuple-element.164), calls=%async_computation.7 | async-start | bytes 524288 | tf_op jit(solution)/shard_map/all_to_all | solution.py:1012
  419.9 0.7 copy-start.4

commit v5 on v4

--- a/solution.py
+++ b/solution.py
@@ -703,9 +703,10 @@
             own = pl.ds(pl.multiple_of(step * BLOCK, BLOCK), BLOCK)
             lanes = lax.broadcasted_iota(jnp.int32, (2 * BLOCK, 128), 1)
             query_low = stacked_heads(query_ref[own, :PAIR].astype(F32)).astype(BF16)
-            grad = stacked_heads(grad_ref[own, :].astype(F32))
-            weighed = stacked_heads(mixed_ref[own, :].astype(F32))
-            inner = jnp.sum(jnp.where(lanes < HEAD_DIM, grad * weighed, 0.0), axis=1, keepdims=True)
+            pair = grad_ref[own, :].astype(F32)
+            grad = stacked_heads(pair)
+            weighed = stacked_heads(pair * mixed_ref[own, :].astype(F32))
+            inner = jnp.sum(jnp.where(lanes < HEAD_DIM, weighed, 0.0), axis=1, keepdims=True)
             grad_low = with_columns(grad, [part.astype(F32) for part in split_three(-inner)], lanes).astype(BF16)
             diagonal = halo // BLOCK + step
 
@@ -1073,14 +1074,14 @@
     mixed, logs = forward_attention(bounds, starts, queries, keyvals, column)
     chosen += list(unpack_adapters(slabs, shapes[2:]))
     if spread:
-        pending.append(logs)
-        move((6, 3, 2, 0), (6, 2, 4, 0), *cores((3, 1), (5, 1), (3, 2)))
+        pending += [logs, chosen[-1]]
+        move((6, 3, 2, 0), (6, 2, 4, 0), *cores((3, 3), (5, 3), (3, 1)))
     mixed_then = lax.optimization_barrier((mixed, slabs))[0]
     mixture_tok = swap(mixed_then.reshape(members, rows, PAIR))
     if spread:
-        pending.append(chosen[-1])
-        move(*cores((5, 2), (7, 1), (1, 3), (3, 3), (5, 3)))
-        pending.append(mixture_tok)
+        ended, pending[:] = pending[:2], pending[2:]
+        move(*cores((5, 1), (3, 2), (5, 2), (7, 1), (1, 3)))
+        pending += [mixture_tok, *ended]
         move(*cores((7, 2), (7, 3)))
         weights = Pieces([((flip, (step,)), block) for (flip, step), block in found.items()], D)
     output, middle_grad, mixture_grad, early = feed_forward(

time: 426 us -> 429 us (level)
  Pallas kernels: 176 us -> 166 us
  starting transfers between devices: 59.2 us -> 65.7 us
  waiting for transfers between devices: 123 us -> 128 us
    all_to_all x3, waiting for transfers between devices: 26.1 us -> 36.2 us  [swap(): lax.all_to_all(value, AXES, 0, 0, axis_index_groups=groups, tiled=True)]
    all_to_all x4, starting transfers between devices: 13.4 us -> 18.6 us  [exchange(): return lax.all_to_all(packed, AXES, 0, 0, tiled=True)]
    ppermute x38, waiting for transfers between devices: 97 us -> 91.8 us  [hop(): return lax.ppermute(value, AXES, pairs)]
  transfers between devices with their start and end apart: 45 -> 45, of which waited for: 27 -> 22; matrix products, arithmetic and copies ran while one was open for 2% -> 2% of each run, Pallas kernels for 26% -> 23%
where the time goes in v5:
time: 429 us; the launch traced here: 426 us
  Pallas kernels  166 us (39%)
  waiting for transfers between devices  128 us (30%)
  starting transfers between devices  65.7 us (15%)
  blocking collectives  53.6 us (12%)
  local copies, waits for them, and re-layouts  7.83 us (2%)
  other arithmetic  4.29 us (1%)
    ppermute x38, waiting for transfers between devices, hop(): return lax.ppermute(value, AXES, pairs)  91.8 us
    pallas_call x1, Pallas kernels, feed_forward(): pl.pallas_call(kernel, in_specs=[VMEM_SPEC] * 10 + [ANY_SPEC] * count, ou...  54.4 us
    all_to_all x1, blocking collectives, swap(): lax.all_to_all(value, AXES, 0, 0, axis_index_groups=groups, tiled=True)  53.6 us
    all_to_all x3, waiting for transfers between devices, swap(): lax.all_to_all(value, AXES, 0, 0, axis_index_groups=groups, tiled=True)  36.2 us
    ppermute x38, starting transfers between devices, hop(): return lax.ppermute(value, AXES, pairs)  34.8 us
    pallas_call x1, Pallas kernels, backward_attention(): pl.pallas_call(kernel, in_specs=[SMEM_SPEC] + [VMEM_SPEC] * (2 + len(arra...  27.1 us
    pallas_call x1, Pallas kernels, forward_attention(): pl.pallas_call(kernel, in_specs=[SMEM_SPEC] + [VMEM_SPEC] * (1 + len(arra...  20.7 us
    all_to_all x4, starting transfers between devices, exchange(): return lax.all_to_all(packed, AXES, 0, 0, tiled=True)  18.6 us
  transfers between devices with their start and end apart: 45, of which 22 were waited for; matrix products, arithmetic and copies ran while one was open for 2% of the time, Pallas kernels for 23%

profile of v5, /device:TPU:0, one launch (start us, length us, event | category | flops | bytes accessed | tf_op | source)
XLA Modules:
  0.0 426.1 jit_solution(17711736193395805068)
XLA Ops:
  0.7 2.2 stack_shard.1.refs_10_
  2.9 2.9 collective-permute-start.3
  5.8 1.5 collective-permute-start.4
  7.4 1.6 collective-permute-start
  8.9 2.6 collective-permute-start.1
  11.5 1.3 collective-permute-start.2
  12.9 2.8 pack_adapters.2
  16.0 3.8 collective-permute-done.1
  20.6 4.6 %all-to-all-start = ((bf16[32,16,256]{2,1,0:T(8,128)(2,1)}), bf16[32,16,256]{2,1,0:T(8,128)(2,1)S(1)}, u32[]{:S(2)}, u32[]{:S(2)}) async-start(bf16[32,16,256]{2,1,0:T(8,128)(2,1)} %pack_adapters.2), calls=%async_computation | async-start | bytes 524288 | tf_op jit(solution)/shard_map/all_to_all | solution.py:1013
  25.2 1.1 pad_maximum_fusion
  26.3 0.9 collective-permute-done.3.refs_11_
  27.3 1.6 collective-permute-done.4.refs_12_
  29.3 0.9 constant_dynamic-update-slice_fusion.5
  30.2 2.2 collective-permute-start.6
  32.4 1.8 collective-permute-start.8
  35.1 1.6 collective-permute-start.7
  37.6 6.9 %collective-permute-done.5 = bf16[128,2048]{1,0:T(8,128)(2,1)S(1)} collective-permute-done((bf16[128,2048]{1,0:T(8,128)(2,1)S(1)}, bf16[128,2048]{1,0:T(8,128)(2,1)S(1)}, u32[]{:S(2)}, u32[]{:S(2)}) %collective-permute-start.5) | collective-permute-done | bytes 524320 | tf_op jit(solution)/shard_map/ppermute | solution.py:96
  44.5 10.6 %collective-permute-done.6 = bf16[128,2048]{1,0:T(8,128)(2,1)S(1)} collective-permute-done((bf16[128,2048]{1,0:T(8,128)(2,1)S(1)}, bf16[128,2048]{1,0:T(8,128)(2,1)S(1)}, u32[]{:S(2)}, u32[]{:S(2)}) %collective-permute-start.6) | collective-permute-done | bytes 524320 | tf_op jit(solution)/shard_map/ppermute | solution.py:96
  55.6 1.1 collective-permute-start.10
  56.8 1.2 collective-permute-start.11
  57.9 1.0 collective-permute-start.12
  59.7 1.0 fusion
  60.7 1.3 pad_maximum_fusion.1
  62.0 1.9 unpack_adapters.2
  63.9 11.1 %project_heads.1 = (bf16[8,512,256]{2,1,0:T(8,128)(2,1)}, bf16[512,48]{1,0:T(8,128)(2,1)}, bf16[512,1536]{1,0:T(8,128)(2,1)}) custom-call(bf16[512,1024]{1,0:T(8,128)(2,1)} %refs_3_.3, f32[1,1024]{1,0:T(1,128)} %bitcast.20, f32[2,128]{1,0:T(2,128)} %pad_maximum_fusion.3.refs_2_.head_gain_ref, f32[512,128]{1,0:T(8,128)} %get-tuple-element.179.refs_3_.cos_ref, ...), custom_call_target="tpu_custom_call" | custom-call | flops 2147483648 | bytes 10485760 | tf_op jit(solution)/shard_map/project_heads/pallas_call | solution.py:226
  74.9 5.9 %collective-permute-done.10.refs_14_ = bf16[464,1024]{1,0:T(8,128)(2,1)} collective-permute-done((bf16[464,1024]{1,0:T(8,128)(2,1)}, bf16[464,1024]{1,0:T(8,128)(2,1)}, u32[]{:S(2)}, u32[]{:S(2)}) %collective-permute-start.10) | collective-permute-done | bytes 950304 | tf_op jit(solution)/shard_map/ppermute | solution.py:96
  81.1 4.0 all-to-all-start.1
  85.1 1.1 collective-permute-start.13
  86.2 1.0 collective-permute-start.14
  87.2 21.7 %collective-permute-done.13.refs_18_ = bf16[464,1024]{1,0:T(8,128)(2,1)} collective-permute-done((bf16[464,1024]{1,0:T(8,128)(2,1)}, bf16[464,1024]{1,0:T(8,128)(2,1)}, u32[]{:S(2)}, u32[]{:S(2)}) %collective-permute-start.13) | collective-permute-done | bytes 950304 | tf_op jit(solution)/shard_map/ppermute | solution.py:96
  109.6 1.0 copy-done.11
  110.6 0.9 collective-permute-start.16
  113.0 1.7 collective-permute-start.20
  115.1 2.7 pack_adapters.3
  117.7 15.5 %collective-permute-done.16.refs_21_ = bf16[464,1024]{1,0:T(8,128)(2,1)S(1)} collective-permute-done((bf16[464,1024]{1,0:T(8,128)(2,1)}, bf16[464,1024]{1,0:T(8,128)(2,1)S(1)}, u32[]{:S(2)}, u32[]{:S(2)}) %collective-permute-start.16) | collective-permute-done | bytes 950304 | tf_op jit(solution)/shard_map/ppermute | solution.py:96
  133.2 1.0 collective-permute-done.17.refs_22_
  134.3 19.8 %all-to-all-done.1 = bf16[8,512,256]{2,1,0:T(8,128)(2,1)S(1)} async-done(((bf16[8,512,256]{2,1,0:T(8,128)(2,1)}), bf16[8,512,256]{2,1,0:T(8,128)(2,1)S(1)}, u32[]{:S(2)}, u32[]{:S(2)}) %all-to-all-start.1) | async-done | bytes 2097184 | tf_op jit(solution)/shard_map/all_to_all | solution.py:1002
  154.1 2.6 all-to-all-start.2
  156.9 1.7 collective-permute-start.21
  158.6 1.5 collective-permute-start.22
  160.6 20.7 %forward_attention.1 = (bf16[4096,128]{1,0:T(8,128)(2,1)}, f32[16,8,512]{2,1,0:T(8,128)S(1)}) custom-call(s32[2,16]{1,0:T(2,128)S(1)} %pad_add_fusion.bound_ref, s32[1,4096]{1,0:T(1,128)S(1)} %bitcast.17, bf16[4096,256]{1,0:T(8,128)(2,1)S(1)} %bitcast.12), custom_call_target="tpu_custom_call" | custom-call | flops 8589934592 | bytes 4194304 | tf_op jit(solution)/shard_map/forward_attention/pallas_call | solution.py:561
  182.2 2.3 unpack_adapters.3
  184.4 2.5 collective-permute-done.21.refs_25_
  188.1 1.0 collective-permute-start.26
  189.0 1.9 collective-permute-start.27
  191.0 4.7 %all-to-all-start.3 = ((bf16[8,512,128]{2,1,0:T(8,128)(2,1)}), bf16[8,512,128]{2,1,0:T(8,128)(2,1)S(1)}, u32[]{:S(2)}, u32[]{:S(2)}) async-start(bf16[8,512,128]{2,1,0:T(8,128)(2,1)} %bitcast.6), calls=%async_computation.3 | async-start | bytes 2097152 | tf_op jit(solution)/shard_map/all_to_all | solution.py:1002
  196.8 14.9 %collective-permute-done.26.refs_30_ = bf16[464,1024]{1,0:T(8,128)(2,1)} collective-permute-done((bf16[464,1024]{1,0:T(8,128)(2,1)}, bf16[464,1024]{1,0:T(8,128)(2,1)}, u32[]{:S(2)}, u32[]{:S(2)}) %collective-permute-start.26) | collective-permute-done | bytes 950304 | tf_op jit(solution)/shard_map/ppermute | solution.py:96
  212.6 9.2 %all-to-all-done.3.refs_0_ = bf16[8,512,128]{2,1,0:T(8,128)(2,1)S(1)} async-done(((bf16[8,512,128]{2,1,0:T(8,128)(2,1)}), bf16[8,512,128]{2,1,0:T(8,128)(2,1)S(1)}, u32[]{:S(2)}, u32[]{:S(2)}) %all-to-all-start.3) | async-done | bytes 1048608 | tf_op jit(solution)/shard_map/all_to_all | solution.py:1002
  222.5 2.4 collective-permute-done.36.refs_40_
  224.8 1.4 collective-permute-done.37.refs_41_
  226.2 54.4 %feed_forward.1 = (bf16[512,1024]{1,0:T(8,128)(2,1)}, f32[512,1024]{1,0:T(8,128)}, bf16[8,512,128]{2,1,0:T(8,128)(2,1)}, f32[16,1024]{1,0:T(8,128)}, f32[16,1024...) custom-call(bf16[8,512,128]{2,1,0:T(8,128)(2,1)} %copy-done.3, ...), custom_call_target="tpu_custom_call" | custom-call | flops 31138512896 | bytes 36700160 | tf_op jit(solution)/shard_map/feed_forward/pallas_call | solution.py:950
  280.6 3.6 all-to-all-start.4
  284.1 2.6 pack_grads.1
  286.7 16.3 %probabilities.1.refs_3_ = bf16[16,10,256,512]{3,2,1,0:T(8,128)(2,1)} custom-call(s32[2,16]{1,0:T(2,128)S(1)} %pad_add_fusion.bound_ref, s32[1,4096]{1,0:T(1,128)S(1)} %bitcast.18, f32[16,8,512]{2,1,0:T(8,128)S(1)} %get-tuple-element.156.log_ref, bf16[4096,256]{1,0:T(8,128)(2,1)S(1)} %bitcast.13), custom_call_target="tpu_custom_call" | custom-call | flops 4294967296 | bytes 20971520 | tf_op jit(solution)/shard_map/probabilities/pallas_call | solution.py:644
  303.0 7.1 %all-to-all-done.4 = bf16[8,512,128]{2,1,0:T(8,128)(2,1)S(1)} async-done(((bf16[8,512,128]{2,1,0:T(8,128)(2,1)}), bf16[8,512,128]{2,1,0:T(8,128)(2,1)S(1)}, u32[]{:S(2)}, u32[]{:S(2)}) %all-to-all-start.4) | async-done | bytes 1048608 | tf_op jit(solution)/shard_map/all_to_all | solution.py:1002
  310.2 3.3 all-to-all-start.5
  313.5 27.1 %backward_attention.1 = bf16[4096,256]{1,0:T(8,128)(2,1)S(1)} custom-call(s32[2,16]{1,0:T(2,128)S(1)} %pad_add_fusion.bound_ref, bf16[4096,256]{1,0:T(8,128)(2,1)S(1)} %bitcast.14, bf16[4096,128]{1,0:T(8,128)(2,1)} %get-tuple-element.121.refs_1_, bf16[4096,128]{1,0:T(8,128)(2,1)S(1)} %bitcast.16, bf16[16,10,256,512]{3,2,1,0:T(8,128)(2,1)} %probabilities.1.refs_3_), custom_call_target="tpu_custom_call" | custom-call | flops 17179869184 | bytes 20971520 | tf_op jit(solution)/shard_map/backward_attention/pallas_call | solution.py:746
  340.7 1.3 copy-done
  342.0 53.6 %all_to_all.40.back_ref = bf16[8,512,256]{2,1,0:T(8,128)(2,1)} all-to-all(bf16[8,512,256]{2,1,0:T(8,128)(2,1)} %bitcast.15), channel_id=1, replica_groups={{0,1,2,3,4,5,6,7},{8,9,10,11,12,13,14,15},{16,17,18,19,20,21,22,23},{24..., dimensions={0} | all-to-all | bytes 4194304 | tf_op jit(solution)/shard_map/all_to_all | solution.py:1002
  395.6 7.6 %project_back.1 = (bf16[512,2048]{1,0:T(8,128)(2,1)}, bf16[512,48]{1,0:T(8,128)(2,1)}, bf16[32,16,256]{2,1,0:T(8,128)(2,1)}) custom-call(bf16[8,512,256]{2,1,0:T(8,128)(2,1)} %all_to_all.40.back_ref, bf16[512,1536]{1,0:T(8,128)(2,1)} %get-tuple-element.159.kept_ref, f32[2,128]{1,0:T(2,128)} %pad_maximum_fusion.3.refs_2_.head_gain_ref, ...), custom_call_target="tpu_custom_call" | custom-call | tf_op jit(solution)/shard_map/project_back/pallas_call | solution.py:308
  403.2 8.1 %all-to-all-start.7 = ((bf16[32,16,256]{2,1,0:T(8,128)(2,1)}), bf16[32,16,256]{2,1,0:T(8,128)(2,1)S(1)}, u32[]{:S(2)}, u32[]{:S(2)}) async-start(bf16[32,16,256]{2,1,0:T(8,128)(2,1)} %get-tuple-element.164), calls=%async_computation.7 | async-start | bytes 524288 | tf_op jit(solution)/shard_map/all_to_all | solution.py:1013
  411.3 2.1 reduce_grads.3
  413.4 8.6 %input_back.1 = f32[512,1024]{1,0:T(8,128)} custom-call(bf16[512,2048]{1,0:T(8,128)(2,1)} %get-tuple-element.161.refs_0_, bf16[512,48]{1,0:T(8,128)(2,1)} %get-tuple-element.162.refs_1_, bf16[48,1024]{1,0:T(8,128)(2,1)} %get-tuple-element.96.refs_5_.refs_2_, bf16[512,1024]{1,0:T(8,128)(2,1)} %refs_3_.3, f32[1,1024]{1,0:T(1,128)} %bitcast.22, ...), custom_call_target="tpu_custom_call" | custom-call | flops 2147483648 | bytes 10485760 | tf_op jit(solution)/shard_map/input_back/pallas_call | solution.py:353
  422.7 3.4 reduce_grads.2
  (99 shorter events, 13.4 us)
Async XLA Ops:
  0.6 15.0 %copy-start.7 = (bf16[32,2048]{1,0:T(8,128)(2,1)S(1)}, bf16[32,2048]{1,0:T(8,128)(2,1)}, u32[]{:S(2)}) copy-start(bf16[32,2048]{1,0:T(8,128)(2,1)} %param.28) | copy-start | bytes 393220
  2.9 29.5 %copy-start.6 = (bf16[464,1024]{1,0:T(8,128)(2,1)S(1)}, bf16[464,1024]{1,0:T(8,128)(2,1)}, u32[]{:S(2)}) copy-start(bf16[464,1024]{1,0:T(8,128)(2,1)} %stack_shard.1.refs_10_) | copy-start | bytes 2850820
  2.9 24.4 %collective-permute-start.3 = (bf16[464,1024]{1,0:T(8,128)(2,1)}, bf16[464,1024]{1,0:T(8,128)(2,1)}, u32[]{:S(2)}, u32[]{:S(2)}) collective-permute-start(bf16[464,1024]{1,0:T(8,128)(2,1)} %stack_shard.1.refs_10_), channel_id=1, source_target_pairs={{0,8},{1,9},{2,10},{3,11},{4,12},{5,13},{6,14},{7,15},{8,0},{9,1},... | collective-permute-start | bytes 2850824 | tf_op jit(solution)/shard_map/ppermute | solution.py:96
  5.8 23.0 %collective-permute-start.4 = (bf16[464,1024]{1,0:T(8,128)(2,1)}, bf16[464,1024]{1,0:T(8,128)(2,1)}, u32[]{:S(2)}, u32[]{:S(2)}) collective-permute-start(bf16[464,1024]{1,0:T(8,128)(2,1)} %stack_shard.1.refs_10_), channel_id=1, source_target_pairs={{0,16},{1,17},{2,18},{3,19},{4,20},{5,21},{6,22},{7,23},{8,24},{9,... | collective-permute-start | bytes 2850824 | tf_op jit(solution)/shard_map/ppermute | solution.py:96
  7.4 8.7 %collective-permute-start = (bf16[32,2048]{1,0:T(8,128)(2,1)}, bf16[32,2048]{1,0:T(8,128)(2,1)}, u32[]{:S(2)}, u32[]{:S(2)}) collective-permute-start(bf16[32,2048]{1,0:T(8,128)(2,1)} %param.28), channel_id=1, source_target_pairs={{0,1},{1,2},{2,3},{3,0},{4,5},{5,6},{6,7},{7,4},{8,9},{9,10},{10,1... | collective-permute-start | bytes 393224 | tf_op jit(solution)/shard_map/ppermute | solution.py:96
  8.9 10.9 %collective-permute-start.1 = (bf16[32,2048]{1,0:T(8,128)(2,1)}, bf16[32,2048]{1,0:T(8,128)(2,1)S(1)}, u32[]{:S(2)}, u32[]{:S(2)}) collective-permute-start(bf16[32,2048]{1,0:T(8,128)(2,1)} %param.28), channel_id=1, source_target_pairs={{0,2},{1,3},{2,0},{3,1},{4,6},{5,7},{6,4},{7,5},{8,10},{9,11},{10,... | collective-permute-start | bytes 393224 | tf_op jit(solution)/shard_map/ppermute | solution.py:96
  11.5 8.4 %collective-permute-start.2 = (bf16[32,2048]{1,0:T(8,128)(2,1)}, bf16[32,2048]{1,0:T(8,128)(2,1)S(1)}, u32[]{:S(2)}, u32[]{:S(2)}) collective-permute-start(bf16[32,2048]{1,0:T(8,128)(2,1)} %param.28), channel_id=1, source_target_pairs={{0,3},{1,0},{2,1},{3,2},{4,7},{5,4},{6,5},{7,6},{8,11},{9,8},{10,9... | collective-permute-start | bytes 393224 | tf_op jit(solution)/shard_map/ppermute | solution.py:96
  19.8 0.7 copy-start.9
  20.0 0.7 copy-start.8
  20.6 34.6 %all-to-all-start = ((bf16[32,16,256]{2,1,0:T(8,128)(2,1)}), bf16[32,16,256]{2,1,0:T(8,128)(2,1)S(1)}, u32[]{:S(2)}, u32[]{:S(2)}) async-start(bf16[32,16,256]{2,1,0:T(8,128)(2,1)} %pack_adapters.2), calls=%async_computation | async-start | bytes 524288 | tf_op jit(solution)/shard_map/all_to_all | solution.py:1013
  26.3 32.7 %copy-start.14 = (f32[64]{0:T(128)S(1)}, f32[64]{0:T(128)}, u32[]{:S(2)}) copy-start(f32[64]{0:T(128)} %param.25) | copy-start | bytes 772
  26.3 32.7 %copy-start.15 = (f32[64]{0:T(128)S(1)}, f32[64]{0:T(128)}, u32[]{:S(2)}) copy-start(f32[64]{0:T(128)} %param.26) | copy-start | bytes 772
  28.8 15.6 %collective-permute-start.5 = (bf16[128,2048]{1,0:T(8,128)(2,1)S(1)}, bf16[128,2048]{1,0:T(8,128)(2,1)S(1)}, u32[]{:S(2)}, u32[]{:S(2)}) collective-permute-start(bf16[128,2048]{1,0:T(8,128)(2,1)S(1)} %pad_maximum_fusion), channel_id=1, source_target_pairs={{0,8},{1,9},{2,10},{3,11},{4,12},{5,13},{6,14},{7,15},{8,0},{9,1},... | collective-permute-start | bytes 1572872 | tf_op jit(solution)/shard_map/ppermute | solution.py:96
  30.2 24.9 %collective-permute-start.6 = (bf16[128,2048]{1,0:T(8,128)(2,1)S(1)}, bf16[128,2048]{1,0:T(8,128)(2,1)S(1)}, u32[]{:S(2)}, u32[]{:S(2)}) collective-permute-start(bf16[128,2048]{1,0:T(8,128)(2,1)S(1)} %pad_maximum_fusion), channel_id=1, source_target_pairs={{0,16},{1,17},{2,18},{3,19},{4,20},{5,21},{6,22},{7,23},{8,24},{9,... | collective-permute-start | bytes 1572872 | tf_op jit(solution)/shard_map/ppermute | solution.py:96
  32.4 22.8 %collective-permute-start.8 = (bf16[464,1024]{1,0:T(8,128)(2,1)S(1)}, bf16[464,1024]{1,0:T(8,128)(2,1)}, u32[]{:S(2)}, u32[]{:S(2)}) collective-permute-start(bf16[464,1024]{1,0:T(8,128)(2,1)S(1)} %copy-done.6), channel_id=1, source_target_pairs={{0,1},{1,2},{2,3},{3,0},{4,5},{5,6},{6,7},{7,4},{8,9},{9,10},{10,1... | collective-permute-start | bytes 2850824 | tf_op jit(solution)/shard_map/ppermute | solution.py:96
  35.1 20.0 %collective-permute-start.7 = (bf16[128,2048]{1,0:T(8,128)(2,1)S(1)}, bf16[128,2048]{1,0:T(8,128)(2,1)S(1)}, u32[]{:S(2)}, u32[]{:S(2)}) collective-permute-start(bf16[128,2048]{1,0:T(8,128)(2,1)S(1)} %pad_maximum_fusion), channel_id=1, source_target_pairs={{0,24},{1,25},{2,26},{3,27},{4,28},{5,29},{6,30},{7,31},{8,16},{9,... | collective-permute-start | bytes 1572872 | tf_op jit(solution)/shard_map/ppermute | solution.py:96
  55.2 8.7 %copy-start.2 = (bf16[512,2048]{1,0:T(8,128)(2,1)}, bf16[512,2048]{1,0:T(8,128)(2,1)S(1)}, u32[]{:S(2)}) copy-start(bf16[512,2048]{1,0:T(8,128)(2,1)S(1)} %constant_dynamic-update-slice_fusion.refs_7_.refs_6_) | copy-start | bytes 6291460
  55.2 6.8 %copy-start.4 = (bf16[32,16,256]{2,1,0:T(8,128)(2,1)}, bf16[32,16,256]{2,1,0:T(8,128)(2,1)S(1)}, u32[]{:S(2)}) copy-start(bf16[32,16,256]{2,1,0:T(8,128)(2,1)S(1)} %all-to-all-done.source) | copy-start | bytes 786436
  55.2 8.6 %collective-permute-start.9 = (bf16[512,2048]{1,0:T(8,128)(2,1)S(1)}, bf16[512,2048]{1,0:T(8,128)(2,1)}, u32[]{:S(2)}, u32[]{:S(2)}) collective-permute-start(bf16[512,2048]{1,0:T(8,128)(2,1)S(1)} %constant_dynamic-update-slice_fusion.refs_7_.refs_6_), channel_id=1, source_target_pairs={{0,4},{1,5},{2,6},{3,7},{4,0},{5,1},{6,2},{7,3},{8,12},{9,13},{10,... | collective-permute-start | bytes 6291464 | tf_op jit(solution)/shard_map/ppermute | solution.py:96
  55.6 25.3 %collective-permute-start.10 = (bf16[464,1024]{1,0:T(8,128)(2,1)}, bf16[464,1024]{1,0:T(8,128)(2,1)}, u32[]{:S(2)}, u32[]{:S(2)}) collective-permute-start(bf16[464,1024]{1,0:T(8,128)(2,1)} %collective-permute-done.8.refs_13_), channel_id=1, source_target_pairs={{0,1},{1,2},{2,3},{3,0},{4,5},{5,6},{6,7},{7,4},{8,9},{9,10},{10,1... | collective-permute-start | bytes 2850824 | tf_op jit(solution)/shard_map/ppermute | solution.py:96
  56.8 24.1 %collective-permute-start.11 = (bf16[464,1024]{1,0:T(8,128)(2,1)}, bf16[464,1024]{1,0:T(8,128)(2,1)}, u32[]{:S(2)}, u32[]{:S(2)}) collective-permute-start(bf16[464,1024]{1,0:T(8,128)(2,1)} %collective-permute-done.8.refs_13_), channel_id=1, source_target_pairs={{0,8},{1,9},{2,10},{3,11},{4,12},{5,13},{6,14},{7,15},{8,0},{9,1},... | collective-permute-start | bytes 2850824 | tf_op jit(solution)/shard_map/ppermute | solution.py:96
  57.9 23.2 %collective-permute-start.12 = (bf16[464,1024]{1,0:T(8,128)(2,1)}, bf16[464,1024]{1,0:T(8,128)(2,1)}, u32[]{:S(2)}, u32[]{:S(2)}) collective-permute-start(bf16[464,1024]{1,0:T(8,128)(2,1)} %collective-permute-done.3.refs_11_), channel_id=1, source_target_pairs={{0,16},{1,17},{2,18},{3,19},{4,20},{5,21},{6,22},{7,23},{8,24},{9,... | collective-permute-start | bytes 2850824 | tf_op jit(solution)/shard_map/ppermute | solution.py:96
  81.1 33.6 %copy-start.10 = (s32[16384]{0:T(1024)S(1)}, s32[16384]{0:T(1024)}, u32[]{:S(2)}) copy-start(s32[16384]{0:T(1024)} %param.22) | copy-start | bytes 196612
  81.1 73.0 %all-to-all-start.1 = ((bf16[8,512,256]{2,1,0:T(8,128)(2,1)}), bf16[8,512,256]{2,1,0:T(8,128)(2,1)S(1)}, u32[]{:S(2)}, u32[]{:S(2)}) async-start(bf16[8,512,256]{2,1,0:T(8,128)(2,1)} %get-tuple-element.109), calls=%async_computation.1 | async-start | bytes 4194304 | tf_op jit(solution)/shard_map/all_to_all | solution.py:1002
  85.1 23.8 %collective-permute-start.13 = (bf16[464,1024]{1,0:T(8,128)(2,1)}, bf16[464,1024]{1,0:T(8,128)(2,1)}, u32[]{:S(2)}, u32[]{:S(2)}) collective-permute-start(bf16[464,1024]{1,0:T(8,128)(2,1)} %collective-permute-done.8.refs_13_), channel_id=1, source_target_pairs={{0,16},{1,17},{2,18},{3,19},{4,20},{5,21},{6,22},{7,23},{8,24},{9,... | collective-permute-start | bytes 2850824 | tf_op jit(solution)/shard_map/ppermute | solution.py:96
  86.2 23.4 %collective-permute-start.14 = (bf16[464,1024]{1,0:T(8,128)(2,1)}, bf16[464,1024]{1,0:T(8,128)(2,1)S(1)}, u32[]{:S(2)}, u32[]{:S(2)}) collective-permute-start(bf16[464,1024]{1,0:T(8,128)(2,1)} %collective-permute-done.10.refs_14_), channel_id=1, source_target_pairs={{0,8},{1,9},{2,10},{3,11},{4,12},{5,13},{6,14},{7,15},{8,0},{9,1},... | collective-permute-start | bytes 2850824 | tf_op jit(solution)/shard_map/ppermute | solution.py:96
  87.2 22.4 %collective-permute-start.15 = (bf16[464,1024]{1,0:T(8,128)(2,1)S(1)}, bf16[464,1024]{1,0:T(8,128)(2,1)S(1)}, u32[]{:S(2)}, u32[]{:S(2)}) collective-permute-start(bf16[464,1024]{1,0:T(8,128)(2,1)S(1)} %copy-done.6), channel_id=1, source_target_pairs={{0,4},{1,5},{2,6},{3,7},{4,0},{5,1},{6,2},{7,3},{8,12},{9,13},{10,... | collective-permute-start | bytes 2850824 | tf_op jit(solution)/shard_map/ppermute | solution.py:96
  109.6 1.0 copy-start.11
  110.6 0.9 copy-start.12
  110.6 22.6 %collective-permute-start.16 = (bf16[464,1024]{1,0:T(8,128)(2,1)}, bf16[464,1024]{1,0:T(8,128)(2,1)S(1)}, u32[]{:S(2)}, u32[]{:S(2)}) collective-permute-start(bf16[464,1024]{1,0:T(8,128)(2,1)} %collective-permute-done.13.refs_18_), channel_id=1, source_target_pairs={{0,8},{1,9},{2,10},{3,11},{4,12},{5,13},{6,14},{7,15},{8,0},{9,1},... | collective-permute-start | bytes 2850824 | tf_op jit(solution)/shard_map/ppermute | solution.py:96
  111.6 22.7 %collective-permute-start.17 = (bf16[464,1024]{1,0:T(8,128)(2,1)}, bf16[464,1024]{1,0:T(8,128)(2,1)}, u32[]{:S(2)}, u32[]{:S(2)}) collective-permute-start(bf16[464,1024]{1,0:T(8,128)(2,1)} %collective-permute-done.10.refs_14_), channel_id=1, source_target_pairs={{0,16},{1,17},{2,18},{3,19},{4,20},{5,21},{6,22},{7,23},{8,24},{9,... | collective-permute-start | bytes 2850824 | tf_op jit(solution)/shard_map/ppermute | solution.py:96
  112.5 21.8 %collective-permute-start.18 = (bf16[464,1024]{1,0:T(8,128)(2,1)}, bf16[464,1024]{1,0:T(8,128)(2,1)}, u32[]{:S(2)}, u32[]{:S(2)}) collective-permute-start(bf16[464,1024]{1,0:T(8,128)(2,1)} %collective-permute-done.8.refs_13_), channel_id=1, source_target_pairs={{0,4},{1,5},{2,6},{3,7},{4,0},{5,1},{6,2},{7,3},{8,12},{9,13},{10,... | collective-permute-start | bytes 2850824 | tf_op jit(solution)/shard_map/ppermute | solution.py:96
  112.5 21.8 %collective-permute-start.19 = (bf16[464,1024]{1,0:T(8,128)(2,1)}, bf16[464,1024]{1,0:T(8,128)(2,1)}, u32[]{:S(2)}, u32[]{:S(2)}) collective-permute-start(bf16[464,1024]{1,0:T(8,128)(2,1)} %collective-permute-done.3.refs_11_), channel_id=1, source_target_pairs={{0,4},{1,5},{2,6},{3,7},{4,0},{5,1},{6,2},{7,3},{8,12},{9,13},{10,... | collective-permute-start | bytes 2850824 | tf_op jit(solution)/shard_map/ppermute | solution.py:96
  113.0 43.9 %collective-permute-start.20 = (bf16[464,1024]{1,0:T(8,128)(2,1)}, bf16[464,1024]{1,0:T(8,128)(2,1)}, u32[]{:S(2)}, u32[]{:S(2)}) collective-permute-start(bf16[464,1024]{1,0:T(8,128)(2,1)} %collective-permute-done.10.refs_14_), channel_id=1, source_target_pairs={{0,1},{1,2},{2,3},{3,0},{4,5},{5,6},{6,7},{7,4},{8,9},{9,10},{10,1... | collective-permute-start | bytes 2850824 | tf_op jit(solution)/shard_map/ppermute | solution.py:96
  133.2 20.8 %copy-start.13 = (bf16[464,1024]{1,0:T(8,128)(2,1)}, bf16[464,1024]{1,0:T(8,128)(2,1)S(1)}, u32[]{:S(2)}) copy-start(bf16[464,1024]{1,0:T(8,128)(2,1)S(1)} %collective-permute-done.16.refs_21_) | copy-start | bytes 2850820
  154.1 27.3 %all-to-all-start.2 = ((bf16[32,16,640]{2,1,0:T(8,128)(2,1)}), bf16[32,16,640]{2,1,0:T(8,128)(2,1)S(1)}, u32[]{:S(2)}, u32[]{:S(2)}) async-start(bf16[32,16,640]{2,1,0:T(8,128)(2,1)} %pack_adapters.3), calls=%async_computation.2 | async-start | bytes 1310720 | tf_op jit(solution)/shard_map/all_to_all | solution.py:1013
  156.9 30.0 %collective-permute-start.21 = (bf16[464,1024]{1,0:T(8,128)(2,1)}, bf16[464,1024]{1,0:T(8,128)(2,1)}, u32[]{:S(2)}, u32[]{:S(2)}) collective-permute-start(bf16[464,1024]{1,0:T(8,128)(2,1)} %collective-permute-done.20.refs_20_), channel_id=1, source_target_pairs={{0,8},{1,9},{2,10},{3,11},{4,12},{5,13},{6,14},{7,15},{8,0},{9,1},... | collective-permute-start | bytes 2850824 | tf_op jit(solution)/shard_map/ppermute | solution.py:96
  158.6 28.8 %collective-permute-start.22 = (bf16[464,1024]{1,0:T(8,128)(2,1)}, bf16[464,1024]{1,0:T(8,128)(2,1)}, u32[]{:S(2)}, u32[]{:S(2)}) collective-permute-start(bf16[464,1024]{1,0:T(8,128)(2,1)} %collective-permute-done.20.refs_20_), channel_id=1, source_target_pairs={{0,16},{1,17},{2,18},{3,19},{4,20},{5,21},{6,22},{7,23},{8,24},{9,... | collective-permute-start | bytes 2850824 | tf_op jit(solution)/shard_map/ppermute | solution.py:96
  160.1 27.3 %collective-permute-start.23 = (bf16[464,1024]{1,0:T(8,128)(2,1)}, bf16[464,1024]{1,0:T(8,128)(2,1)}, u32[]{:S(2)}, u32[]{:S(2)}) collective-permute-start(bf16[464,1024]{1,0:T(8,128)(2,1)} %collective-permute-done.4.refs_12_), channel_id=1, source_target_pairs={{0,4},{1,5},{2,6},{3,7},{4,0},{5,1},{6,2},{7,3},{8,12},{9,13},{10,... | collective-permute-start | bytes 2850824 | tf_op jit(solution)/shard_map/ppermute | solution.py:96
  160.1 27.3 %collective-permute-start.24 = (bf16[464,1024]{1,0:T(8,128)(2,1)}, bf16[464,1024]{1,0:T(8,128)(2,1)}, u32[]{:S(2)}, u32[]{:S(2)}) collective-permute-start(bf16[464,1024]{1,0:T(8,128)(2,1)} %collective-permute-done.12.refs_16_), channel_id=1, source_target_pairs={{0,4},{1,5},{2,6},{3,7},{4,0},{5,1},{6,2},{7,3},{8,12},{9,13},{10,... | collective-permute-start | bytes 2850824 | tf_op jit(solution)/shard_map/ppermute | solution.py:96
  160.6 26.8 %collective-permute-start.25 = (bf16[464,1024]{1,0:T(8,128)(2,1)}, bf16[464,1024]{1,0:T(8,128)(2,1)}, u32[]{:S(2)}, u32[]{:S(2)}) collective-permute-start(bf16[464,1024]{1,0:T(8,128)(2,1)} %collective-permute-done.10.refs_14_), channel_id=1, source_target_pairs={{0,4},{1,5},{2,6},{3,7},{4,0},{5,1},{6,2},{7,3},{8,12},{9,13},{10,... | collective-permute-start | bytes 2850824 | tf_op jit(solution)/shard_map/ppermute | solution.py:96
  181.3 0.8 copy-start.1
  187.4 8.3 %collective-permute-start.28 = (bf16[464,1024]{1,0:T(8,128)(2,1)}, bf16[464,1024]{1,0:T(8,128)(2,1)}, u32[]{:S(2)}, u32[]{:S(2)}) collective-permute-start(bf16[464,1024]{1,0:T(8,128)(2,1)} %collective-permute-done.21.refs_25_), channel_id=1, source_target_pairs={{0,4},{1,5},{2,6},{3,7},{4,0},{5,1},{6,2},{7,3},{8,12},{9,13},{10,... | collective-permute-start | bytes 2850824 | tf_op jit(solution)/shard_map/ppermute | solution.py:96
  187.5 8.2 %collective-permute-start.29 = (bf16[464,1024]{1,0:T(8,128)(2,1)}, bf16[464,1024]{1,0:T(8,128)(2,1)}, u32[]{:S(2)}, u32[]{:S(2)}) collective-permute-start(bf16[464,1024]{1,0:T(8,128)(2,1)} %collective-permute-done.22.refs_26_), channel_id=1, source_target_pairs={{0,4},{1,5},{2,6},{3,7},{4,0},{5,1},{6,2},{7,3},{8,12},{9,13},{10,... | collective-permute-start | bytes 2850824 | tf_op jit(solution)/shard_map/ppermute | solution.py:96
  188.0 7.8 %collective-permute-start.30 = (bf16[464,1024]{1,0:T(8,128)(2,1)}, bf16[464,1024]{1,0:T(8,128)(2,1)}, u32[]{:S(2)}, u32[]{:S(2)}) collective-permute-start(bf16[464,1024]{1,0:T(8,128)(2,1)} %collective-permute-done.11.refs_15_), channel_id=1, source_target_pairs={{0,4},{1,5},{2,6},{3,7},{4,0},{5,1},{6,2},{7,3},{8,12},{9,13},{10,... | collective-permute-start | bytes 2850824 | tf_op jit(solution)/shard_map/ppermute | solution.py:96
  188.1 23.7 %collective-permute-start.26 = (bf16[464,1024]{1,0:T(8,128)(2,1)}, bf16[464,1024]{1,0:T(8,128)(2,1)}, u32[]{:S(2)}, u32[]{:S(2)}) collective-permute-start(bf16[464,1024]{1,0:T(8,128)(2,1)} %collective-permute-done.22.refs_26_), channel_id=1, source_target_pairs={{0,8},{1,9},{2,10},{3,11},{4,12},{5,13},{6,14},{7,15},{8,0},{9,1},... | collective-permute-start | bytes 2850824 | tf_op jit(solution)/shard_map/ppermute | solution.py:96
  189.0 23.5 %collective-permute-start.27 = (bf16[464,1024]{1,0:T(8,128)(2,1)}, bf16[464,1024]{1,0:T(8,128)(2,1)}, u32[]{:S(2)}, u32[]{:S(2)}) collective-permute-start(bf16[464,1024]{1,0:T(8,128)(2,1)} %copy-done.11), channel_id=1, source_target_pairs={{0,16},{1,17},{2,18},{3,19},{4,20},{5,21},{6,22},{7,23},{8,24},{9,... | collective-permute-start | bytes 2850824 | tf_op jit(solution)/shard_map/ppermute | solution.py:96
  191.0 30.9 %all-to-all-start.3 = ((bf16[8,512,128]{2,1,0:T(8,128)(2,1)}), bf16[8,512,128]{2,1,0:T(8,128)(2,1)S(1)}, u32[]{:S(2)}, u32[]{:S(2)}) async-start(bf16[8,512,128]{2,1,0:T(8,128)(2,1)} %bitcast.6), calls=%async_computation.3 | async-start | bytes 2097152 | tf_op jit(solution)/shard_map/all_to_all | solution.py:1002
  195.8 26.1 %collective-permute-start.31 = (bf16[464,1024]{1,0:T(8,128)(2,1)}, bf16[464,1024]{1,0:T(8,128)(2,1)}, u32[]{:S(2)}, u32[]{:S(2)}) collective-permute-start(bf16[464,1024]{1,0:T(8,128)(2,1)} %collective-permute-done.13.refs_18_), channel_id=1, source_target_pairs={{0,4},{1,5},{2,6},{3,7},{4,0},{5,1},{6,2},{7,3},{8,12},{9,13},{10,... | collective-permute-start | bytes 2850824 | tf_op jit(solution)/shard_map/ppermute | solution.py:96
  196.3 25.5 %collective-permute-start.32 = (bf16[464,1024]{1,0:T(8,128)(2,1)}, bf16[464,1024]{1,0:T(8,128)(2,1)}, u32[]{:S(2)}, u32[]{:S(2)}) collective-permute-start(bf16[464,1024]{1,0:T(8,128)(2,1)} %copy-done.11), channel_id=1, source_target_pairs={{0,4},{1,5},{2,6},{3,7},{4,0},{5,1},{6,2},{7,3},{8,12},{9,13},{10,... | collective-permute-start | bytes 2850824 | tf_op jit(solution)/shard_map/ppermute | solution.py:96
  196.4 25.5 %collective-permute-start.33 = (bf16[464,1024]{1,0:T(8,128)(2,1)}, bf16[464,1024]{1,0:T(8,128)(2,1)}, u32[]{:S(2)}, u32[]{:S(2)}) collective-permute-start(bf16[464,1024]{1,0:T(8,128)(2,1)} %collective-permute-done.17.refs_22_), channel_id=1, source_target_pairs={{0,4},{1,5},{2,6},{3,7},{4,0},{5,1},{6,2},{7,3},{8,12},{9,13},{10,... | collective-permute-start | bytes 2850824 | tf_op jit(solution)/shard_map/ppermute | solution.py:96
  211.8 10.1 %collective-permute-start.34 = (bf16[464,1024]{1,0:T(8,128)(2,1)}, bf16[464,1024]{1,0:T(8,128)(2,1)}, u32[]{:S(2)}, u32[]{:S(2)}) collective-permute-start(bf16[464,1024]{1,0:T(8,128)(2,1)} %copy-done.13), channel_id=1, source_target_pairs={{0,4},{1,5},{2,6},{3,7},{4,0},{5,1},{6,2},{7,3},{8,12},{9,13},{10,... | collective-permute-start | bytes 2850824 | tf_op jit(solution)/shard_map/ppermute | solution.py:96
  212.6 9.3 %collective-permute-start.35 = (bf16[464,1024]{1,0:T(8,128)(2,1)}, bf16[464,1024]{1,0:T(8,128)(2,1)}, u32[]{:S(2)}, u32[]{:S(2)}) collective-permute-start(bf16[464,1024]{1,0:T(8,128)(2,1)} %collective-permute-done.20.refs_20_), channel_id=1, source_target_pairs={{0,4},{1,5},{2,6},{3,7},{4,0},{5,1},{6,2},{7,3},{8,12},{9,13},{10,... | collective-permute-start | bytes 2850824 | tf_op jit(solution)/shard_map/ppermute | solution.py:96
  221.8 4.3 %copy-start.3 = (bf16[8,512,128]{2,1,0:T(8,128)(2,1)}, bf16[8,512,128]{2,1,0:T(8,128)(2,1)S(1)}, u32[]{:S(2)}) copy-start(bf16[8,512,128]{2,1,0:T(8,128)(2,1)S(1)} %all-to-all-done.3.refs_0_) | copy-start | bytes 3145732
  221.9 2.9 collective-permute-start.36
  222.2 3.9 collective-permute-start.37
  280.6 29.6 %all-to-all-start.4 = ((bf16[8,512,128]{2,1,0:T(8,128)(2,1)}), bf16[8,512,128]{2,1,0:T(8,128)(2,1)S(1)}, u32[]{:S(2)}, u32[]{:S(2)}) async-start(bf16[8,512,128]{2,1,0:T(8,128)(2,1)} %get-tuple-element.154), calls=%async_computation.4 | async-start | bytes 2097152 | tf_op jit(solution)/shard_map/all_to_all | solution.py:1002
  310.2 31.8 %all-to-all-start.5 = ((bf16[32,16,640]{2,1,0:T(8,128)(2,1)}), bf16[32,16,640]{2,1,0:T(8,128)(2,1)}, u32[]{:S(2)}, u32[]{:S(2)}) async-start(bf16[32,16,640]{2,1,0:T(8,128)(2,1)} %pack_grads.1), calls=%async_computation.5 | async-start | bytes 1310720 | tf_op jit(solution)/shard_map/all_to_all | solution.py:1013
  340.7 1.3 copy-start
  403.2 18.8 %all-to-all-start.7 = ((bf16[32,16,256]{2,1,0:T(8,128)(2,1)}), bf16[32,16,256]{2,1,0:T(8,128)(2,1)S(1)}, u32[]{:S(2)}, u32[]{:S(2)}) async-start(bf16[32,16,256]{2,1,0:T(8,128)(2,1)} %get-tuple-element.164), calls=%async_computation.7 | async-start | bytes 524288 | tf_op jit(solution)/shard_map/all_to_all | solution.py:1013
  422.0 0.7 copy-start.5
